TPU v7x, 32 devices: a whole 2x2x4 slice. The times are simulated.
32 devices in a mesh: ctx: 2 (over x), tp: 4 (over y, core), pp: 4 (over z).
Axes of the slice: x: 2, y: 2, z: 4, core: 2. Of those that a mesh axis runs over, the one named last changes fastest.
Arguments:
- lin_query: bfloat16 [4, 512, 8192], P('pp', 'ctx', 'tp'), may hold values from -6 to 6
- lin_key: bfloat16 [4, 512, 8192], P('pp', 'ctx', 'tp'), may hold values from -6 to 6
- lin_value: bfloat16 [4, 512, 8192], P('pp', 'ctx', 'tp'), may hold values from -6 to 6
- log_decay: float32 [4, 512, 64], P('pp', 'ctx', 'tp'), may hold values from -1 to 0, as said below
- out_gate: bfloat16 [4, 512, 8192], P('pp', 'ctx', 'tp'), may hold values from -6 to 6
- norm_gain: float32 [4, 8192], P('pp', 'tp'), may hold values from 0.1 to 1.9
- soft_query: bfloat16 [4, 512, 8192], P('pp', 'ctx', 'tp'), may hold values from -5 to 5
- soft_key: bfloat16 [4, 512, 1024], P('pp', 'ctx', 'tp'), may hold values from -5 to 5
- soft_value: bfloat16 [4, 512, 1024], P('pp', 'ctx', 'tp'), may hold values from -6 to 6
Outputs:
- lin_handed: bfloat16 [4, 512, 8192], P('pp', 'ctx', 'tp')
- soft_handed: bfloat16 [4, 512, 8192], P('pp', 'ctx', 'tp')
Inputs may be any that keep to these rules, and one draw needn't show every extreme that they name: `log_decay`: negative everywhere.
All inputs are finite; a program needn't handle non-finite values.
Results may differ from a plain program's by a relative error of at most 0.0049.
Values may be sent and summed in bfloat16 or wider, within the bound.
No kernel may reach another device: no remote copies, remote signals or barrier semaphores. Data moves between devices by JAX's collectives and lax.ppermute only.
A program may use at most 128 MiB of HBM per device.

v0:
```python
import math

import jax
import jax.numpy as jnp
from jax import lax
from jax.sharding import PartitionSpec as P

HEADS = 64
KV_HEADS = 8
HD = 128
BLK = 256


epsilon = 1e-06
lowest = -1e30


def passed_along(block, axis, distance):
    devices = range(lax.axis_size(axis))
    route = [((i - distance) % len(devices), i) for i in devices]
    return lax.ppermute(block, axis, route)


def lightning_local(query_rows, key_rows, value_rows, decays):
    length, head_count = decays.shape
    blocks = length // BLK
    queries = query_rows.reshape(blocks, BLK, head_count, HD)
    keys_all = key_rows.reshape(blocks, BLK, head_count, HD)
    values_all = value_rows.reshape(blocks, BLK, head_count, HD)
    running_log = jnp.cumsum(decays.reshape(blocks, BLK, head_count), axis=1)
    closing_log = running_log[:, -1, :]
    scores = jnp.einsum("bthd,bshd->bhts", queries, keys_all, preferred_element_type=jnp.float32)
    log_turned = jnp.swapaxes(running_log, 1, 2)
    log_gap = log_turned[:, :, :, None] - log_turned[:, :, None, :]
    causal = lax.iota(jnp.int32, BLK)[:, None] >= lax.iota(jnp.int32, BLK)[None, :]
    decay_mask = jnp.where(causal, jnp.exp(jnp.where(causal, log_gap, 0.0)), 0.0)
    weights = (scores * decay_mask).astype(jnp.bfloat16)
    inside = jnp.einsum("bhts,bshd->bthd", weights, values_all, preferred_element_type=jnp.float32)
    pressed = (
        keys_all.astype(jnp.float32) * jnp.exp(closing_log[:, None, :] - running_log)[..., None]
    ).astype(jnp.bfloat16)
    updates = jnp.einsum("bshd,bshe->bhde", pressed, values_all, preferred_element_type=jnp.float32)

    def advance(state, inputs):
        factor_log, update = inputs
        return (jnp.exp(factor_log)[:, None, None] * state + update, state)

    closing, before = lax.scan(
        advance, jnp.zeros((head_count, HD, HD), jnp.float32), (closing_log, updates)
    )
    lifted = queries.astype(jnp.float32) * jnp.exp(running_log)[..., None]
    earlier_part = jnp.einsum("bthd,bhde->bthe", lifted, before, precision=lax.Precision.HIGHEST)
    offsets = jnp.cumsum(closing_log, axis=0) - closing_log
    carried = lifted * jnp.exp(offsets)[:, None, :, None]
    return (inside + earlier_part, carried, closing, jnp.sum(closing_log, axis=0))


def absorb(running, query_rows, row_pos, key_rows, value_rows, key_pos):
    row_peak, totals, weighted = running
    scores = jnp.einsum(
        "tkgd,skd->tkgs", query_rows, key_rows, preferred_element_type=jnp.float32
    ) * HD ** (-0.5)
    causal = (row_pos[:, None] >= key_pos[None, :])[:, None, None, :]
    block_peak = jnp.max(jnp.where(causal, scores, lowest), axis=-1)
    new_peak = jnp.maximum(row_peak, block_peak)
    unscaled = jnp.where(causal, jnp.exp(scores - new_peak[..., None]), 0.0)
    shrink = jnp.exp(row_peak - new_peak)
    totals = shrink * totals + jnp.sum(unscaled, axis=-1)
    weighted = shrink[..., None] * weighted + jnp.einsum(
        "tkgs,skd->tkgd",
        unscaled.astype(jnp.bfloat16),
        value_rows,
        preferred_element_type=jnp.float32,
    )
    return (new_peak, totals, weighted)


def empty_state(length, kv_count, group_size):
    return (
        jnp.full((length, kv_count, group_size), lowest, jnp.float32),
        jnp.zeros((length, kv_count, group_size), jnp.float32),
        jnp.zeros((length, kv_count, group_size, HD), jnp.float32),
    )


def local(
    lin_query, lin_key, lin_value, log_decay, out_gate, norm_gain, soft_query, soft_key, soft_value
):
    length = lin_query.shape[1]
    head_count = log_decay.shape[2]
    kv_count = soft_key.shape[2] // HD
    group_size = HEADS // KV_HEADS
    position = lax.axis_index("ctx")
    local_part, carried, closing, device_log = lightning_local(
        lin_query[0], lin_key[0], lin_value[0], log_decay[0]
    )
    gathered_states, device_logs = (
        lax.all_gather(closing[None], "ctx", axis=0, tiled=True),
        lax.all_gather(device_log[None, :], "ctx", axis=0, tiled=True),
    )
    devices = device_logs.shape[0]
    rising = jnp.cumsum(device_logs, axis=0)
    owners = lax.iota(jnp.int32, devices)
    earlier_mask = (owners < position)[:, None]
    reached = jnp.sum(jnp.where(earlier_mask, device_logs, 0.0), axis=0)
    weight = jnp.where(
        earlier_mask, jnp.exp(jnp.where(earlier_mask, reached[None, :] - rising, 0.0)), 0.0
    )
    incoming = jnp.einsum("jh,jhde->hde", weight, gathered_states, precision=lax.Precision.HIGHEST)
    arrived = jnp.einsum("bthd,hde->bthe", carried, incoming, precision=lax.Precision.HIGHEST)
    mixture = (local_part + arrived).reshape(length, head_count, HD)
    normed = mixture * lax.rsqrt(jnp.mean(mixture * mixture, axis=-1, keepdims=True) + epsilon)
    lin_out = (
        normed.reshape(length, head_count * HD)
        * norm_gain[0][None, :]
        * jax.nn.sigmoid(out_gate[0].astype(jnp.float32))
    ).astype(jnp.bfloat16)
    query_rows = soft_query[0].reshape(length, kv_count, group_size, HD)
    key_rows = soft_key[0].reshape(length, kv_count, HD)
    value_rows = soft_value[0].reshape(length, kv_count, HD)
    row_pos = position * length + lax.iota(jnp.int32, length)
    last_row = position * length + length - 1
    key_piece = lax.all_gather(key_rows, "ctx", axis=0, tiled=True)
    value_piece = lax.all_gather(value_rows, "ctx", axis=0, tiled=True)
    piece_rows = key_piece.shape[0]
    stride = math.gcd(piece_rows, 512)

    def absorb_block(turn, kept):
        offset = turn * stride
        key_part = lax.dynamic_slice_in_dim(key_piece, offset, stride, 0)
        value_part = lax.dynamic_slice_in_dim(value_piece, offset, stride, 0)
        key_pos = offset + lax.iota(jnp.int32, stride)
        return absorb(kept, query_rows, row_pos, key_part, value_part, key_pos)

    def work_all(kept):
        return lax.fori_loop(0, piece_rows // stride, absorb_block, kept)

    def skip_all(kept):
        return kept

    row_peak, totals, weighted = lax.cond(
        jnp.int32(0) <= last_row, work_all, skip_all, empty_state(length, kv_count, group_size)
    )
    soft_out = (weighted / totals[..., None]).astype(jnp.bfloat16).reshape(length, head_count * HD)
    lin_handed, soft_handed = passed_along((lin_out[None], soft_out[None]), "pp", 1)
    return (lin_handed, soft_handed)


def solution(mesh):
    return jax.shard_map(
        local,
        mesh=mesh,
        in_specs=(
            P("pp", "ctx", "tp"),
            P("pp", "ctx", "tp"),
            P("pp", "ctx", "tp"),
            P("pp", "ctx", "tp"),
            P("pp", "ctx", "tp"),
            P("pp", "tp"),
            P("pp", "ctx", "tp"),
            P("pp", "ctx", "tp"),
            P("pp", "ctx", "tp"),
        ),
        out_specs=(P("pp", "ctx", "tp"), P("pp", "ctx", "tp")),
        check_vma=False,
    )
```

profile of v0, /device:TPU:1, one launch (start us, length us, event | category | flops | bytes accessed | tf_op | source)
XLA Modules:
  0.0 103.7 jit_solution(13572819028677515258)
XLA Ops:
  7.2 0.7 copy-done
  7.9 0.6 reduce-window.6
  8.9 0.3 fusion.35
  9.3 1.5 %copy.98 = bf16[1,256,2048]{1,2,0:T(8,128)(2,1)S(1)} copy(bf16[1,256,2048]{2,1,0:T(8,128)(2,1)} %param.12) | data formatting | bytes 2097152 | tf_op jit(solution)/shard_map/reshape.8
  10.8 1.3 %copy.104 = bf16[32,8,16,128]{3,2,1,0:T(8,128)(2,1)} copy(bf16[32,8,16,128]{3,1,2,0:T(8,128)(2,1)S(1)} %bitcast.100) | data formatting | bytes 2097152
  12.1 2.8 %convolution_add_fusion = f32[16,128,128]{2,1,0:T(8,128)} fusion(bf16[256,16,128]{0,2,1:T(8,128)(2,1)S(1)} %bitcast.103, f32[256,16]{0,1:T(8,128)S(1)} %bitcast.113, bf16[256,16,128]{2,1,0:T(8,128)(2,1)} %bitcast.49, f32[16]{0:T(128)S(1)} %get-tuple-element.92), kind=kOutput, calls=%fused_computation.34 | convolution fusion | flops 136052736 | bytes 3162176 | tf_op jit(solution)/shard_map/bshd,bshe->bhde/dot_general | solution.py:42
  15.3 5.9 %all_gather.14 = bf16[512,2,128]{0,2,1:T(8,128)(2,1)S(1)} all-gather(bf16[256,2,128]{0,2,1:T(8,128)(2,1)S(1)} %bitcast.106), channel_id=1, replica_groups=mesh['ctx'=2,'tp'=4,'pp'=4] {'ctx'}, dimensions={0}, use_global_device_ids=true | all-gather | bytes 393216 | tf_op jit(solution)/shard_map/all_gather | solution.py:123
  21.2 4.5 %all_gather.15 = bf16[512,2,128]{0,2,1:T(8,128)(2,1)S(1)} all-gather(bf16[256,2,128]{0,2,1:T(8,128)(2,1)S(1)} %bitcast.105), channel_id=1, replica_groups=mesh['ctx'=2,'tp'=4,'pp'=4] {'ctx'}, dimensions={0}, use_global_device_ids=true | all-gather | bytes 393216 | tf_op jit(solution)/shard_map/all_gather | solution.py:124
  25.7 6.3 %conditional.1 = (f32[256,2,8]{0,2,1:T(8,128)S(1)}, f32[256,2,8,128]{3,0,2,1:T(8,128)S(1)}) conditional(s32[]{:T(128)} %convert_element_type.48, () %tuple.20, (s32[]{:T(128)}, s32[256]{0:T(256)S(1)}, bf16[1,256,2048]{2,1,0:T(8,128)(2,1)S(1)}, bf16[512,2,128]{0,2,1:T(8,128)(2,1)S(1)}, bf16[512,2,128]{0,2,1:T(8,128)(2,1)S(1)}) %tuple.38), branch_computations={%region_5.6_spmd, %region_6.9_spmd} | conditional | flops 1097478400 | bytes 31640596 | solution.py:141
  25.8 0.2 copy.99
  26.0 1.7 %fusion = (f32[256,2,8]{0,2,1:T(8,128)S(1)}, f32[2,512,256,8]{2,1,3,0:T(8,128)S(1)}) fusion(pred[256,512]{0,1:T(8,128)(4,1)S(1)} %iota_compare_fusion, bf16[256,2,8,128]{3,2,1,0:T(8,128)(2,1)S(1)} %bitcast.98, bf16[512,2,128]{0,2,1:T(8,128)(2,1)S(1)} %get-tuple-element.81), kind=kOutput, calls=%fused_computation.2 | convolution fusion | flops 543158272 | bytes 9846784 | tf_op jit(solution)/shard_map/cond/branch_1_fun/while/body/eval_jaxpr/tkgd,skd->tkgs/dot_general | solution.py:60
  27.7 1.7 %fusion.4 = f32[256,2,8]{0,2,1:T(8,128)S(1)} fusion(f32[2,512,256,8]{2,1,3,0:T(8,128)S(1)} %get-tuple-element.88, f32[256,2,8]{0,2,1:T(8,128)S(1)} %broadcast_maximum_fusion, pred[256,512]{0,1:T(8,128)(4,1)S(1)} %iota_compare_fusion), kind=kLoop, calls=%fused_computation.6 | loop fusion | flops 8384512 | bytes 8552448 | tf_op jit(solution)/shard_map/cond/branch_1_fun/while/body/eval_jaxpr/reduce_sum | solution.py:68
  29.4 2.6 %bitcast_add_fusion = f32[256,2,8,128]{3,0,2,1:T(8,128)S(1)} fusion(f32[2,512,256,8]{2,1,3,0:T(8,128)S(1)} %get-tuple-element.88, f32[256,2,8]{0,2,1:T(8,128)S(1)} %broadcast_maximum_fusion, pred[256,512]{0,1:T(8,128)(4,1)S(1)} %iota_compare_fusion, f32[256,2,8]{0,2,1:T(8,128)S(1)} %get-tuple-element.85, bf16[512,2,128]{0,2,1:T(8,128)(2,1)S(1)} %get-tuple-element.82), kind=kOutput, calls=%fused_computation.9 | convolution fusion | flops 545783808 | bytes 10911744 | tf_op jit(solution)/shard_map/cond/branch_1_fun/while/body/eval_jaxpr/tkgs,skd->tkgd/dot_general | solution.py:69
  32.0 0.7 divide_convert_fusion
  32.7 0.7 copy.79
  33.4 1.3 %broadcast_in_dim_reshape.3 = bf16[1,256,2048]{2,1,0:T(8,128)(2,1)} reshape(bf16[256,2,8,128]{3,2,1,0:T(8,128)(2,1)S(1)} %copy.79) | data formatting | bytes 2097152 | tf_op jit(solution)/shard_map/broadcast_in_dim;reshape | solution.py:145
  34.7 1.2 %collective-permute-start.1 = (bf16[1,256,2048]{2,1,0:T(8,128)(2,1)}, bf16[1,256,2048]{2,1,0:T(8,128)(2,1)}, u32[]{:S(2)}, u32[]{:S(2)}) collective-permute-start(bf16[1,256,2048]{2,1,0:T(8,128)(2,1)} %broadcast_in_dim_reshape.3), channel_id=1, source_target_pairs={{3,0},{0,1},{1,2},{2,3},{7,4},{4,5},{5,6},{6,7},{11,8},{8,9},{9,10... | collective-permute-start | bytes 3145736 | tf_op jit(solution)/shard_map/ppermute | solution.py:21
  36.0 3.6 %all-gather = f32[2,1,16]{2,1,0:T(1,128)S(1)} all-gather(f32[1,1,16]{2,1,0:T(1,128)S(1)} %copy.70), channel_id=2, replica_groups=mesh['ctx'=2,'tp'=4,'pp'=4] {'ctx'}, dimensions={0}, use_global_device_ids=true | all-gather | bytes 192 | tf_op jit(solution)/shard_map/all_gather | solution.py:99
  39.7 0.2 copy.101
  40.1 4.4 %fusion.20 = f32[16,256,128]{1,2,0:T(8,128)} fusion(bf16[256,16,128]{0,2,1:T(8,128)(2,1)S(1)} %bitcast.104, f32[16,256]{1,0:T(8,128)S(1)} %bitcast_add_fusion.3, pred[256,256]{1,0:T(8,128)(4,1)S(1)} %iota_compare_fusion.1, bf16[256,16,128]{2,1,0:T(8,128)(2,1)} %bitcast.49, bf16[256,16,128]{2,1,0:T(8,128)(2,1)S(1)} %bitcast.94), kind=kOutput, calls=%fused_computation.33 | convolution fusion | flops 542113792 | bytes 5324800 | tf_op jit(solution)/shard_map/bhts,bshd->bthd/dot_general | solution.py:38
  44.5 5.8 %all-gather.4.cloned.1.call-done = f32[32,128,128]{2,1,0:T(8,128)} async-done(((f32[16,128,128]{2,1,0:T(8,128)}), f32[32,128,128]{2,1,0:T(8,128)}) %all-gather.4.cloned.1.call-update) | async-done | bytes 2097168 | tf_op jit(solution)/shard_map/all_gather | solution.py:98
  50.3 1.9 %multiply_reduce_fusion = f32[16,128,128]{2,1,0:T(8,128)S(1)} fusion(f32[16,2,128,128]{3,2,0,1:T(8,128)} %bitcast.99, f32[16,2]{0,1:T(2,128)S(1)} %select_bitcast_fusion), kind=kLoop, calls=%fused_computation.24 | loop fusion | flops 786432 | bytes 3145856 | tf_op jit(solution)/shard_map/jh,jhde->hde/dot_general | solution.py:109
  52.2 3.0 %fusion.17 = f32[16,128,256]{2,1,0:T(8,128)S(1)} fusion(f32[16,128,128]{2,1,0:T(8,128)S(1)} %multiply_reduce_fusion, f32[16]{0:T(128)S(1)} %get-tuple-element.91, f32[256,16]{0,1:T(8,128)S(1)} %bitcast.107, bf16[256,16,128]{2,1,0:T(8,128)(2,1)S(1)} %bitcast.95), kind=kOutput, calls=%fused_computation.28 | convolution fusion | flops 806879232 | bytes 4210752 | tf_op jit(solution)/shard_map/bthd,hde->bthe/dot_general | solution.py:110
  55.2 2.8 %multiply_reduce_fusion.1 = (f32[256,16]{0,1:T(8,128)S(1)}, f32[1,256,16,128]{1,3,2,0:T(8,128)S(1)}) fusion(f32[16,128,256]{2,1,0:T(8,128)S(1)} %fusion.17, f32[256,16]{0,1:T(8,128)S(1)} %bitcast.108, bf16[256,16,128]{2,1,0:T(8,128)(2,1)S(1)} %bitcast.96, f32[16,256,128]{1,2,0:T(8,128)S(1)} %copy-done.2), kind=kOutput, calls=%fused_computation.27 | convolution fusion | flops 808448000 | bytes 7372800 | tf_op jit(solution)/shard_map/bthd,bhde->bthe/dot_general | solution.py:52
  58.0 1.9 %copy.74 = f32[1,256,2048]{2,1,0:T(8,128)} copy(f32[1,256,2048]{1,2,0:T(8,128)S(1)} %bitcast.97) | data formatting | bytes 4194304 | tf_op jit(solution)/shard_map/reshape | solution.py:111
  60.0 1.9 %mul.139 = f32[256,16,128]{2,1,0:T(8,128)} broadcast(f32[256,16]{1,0:T(8,128)S(1)} %copy.73), dimensions={0,1} | broadcast | bytes 2113536 | tf_op jit(solution)/shard_map/mul | solution.py:112
  61.9 2.8 %mul.140 = f32[1,256,2048]{2,1,0:T(8,128)} reshape(f32[256,16,128]{2,1,0:T(8,128)} %mul.139) | data formatting | bytes 4194304 | tf_op jit(solution)/shard_map/mul | solution.py:112
  64.8 2.2 %multiply_convert_fusion.1 = bf16[1,256,2048]{2,1,0:T(8,128)(2,1)S(1)} fusion(bf16[1,256,2048]{2,1,0:T(8,128)(2,1)S(1)} %copy-done.8, f32[1,256,2048]{2,1,0:T(8,128)S(1)} %copy-done.1, f32[1,256,2048]{2,1,0:T(8,128)} %mul.140, f32[2048]{0:T(1024)S(1)} %bitcast.114), kind=kLoop, calls=%fused_computation.26 | loop fusion | flops 4194304 | bytes 6299648 | tf_op jit(solution)/shard_map/convert_element_type | solution.py:117
  67.0 1.5 %collective-permute-start = (bf16[1,256,2048]{2,1,0:T(8,128)(2,1)S(1)}, bf16[1,256,2048]{2,1,0:T(8,128)(2,1)S(1)}, u32[]{:S(2)}, u32[]{:S(2)}) collective-permute-start(bf16[1,256,2048]{2,1,0:T(8,128)(2,1)S(1)} %multiply_convert_fusion.1), channel_id=1, source_target_pairs={{3,0},{0,1},{1,2},{2,3},{7,4},{4,5},{5,6},{6,7},{11,8},{8,9},{9,10... | collective-permute-start | bytes 3145736 | tf_op jit(solution)/shard_map/ppermute | solution.py:21
  68.5 25.0 %collective-permute-done = bf16[1,256,2048]{2,1,0:T(8,128)(2,1)S(1)} collective-permute-done((bf16[1,256,2048]{2,1,0:T(8,128)(2,1)S(1)}, bf16[1,256,2048]{2,1,0:T(8,128)(2,1)S(1)}, u32[]{:S(2)}, u32[]{:S(2)}) %collective-permute-start) | collective-permute-done | bytes 1048608 | tf_op jit(solution)/shard_map/ppermute | solution.py:21
  93.6 1.0 copy.139
  94.5 2.3 %copy.140 = bf16[1,256,2048]{2,1,0:T(8,128)(2,1)} copy(bf16[1,256,2048]{2,1,0:T(8,128)(2,1)} %collective-permute-done.1) | data formatting | bytes 2097152
  (55 shorter events, 1.4 us)
Async XLA Ops:
  7.2 0.7 copy-start
  7.2 3.6 %copy-start.3 = (bf16[1,256,2048]{2,1,0:T(8,128)(2,1)S(1)}, bf16[1,256,2048]{2,1,0:T(8,128)(2,1)}, u32[]{:S(2)}) copy-start(bf16[1,256,2048]{2,1,0:T(8,128)(2,1)} %param.13) | copy-start | bytes 3145732
  7.2 43.1 %all-gather.4.cloned.1.call-start = ((), (), s32[]{:S(2)}) async-start(), calls=%async_computation | async-start | bytes 3145728 | tf_op jit(solution)/shard_map/all_gather | solution.py:98
  10.8 4.1 %copy-start.6 = (bf16[1,256,2048]{1,2,0:T(8,128)(2,1)}, bf16[1,256,2048]{1,2,0:T(8,128)(2,1)S(1)}, u32[]{:S(2)}) copy-start(bf16[1,256,2048]{1,2,0:T(8,128)(2,1)S(1)} %copy.98) | copy-start | bytes 3145732
  12.1 2.9 %copy-start.9 = (bf16[1,256,256]{2,1,0:T(8,128)(2,1)S(1)}, bf16[1,256,256]{2,1,0:T(8,128)(2,1)}, u32[]{:S(2)}) copy-start(bf16[1,256,256]{2,1,0:T(8,128)(2,1)} %param.18) | copy-start | bytes 393220
  12.1 3.0 %copy-start.10 = (bf16[1,256,256]{2,1,0:T(8,128)(2,1)S(1)}, bf16[1,256,256]{2,1,0:T(8,128)(2,1)}, u32[]{:S(2)}) copy-start(bf16[1,256,256]{2,1,0:T(8,128)(2,1)} %param.19) | copy-start | bytes 393220
  12.1 13.6 %copy-start.4 = (bf16[1,256,2048]{2,1,0:T(8,128)(2,1)S(1)}, bf16[1,256,2048]{2,1,0:T(8,128)(2,1)}, u32[]{:S(2)}) copy-start(bf16[1,256,2048]{2,1,0:T(8,128)(2,1)} %param.17) | copy-start | bytes 3145732
  32.7 6.9 %copy-start.5 = (bf16[1,256,2048]{2,1,0:T(8,128)(2,1)S(1)}, bf16[1,256,2048]{2,1,0:T(8,128)(2,1)}, u32[]{:S(2)}) copy-start(bf16[1,256,2048]{2,1,0:T(8,128)(2,1)} %param.11) | copy-start | bytes 3145732
  33.4 6.7 %copy-start.7 = (bf16[1,256,2048]{1,2,0:T(8,128)(2,1)S(1)}, bf16[1,256,2048]{1,2,0:T(8,128)(2,1)}, u32[]{:S(2)}) copy-start(bf16[1,256,2048]{1,2,0:T(8,128)(2,1)} %copy-done.6) | copy-start | bytes 3145732
  34.7 33.8 %collective-permute-start.1 = (bf16[1,256,2048]{2,1,0:T(8,128)(2,1)}, bf16[1,256,2048]{2,1,0:T(8,128)(2,1)}, u32[]{:S(2)}, u32[]{:S(2)}) collective-permute-start(bf16[1,256,2048]{2,1,0:T(8,128)(2,1)} %broadcast_in_dim_reshape.3), channel_id=1, source_target_pairs={{3,0},{0,1},{1,2},{2,3},{7,4},{4,5},{5,6},{6,7},{11,8},{8,9},{9,10... | collective-permute-start | bytes 3145736 | tf_op jit(solution)/shard_map/ppermute | solution.py:21
  52.2 3.0 %copy-start.2 = (f32[16,256,128]{1,2,0:T(8,128)S(1)}, f32[16,256,128]{1,2,0:T(8,128)}, u32[]{:S(2)}) copy-start(f32[16,256,128]{1,2,0:T(8,128)} %fusion.20) | copy-start | bytes 6291460
  61.9 2.8 %copy-start.1 = (f32[1,256,2048]{2,1,0:T(8,128)S(1)}, f32[1,256,2048]{2,1,0:T(8,128)}, u32[]{:S(2)}) copy-start(f32[1,256,2048]{2,1,0:T(8,128)} %copy.74) | copy-start | bytes 6291460
  61.9 2.8 %copy-start.8 = (bf16[1,256,2048]{2,1,0:T(8,128)(2,1)S(1)}, bf16[1,256,2048]{2,1,0:T(8,128)(2,1)}, u32[]{:S(2)}) copy-start(bf16[1,256,2048]{2,1,0:T(8,128)(2,1)} %param.15) | copy-start | bytes 3145732
  61.9 2.8 %copy-start.11 = (f32[1,2048]{1,0:T(1,128)S(1)}, f32[1,2048]{1,0:T(1,128)}, u32[]{:S(2)}) copy-start(f32[1,2048]{1,0:T(1,128)} %param.16) | copy-start | bytes 24580
  67.0 26.6 %collective-permute-start = (bf16[1,256,2048]{2,1,0:T(8,128)(2,1)S(1)}, bf16[1,256,2048]{2,1,0:T(8,128)(2,1)S(1)}, u32[]{:S(2)}, u32[]{:S(2)}) collective-permute-start(bf16[1,256,2048]{2,1,0:T(8,128)(2,1)S(1)} %multiply_convert_fusion.1), channel_id=1, source_target_pairs={{3,0},{0,1},{1,2},{2,3},{7,4},{4,5},{5,6},{6,7},{11,8},{8,9},{9,10... | collective-permute-start | bytes 3145736 | tf_op jit(solution)/shard_map/ppermute | solution.py:21
Sparse Core Ops, SparseCore 0:
  15.1 35.1 all-gather.3
where the time goes:
time: 105 us; the launch traced here: 104 us
  waiting for transfers between devices  30.8 us (29%)
  matrix products  17.2 us (16%)
  local copies, waits for them, and re-layouts  16.8 us (16%)
  between operations  14.3 us (14%)
  blocking collectives  14 us (13%)
  other arithmetic  7.62 us (7%)
  starting transfers between devices  2.83 us (3%)
    ppermute x2, waiting for transfers between devices, passed_along(): return lax.ppermute(block, axis, route)  25 us
    all_gather x1, blocking collectives, local(): key_piece = lax.all_gather(key_rows, 'ctx', axis=0, tiled=True)  5.92 us
    all_gather x1, waiting for transfers between devices, local(): lax.all_gather(closing[None], 'ctx', axis=0, tiled=True)  5.78 us
    unnamed x32, local copies, waits for them, and re-layouts  5.69 us
    mul x2, local copies, waits for them, and re-layouts, local(): mixture * lax.rsqrt(jnp.mean(mixture * mixture, axis=-1, keepdims=True) +...  4.77 us
    all_gather x1, blocking collectives, local(): value_piece = lax.all_gather(value_rows, 'ctx', axis=0, tiled=True)  4.48 us
    dot_general x1, matrix products, lightning_local(): jnp.einsum('bhts,bshd->bthd', weights, values_all, preferred_element_type...  4.42 us
    all_gather x1, blocking collectives, local(): lax.all_gather(device_log[None, :], 'ctx', axis=0, tiled=True)  3.64 us
  transfers between devices with their start and end apart: 3, of which 2 were waited for; matrix products, arithmetic and copies ran while one was open for 30% of the time, Pallas kernels for 0%

commit v1 on v0

v1 whole, which is shorter than its diff:
```python
import functools

import jax
import jax.numpy as jnp
from jax import lax
from jax.experimental import pallas as pl
from jax.experimental.pallas import tpu as pltpu
from jax.sharding import PartitionSpec as P

HEADS = 64
KV_HEADS = 8
HD = 128
BLK = 256
GROUP = HEADS // KV_HEADS
HALF = BLK // 2

epsilon = 1e-06
lowest = -1e30
LOG2E = 1.4426950408889634
MIB = 1 << 20


def passed_along(block, axis, distance):
    devices = lax.axis_size(axis)
    return lax.ppermute(block, axis, [((i - distance) % devices, i) for i in range(devices)])


def running_sums(decay_rows):
    total = decay_rows
    place = lax.broadcasted_iota(jnp.int32, total.shape, 1)
    reach = 1
    while reach < total.shape[1]:
        total = total + jnp.where(place >= reach, pltpu.roll(total, reach, 1), 0.0)
        reach *= 2
    return total


def turned(rows):
    fill = jnp.zeros((HD - rows.shape[0], rows.shape[1]), rows.dtype)
    return jnp.transpose(jnp.concatenate([rows, fill], axis=0))


def states_kernel(key_ref, value_ref, decay_ref, state_ref):
    running = running_sums(decay_ref[0])
    press = turned(jnp.exp(running[:, BLK - 1 :] - running))
    for h in range(state_ref.shape[0]):
        lanes = slice(h * HD, (h + 1) * HD)
        pressed = (key_ref[0, :, lanes].astype(jnp.float32) * press[:, h : h + 1]).astype(jnp.bfloat16)
        state_ref[h] = lax.dot_general(
            pressed, value_ref[0, :, lanes], (((0,), (0,)), ((), ())), preferred_element_type=jnp.float32
        ).astype(state_ref.dtype)


def closing_states(lin_key, lin_value, decay_rows, part, parts):
    heads = decay_rows.shape[1] // parts
    wide = pl.BlockSpec((1, BLK, heads * HD), lambda i: (0, 0, part))
    return pl.pallas_call(
        states_kernel,
        grid=(1,),
        in_specs=[wide, wide, pl.BlockSpec((1, heads, BLK), lambda i: (0, part, 0))],
        out_specs=pl.BlockSpec((heads, HD, HD), lambda i: (0, 0, 0)),
        out_shape=jax.ShapeDtypeStruct((heads, HD, HD), jnp.bfloat16),
        compiler_params=pltpu.CompilerParams(vmem_limit_bytes=16 * MIB),
        name="closing_states",
    )(lin_key, lin_value, decay_rows)


def mix_kernel(query_ref, key_ref, value_ref, decay_ref, gate_ref, gain_ref, state_ref, out_ref):
    running = running_sums(decay_ref[0])
    columns = turned(running)
    lift = jnp.exp(columns)
    causal = lax.broadcasted_iota(jnp.int32, (HALF, HALF), 0) >= lax.broadcasted_iota(
        jnp.int32, (HALF, HALF), 1
    )
    turned_dims = (((1,), (1,)), ((), ()))
    for h in range(state_ref.shape[0]):
        lanes = slice(h * HD, (h + 1) * HD)
        queries = query_ref[0, :, lanes]
        keys = key_ref[0, :, lanes]
        values = value_ref[0, :, lanes]
        column = columns[:, h : h + 1]
        row = running[h : h + 1, :]
        earlier = jnp.dot(queries, state_ref[h], preferred_element_type=jnp.float32) * lift[:, h : h + 1]
        parts = []
        for b in range(2):
            rows = slice(b * HALF, (b + 1) * HALF)
            seen = (b + 1) * HALF
            scores = lax.dot_general(
                queries[rows], keys[:seen], turned_dims, preferred_element_type=jnp.float32
            )
            pieces = []
            for c in range(b + 1):
                span = slice(c * HALF, (c + 1) * HALF)
                gap = column[rows] - row[:, span]
                if c == b:
                    fall = jnp.where(causal, jnp.exp(jnp.where(causal, gap, 0.0)), 0.0)
                else:
                    fall = jnp.exp(gap)
                pieces.append((scores[:, span] * fall).astype(jnp.bfloat16))
            weights = pieces[0] if b == 0 else jnp.concatenate(pieces, axis=1)
            parts.append(jnp.dot(weights, values[:seen], preferred_element_type=jnp.float32))
        mixture = jnp.concatenate(parts, axis=0) + earlier
        scale = lax.rsqrt(jnp.mean(mixture * mixture, axis=1, keepdims=True) + epsilon)
        gate = jax.nn.sigmoid(gate_ref[0, :, lanes].astype(jnp.float32))
        out_ref[0, :, lanes] = (mixture * scale * gain_ref[0:1, lanes] * gate).astype(out_ref.dtype)


def lightning(lin_query, lin_key, lin_value, decay_rows, out_gate, norm_gain, incoming, part, parts):
    heads = decay_rows.shape[1] // parts
    wide = pl.BlockSpec((1, BLK, heads * HD), lambda i: (0, 0, part))
    return pl.pallas_call(
        mix_kernel,
        grid=(1,),
        in_specs=[
            wide,
            wide,
            wide,
            pl.BlockSpec((1, heads, BLK), lambda i: (0, part, 0)),
            wide,
            pl.BlockSpec((1, heads * HD), lambda i: (0, part)),
            pl.BlockSpec((heads, HD, HD), lambda i: (0, 0, 0)),
        ],
        out_specs=pl.BlockSpec((1, BLK, heads * HD), lambda i: (0, 0, 0)),
        out_shape=jax.ShapeDtypeStruct((1, BLK, heads * HD), jnp.bfloat16),
        compiler_params=pltpu.CompilerParams(vmem_limit_bytes=20 * MIB),
        name="lightning_mix",
    )(lin_query, lin_key, lin_value, decay_rows, out_gate, norm_gain, incoming)


def pack_kernel(query_ref, key_ref, value_ref, raw_ref, *refs):
    pair_refs, sems = refs[:-1], refs[-1]
    width = GROUP * HD
    copies = [
        (key_ref.at[:, :, pl.ds(0, HD)], raw_ref.at[:, :, pl.ds(width, HD)]),
        (value_ref.at[:, :, pl.ds(0, HD)], raw_ref.at[:, :, pl.ds(width + HD, HD)]),
        (query_ref.at[:, :, pl.ds(0, width)], raw_ref.at[:, :, pl.ds(0, width)]),
    ]
    for i, pair_ref in enumerate(pair_refs):
        lanes = pl.ds((i + 1) * HD, HD)
        copies.append((key_ref.at[:, :, lanes], pair_ref.at[:, :, pl.ds(0, HD)]))
        copies.append((value_ref.at[:, :, lanes], pair_ref.at[:, :, pl.ds(HD, HD)]))
    started = [pltpu.make_async_copy(a, b, sems.at[i]) for i, (a, b) in enumerate(copies)]
    for copy in started:
        copy.start()
    for copy in started:
        copy.wait()


def packed(soft_query, soft_key, soft_value):
    kv_count = soft_key.shape[2] // HD
    in_hbm = pl.BlockSpec(memory_space=pltpu.HBM)
    in_vmem = pl.BlockSpec(memory_space=pltpu.VMEM)
    widths = [(GROUP + 2) * HD] + [2 * HD] * (kv_count - 1)
    return pl.pallas_call(
        pack_kernel,
        in_specs=[in_hbm] * 3,
        out_specs=[in_vmem] * kv_count,
        out_shape=[jax.ShapeDtypeStruct((1, BLK, width), jnp.bfloat16) for width in widths],
        scratch_shapes=[pltpu.SemaphoreType.DMA((1 + 2 * kv_count,))],
        compiler_params=pltpu.CompilerParams(vmem_limit_bytes=60 * MIB),
        name="packed",
    )(soft_query, soft_key, soft_value)


def attend(place, query_ref, key_ref, value_ref, before_ref, out_ref):
    others = before_ref.shape[0]
    factor = HD ** (-0.5) * LOG2E
    causal = lax.broadcasted_iota(jnp.int32, (BLK, BLK), 0) >= lax.broadcasted_iota(jnp.int32, (BLK, BLK), 1)
    turned_dims = (((1,), (1,)), ((), ()))
    keys, values = slice(0, HD), slice(HD, 2 * HD)

    def scored(queries, keys):
        return lax.dot_general(queries, keys, turned_dims, preferred_element_type=jnp.float32)

    for h in range(GROUP):
        lanes = slice(h * HD, (h + 1) * HD)
        queries = query_ref[0, :, lanes]
        own = jnp.where(causal, scored(queries, key_ref[0]), lowest)
        peak = jnp.max(own, axis=1, keepdims=True)
        if others == 1:
            before = jnp.where(place > 0, scored(queries, before_ref[0, :, keys]), lowest)
            peak = jnp.maximum(peak, jnp.max(before, axis=1, keepdims=True))
            own = jnp.exp2((own - peak) * factor)
            before = jnp.exp2((before - peak) * factor)
            totals = jnp.sum(own, axis=1, keepdims=True) + jnp.sum(before, axis=1, keepdims=True)
            weighted = jnp.dot(
                own.astype(jnp.bfloat16), value_ref[0], preferred_element_type=jnp.float32
            ) + jnp.dot(
                before.astype(jnp.bfloat16), before_ref[0, :, values], preferred_element_type=jnp.float32
            )
        else:
            own = jnp.exp2((own - peak) * factor)
            totals = jnp.sum(own, axis=1, keepdims=True)
            weighted = jnp.dot(
                own.astype(jnp.bfloat16), value_ref[0], preferred_element_type=jnp.float32
            )

            def absorb(turn, kept):
                peak, totals, weighted = kept
                scores = scored(queries, before_ref[turn, :, keys])
                new_peak = jnp.maximum(peak, jnp.max(scores, axis=1, keepdims=True))
                shrink = jnp.exp2((peak - new_peak) * factor)
                scores = jnp.exp2((scores - new_peak) * factor)
                totals = totals * shrink + jnp.sum(scores, axis=1, keepdims=True)
                weighted = weighted * shrink + jnp.dot(
                    scores.astype(jnp.bfloat16),
                    before_ref[turn, :, values],
                    preferred_element_type=jnp.float32,
                )
                return (new_peak, totals, weighted)

            peak, totals, weighted = lax.fori_loop(0, place, absorb, (peak, totals, weighted))
        out_ref[0, :, lanes] = (weighted / totals).astype(out_ref.dtype)


def soft_kernel(place_ref, query_ref, key_ref, value_ref, before_ref, out_ref):
    attend(place_ref[0], query_ref, key_ref, value_ref, before_ref, out_ref)


def soft_cost(others):
    return pl.CostEstimate(
        flops=4 * GROUP * BLK * BLK * (others + 1) * HD,
        bytes_accessed=5 * GROUP * BLK * HD,
        transcendentals=GROUP * BLK * BLK * (others + 1),
    )


def softmax_group(place, soft_query, pair, before, group):
    others = before.shape[0]
    wide = (1, BLK, GROUP * HD)
    return pl.pallas_call(
        soft_kernel,
        grid_spec=pltpu.PrefetchScalarGridSpec(
            num_scalar_prefetch=1,
            grid=(1,),
            in_specs=[
                pl.BlockSpec(wide, lambda i, place: (0, 0, group)),
                pl.BlockSpec((1, BLK, HD), lambda i, place: (0, 0, 0)),
                pl.BlockSpec((1, BLK, HD), lambda i, place: (0, 0, 1)),
                pl.BlockSpec((others, BLK, 2 * HD), lambda i, place: (0, 0, 0)),
            ],
            out_specs=pl.BlockSpec(wide, lambda i, place: (0, 0, 0)),
        ),
        out_shape=jax.ShapeDtypeStruct(wide, jnp.bfloat16),
        compiler_params=pltpu.CompilerParams(vmem_limit_bytes=20 * MIB),
        name="softmax_group",
    )(place, soft_query, pair, pair, before)


def finish_kernel(place_ref, query_ref, key_ref, value_ref, before_ref, ready_ref, out_ref):
    @pl.when(pl.program_id(0) == 0)
    def _():
        attend(place_ref[0], query_ref, key_ref, value_ref, before_ref, out_ref)

    @pl.when(pl.program_id(0) > 0)
    def _():
        out_ref[...] = ready_ref[...]


def softmax_finish(place, raw, before, ready):
    others = before.shape[0]
    wide = (1, BLK, GROUP * HD)
    groups = 1 + ready.shape[2] // (GROUP * HD)
    return pl.pallas_call(
        finish_kernel,
        grid_spec=pltpu.PrefetchScalarGridSpec(
            num_scalar_prefetch=1,
            grid=(groups,),
            in_specs=[
                pl.BlockSpec(wide, lambda i, place: (0, 0, 0)),
                pl.BlockSpec((1, BLK, HD), lambda i, place: (0, 0, GROUP)),
                pl.BlockSpec((1, BLK, HD), lambda i, place: (0, 0, GROUP + 1)),
                pl.BlockSpec((others, BLK, 2 * HD), lambda i, place: (0, 0, 0)),
                pl.BlockSpec(wide, lambda i, place: (0, 0, jnp.maximum(i - 1, 0))),
            ],
            out_specs=pl.BlockSpec(wide, lambda i, place: (0, 0, i)),
        ),
        out_shape=jax.ShapeDtypeStruct((1, BLK, groups * GROUP * HD), jnp.bfloat16),
        compiler_params=pltpu.CompilerParams(vmem_limit_bytes=20 * MIB),
        name="softmax_finish",
    )(place, raw, raw, raw, before, ready)


def place_kernel(part, block_ref, *refs):
    whole_ref, sem = refs[-2:]
    width = block_ref.shape[2]
    copy = pltpu.make_async_copy(block_ref, whole_ref.at[:, :, pl.ds(part * width, width)], sem)
    copy.start()
    copy.wait()


def placed(block, part, parts, whole=None):
    anywhere = pl.BlockSpec(memory_space=pl.ANY)
    operands = (block,) if whole is None else (block, whole)
    return pl.pallas_call(
        functools.partial(place_kernel, part),
        in_specs=[anywhere] * len(operands),
        out_specs=anywhere,
        out_shape=jax.ShapeDtypeStruct(block.shape[:2] + (parts * block.shape[2],), block.dtype),
        scratch_shapes=[pltpu.SemaphoreType.DMA],
        input_output_aliases={} if whole is None else {1: 0},
        compiler_params=pltpu.CompilerParams(vmem_limit_bytes=1 * MIB),
        name="placed",
    )(*operands)


def earlier_blocks(block):
    devices = lax.axis_size("ctx")
    if devices == 2:
        return lax.ppermute(block, "ctx", [(0, 1)])
    return lax.all_gather(block, "ctx", axis=0, tiled=True)[: devices - 1]


def incoming_states(closing, decay_rows):
    if lax.axis_size("ctx") == 2:
        return lax.ppermute(closing, "ctx", [(0, 1)])
    states = lax.all_gather(closing[None], "ctx", axis=0, tiled=True)
    logs = lax.all_gather(jnp.sum(decay_rows, axis=2), "ctx", axis=0, tiled=True)
    earlier = (lax.iota(jnp.int32, logs.shape[0]) < lax.axis_index("ctx"))[:, None]
    reached = jnp.sum(jnp.where(earlier, logs, 0.0), axis=0)
    rising = jnp.cumsum(logs, axis=0)
    weight = jnp.where(earlier, jnp.exp(jnp.where(earlier, reached[None, :] - rising, 0.0)), 0.0)
    return jnp.sum(weight[:, :, None, None] * states.astype(jnp.float32), axis=0).astype(jnp.bfloat16)


PARTS = 2


def local(
    lin_query, lin_key, lin_value, log_decay, out_gate, norm_gain, soft_query, soft_key, soft_value
):
    place = lax.axis_index("ctx").astype(jnp.int32)[None]
    decay_rows = jnp.swapaxes(log_decay, 1, 2)
    heads = decay_rows.shape[1] // PARTS
    raw, *pairs = packed(soft_query, soft_key, soft_value)
    handed_raw = passed_along(raw, "pp", 1)
    befores = [earlier_blocks(pair) for pair in pairs]
    ready = [
        passed_along(softmax_group(place, soft_query, pair, before, g + 1), "pp", 1)
        for g, (pair, before) in enumerate(zip(pairs, befores))
    ]
    ready = ready[0] if len(ready) == 1 else jnp.concatenate(ready, axis=2)
    lin_key, lin_value, *befores = lax.optimization_barrier((lin_key, lin_value, *befores))
    incoming = []
    for part in range(PARTS):
        closing = closing_states(lin_key, lin_value, decay_rows, part, PARTS)
        incoming.append(incoming_states(closing, decay_rows[:, part * heads : (part + 1) * heads]))
    incoming[0], handed_raw = lax.optimization_barrier((incoming[0], handed_raw))
    lin_parts = [
        passed_along(
            lightning(
                lin_query, lin_key, lin_value, decay_rows, out_gate, norm_gain, incoming[part], part, PARTS
            ),
            "pp",
            1,
        )
        for part in range(PARTS)
    ]
    before = earlier_blocks(handed_raw[:, :, GROUP * HD :])
    soft_handed = softmax_finish(place, handed_raw, before, ready)
    lin_handed = None
    for part in range(PARTS):
        lin_handed = placed(lin_parts[part], part, PARTS, lin_handed)
    return (lin_handed, soft_handed)


def solution(mesh):
    wide = P("pp", "ctx", "tp")
    return jax.shard_map(
        local,
        mesh=mesh,
        in_specs=(wide, wide, wide, wide, wide, P("pp", "tp"), wide, wide, wide),
        out_specs=(wide, wide),
        check_vma=False,
    )
```

time: 105 us -> 64.9 us (0.62)
  the two profiles are of different devices: /device:TPU:1 before, /device:TPU:0 now
where the time goes in v1:
time: 64.9 us; the launch traced here: 64.5 us
  starting transfers between devices  20.3 us (31%)
  waiting for transfers between devices  19.6 us (30%)
  Pallas kernels  18.9 us (29%)
  local copies, waits for them, and re-layouts  4.92 us (8%)
  between operations  0.77 us (1%)
    ppermute x4, waiting for transfers between devices, passed_along(): lax.ppermute(block, axis, [((i - distance) % devices, i) for i in range(d...  15.6 us
    ppermute x2, starting transfers between devices, earlier_blocks(): return lax.ppermute(block, 'ctx', [(0, 1)])  7.09 us
    ppermute x4, starting transfers between devices, passed_along(): lax.ppermute(block, axis, [((i - distance) % devices, i) for i in range(d...  6.67 us
    ppermute x2, starting transfers between devices, incoming_states(): return lax.ppermute(closing, 'ctx', [(0, 1)])  6.5 us
    pallas_call x2, Pallas kernels, lightning(): pl.pallas_call(mix_kernel, grid=(1,), in_specs=[wide, wide, wide, pl.Bloc...  5.57 us
    unnamed x18, local copies, waits for them, and re-layouts  4.91 us
    ppermute x2, waiting for transfers between devices, earlier_blocks(): return lax.ppermute(block, 'ctx', [(0, 1)])  3.97 us
    pallas_call x1, Pallas kernels, softmax_finish(): pl.pallas_call(finish_kernel, grid_spec=pltpu.PrefetchScalarGridSpec(num_...  3.61 us
  transfers between devices with their start and end apart: 8, of which 5 were waited for; matrix products, arithmetic and copies ran while one was open for 0% of the time, Pallas kernels for 25%

profile of v1, /device:TPU:0, one launch (start us, length us, event | category | flops | bytes accessed | tf_op | source)
XLA Modules:
  0.0 64.5 jit_solution(7200160601030565247)
XLA Ops:
  0.7 2.1 %packed.1 = (bf16[1,256,1280]{2,1,0:T(8,128)(2,1)}, bf16[1,256,256]{2,1,0:T(8,128)(2,1)}) custom-call(bf16[1,256,2048]{2,1,0:T(8,128)(2,1)} %query_ref.7, bf16[1,256,256]{2,1,0:T(8,128)(2,1)} %key_ref.1, bf16[1,256,256]{2,1,0:T(8,128)(2,1)} %value_ref.1), custom_call_target="tpu_custom_call" | custom-call | tf_op jit(solution)/shard_map/packed/pallas_call | solution.py:154
  2.8 3.1 %collective-permute-start.4 = (bf16[1,256,1280]{2,1,0:T(8,128)(2,1)}, bf16[1,256,1280]{2,1,0:T(8,128)(2,1)S(1)}, u32[]{:S(2)}, u32[]{:S(2)}) collective-permute-start(bf16[1,256,1280]{2,1,0:T(8,128)(2,1)} %get-tuple-element.11), channel_id=1, source_target_pairs={{3,0},{0,1},{1,2},{2,3},{7,4},{4,5},{5,6},{6,7},{11,8},{8,9},{9,10... | collective-permute-start | bytes 1966088 | tf_op jit(solution)/shard_map/ppermute | solution.py:25
  5.8 3.4 %collective-permute-start = (bf16[1,256,256]{2,1,0:T(8,128)(2,1)}, bf16[1,256,256]{2,1,0:T(8,128)(2,1)S(1)}, u32[]{:S(2)}, u32[]{:S(2)}) collective-permute-start(bf16[1,256,256]{2,1,0:T(8,128)(2,1)} %get-tuple-element.8.key_ref.value_ref), channel_id=1, source_target_pairs={{0,16},{1,17},{2,18},{3,19},{4,20},{5,21},{6,22},{7,23},{8,24},{9,... | collective-permute-start | bytes 393224 | tf_op jit(solution)/shard_map/ppermute | solution.py:310
  9.2 2.8 %collective-permute-done.before_ref = bf16[1,256,256]{2,1,0:T(8,128)(2,1)S(1)} collective-permute-done((bf16[1,256,256]{2,1,0:T(8,128)(2,1)}, bf16[1,256,256]{2,1,0:T(8,128)(2,1)S(1)}, u32[]{:S(2)}, u32[]{:S(2)}) %collective-permute-start) | collective-permute-done | bytes 131104 | tf_op jit(solution)/shard_map/ppermute | solution.py:310
  12.1 1.2 %copy-done.1 = bf16[1,256,2048]{2,1,0:T(8,128)(2,1)S(1)} copy-done((bf16[1,256,2048]{2,1,0:T(8,128)(2,1)S(1)}, bf16[1,256,2048]{2,1,0:T(8,128)(2,1)}, u32[]{:S(2)}) %copy-start.1) | copy-done | bytes 1048600
  13.3 2.1 %closing_states.3 = bf16[8,128,128]{2,1,0:T(8,128)(2,1)} custom-call(bf16[1,256,2048]{2,1,0:T(8,128)(2,1)S(1)} %copy-done, bf16[1,256,2048]{2,1,0:T(8,128)(2,1)S(1)} %copy-done.1, f32[1,16,256]{2,1,0:T(8,128)S(1)} %bitcast.2), custom_call_target="tpu_custom_call" | custom-call | tf_op jit(solution)/shard_map/closing_states/pallas_call | solution.py:57
  15.4 5.1 %collective-permute-start.3 = (bf16[8,128,128]{2,1,0:T(8,128)(2,1)}, bf16[8,128,128]{2,1,0:T(8,128)(2,1)}, u32[]{:S(2)}, u32[]{:S(2)}) collective-permute-start(bf16[8,128,128]{2,1,0:T(8,128)(2,1)} %closing_states.3), channel_id=1, source_target_pairs={{0,16},{1,17},{2,18},{3,19},{4,20},{5,21},{6,22},{7,23},{8,24},{9,... | collective-permute-start | bytes 786440 | tf_op jit(solution)/shard_map/ppermute | solution.py:316
  20.4 1.4 %closing_states.2 = bf16[8,128,128]{2,1,0:T(8,128)(2,1)S(1)} custom-call(bf16[1,256,2048]{2,1,0:T(8,128)(2,1)S(1)} %copy-done, bf16[1,256,2048]{2,1,0:T(8,128)(2,1)S(1)} %copy-done.1, f32[1,16,256]{2,1,0:T(8,128)S(1)} %bitcast.3), custom_call_target="tpu_custom_call" | custom-call | tf_op jit(solution)/shard_map/closing_states/pallas_call | solution.py:57
  21.8 0.0 copy-start.2
  21.8 1.4 %collective-permute-start.1 = (bf16[8,128,128]{2,1,0:T(8,128)(2,1)S(1)}, bf16[8,128,128]{2,1,0:T(8,128)(2,1)S(1)}, u32[]{:S(2)}, u32[]{:S(2)}) collective-permute-start(bf16[8,128,128]{2,1,0:T(8,128)(2,1)S(1)} %closing_states.2), channel_id=1, source_target_pairs={{0,16},{1,17},{2,18},{3,19},{4,20},{5,21},{6,22},{7,23},{8,24},{9,... | collective-permute-start | bytes 786440 | tf_op jit(solution)/shard_map/ppermute | solution.py:316
  23.3 0.0 copy-start.5
  23.3 1.2 %copy-done.5 = bf16[1,256,2048]{2,1,0:T(8,128)(2,1)S(1)} copy-done((bf16[1,256,2048]{2,1,0:T(8,128)(2,1)S(1)}, bf16[1,256,2048]{2,1,0:T(8,128)(2,1)}, u32[]{:S(2)}) %copy-start.5) | copy-done | bytes 1048600
  24.5 2.6 %softmax_group.1 = bf16[1,256,1024]{2,1,0:T(8,128)(2,1)S(1)} custom-call(s32[1]{0:T(128)} %bitcast.1.place_ref, bf16[1,256,2048]{2,1,0:T(8,128)(2,1)S(1)} %copy-done.5, bf16[1,256,256]{2,1,0:T(8,128)(2,1)S(1)} %copy-done.6, bf16[1,256,256]{2,1,0:T(8,128)(2,1)S(1)} %copy-done.6, bf16[1,256,256]{2,1,0:T(8,128)(2,1)S(1)} %collective-permute-done.before_ref), custom_call_target="tpu_custom_call" | custom-call | tf_op jit(solution)/shard_map/softmax_group/pallas_call | solution.py:231
  27.1 1.6 %collective-permute-start.7 = (bf16[1,256,1024]{2,1,0:T(8,128)(2,1)S(1)}, bf16[1,256,1024]{2,1,0:T(8,128)(2,1)S(1)}, u32[]{:S(2)}, u32[]{:S(2)}) collective-permute-start(bf16[1,256,1024]{2,1,0:T(8,128)(2,1)S(1)} %softmax_group.1), channel_id=1, source_target_pairs={{3,0},{0,1},{1,2},{2,3},{7,4},{4,5},{5,6},{6,7},{11,8},{8,9},{9,10... | collective-permute-start | bytes 1572872 | tf_op jit(solution)/shard_map/ppermute | solution.py:25
  28.8 0.0 collective-permute-done.3.state_ref
  28.8 0.0 collective-permute-done.4.query_ref.key_ref.value_ref
  28.8 0.0 copy-start.3
  28.8 1.2 %copy-done.3 = bf16[1,256,2048]{2,1,0:T(8,128)(2,1)S(1)} copy-done((bf16[1,256,2048]{2,1,0:T(8,128)(2,1)S(1)}, bf16[1,256,2048]{2,1,0:T(8,128)(2,1)}, u32[]{:S(2)}) %copy-start.3) | copy-done | bytes 1048600
  30.0 1.2 %copy-done.4 = bf16[1,256,2048]{2,1,0:T(8,128)(2,1)S(1)} copy-done((bf16[1,256,2048]{2,1,0:T(8,128)(2,1)S(1)}, bf16[1,256,2048]{2,1,0:T(8,128)(2,1)}, u32[]{:S(2)}) %copy-start.4) | copy-done | bytes 1048600
  31.2 3.3 %lightning_mix.3 = bf16[1,256,1024]{2,1,0:T(8,128)(2,1)S(1)} custom-call(bf16[1,256,2048]{2,1,0:T(8,128)(2,1)S(1)} %copy-done.3, bf16[1,256,2048]{2,1,0:T(8,128)(2,1)S(1)} %copy-done, bf16[1,256,2048]{2,1,0:T(8,128)(2,1)S(1)} %copy-done.2, f32[1,16,256]{2,1,0:T(8,128)S(1)} %bitcast.4, bf16[1,256,2048]{2,1,0:T(8,128)(2,1)S(1)} %copy-done.4, ...), custom_call_target="tpu_custom_call" | custom-call | tf_op jit(solution)/shard_map/lightning_mix/pallas_call | solution.py:111
  34.5 1.6 %collective-permute-start.5 = (bf16[1,256,1024]{2,1,0:T(8,128)(2,1)S(1)}, bf16[1,256,1024]{2,1,0:T(8,128)(2,1)S(1)}, u32[]{:S(2)}, u32[]{:S(2)}) collective-permute-start(bf16[1,256,1024]{2,1,0:T(8,128)(2,1)S(1)} %lightning_mix.3), channel_id=1, source_target_pairs={{3,0},{0,1},{1,2},{2,3},{7,4},{4,5},{5,6},{6,7},{11,8},{8,9},{9,10... | collective-permute-start | bytes 1572872 | tf_op jit(solution)/shard_map/ppermute | solution.py:25
  36.1 0.0 collective-permute-done.1.state_ref
  36.1 2.3 %lightning_mix.2 = bf16[1,256,1024]{2,1,0:T(8,128)(2,1)S(1)} custom-call(bf16[1,256,2048]{2,1,0:T(8,128)(2,1)S(1)} %copy-done.3, bf16[1,256,2048]{2,1,0:T(8,128)(2,1)S(1)} %copy-done, bf16[1,256,2048]{2,1,0:T(8,128)(2,1)S(1)} %copy-done.2, f32[1,16,256]{2,1,0:T(8,128)S(1)} %bitcast.5, bf16[1,256,2048]{2,1,0:T(8,128)(2,1)S(1)} %copy-done.4, ...), custom_call_target="tpu_custom_call" | custom-call | tf_op jit(solution)/shard_map/lightning_mix/pallas_call | solution.py:111
  38.4 0.3 collective-permute-start.2
  38.8 3.7 %collective-permute-start.6 = (bf16[1,256,256]{2,1,0:T(8,128)(2,1)S(1)}, bf16[1,256,256]{2,1,0:T(8,128)(2,1)S(1)}, u32[]{:S(2)}, u32[]{:S(2)}) collective-permute-start(bf16[1,256,256]{2,1,0:T(8,128)(2,1)S(1)} %slice.3), channel_id=1, source_target_pairs={{0,16},{1,17},{2,18},{3,19},{4,20},{5,21},{6,22},{7,23},{8,24},{9,... | collective-permute-start | bytes 393224 | tf_op jit(solution)/shard_map/ppermute | solution.py:310
  42.5 1.3 %collective-permute-done.7.ready_ref = bf16[1,256,1024]{2,1,0:T(8,128)(2,1)S(1)} collective-permute-done((bf16[1,256,1024]{2,1,0:T(8,128)(2,1)S(1)}, bf16[1,256,1024]{2,1,0:T(8,128)(2,1)S(1)}, u32[]{:S(2)}, u32[]{:S(2)}) %collective-permute-start.7) | collective-permute-done | bytes 524320 | tf_op jit(solution)/shard_map/ppermute | solution.py:25
  43.8 1.2 %collective-permute-done.6.before_ref = bf16[1,256,256]{2,1,0:T(8,128)(2,1)S(1)} collective-permute-done((bf16[1,256,256]{2,1,0:T(8,128)(2,1)S(1)}, bf16[1,256,256]{2,1,0:T(8,128)(2,1)S(1)}, u32[]{:S(2)}, u32[]{:S(2)}) %collective-permute-start.6) | collective-permute-done | bytes 131104 | tf_op jit(solution)/shard_map/ppermute | solution.py:310
  45.0 3.6 %softmax_finish.1 = bf16[1,256,2048]{2,1,0:T(8,128)(2,1)} custom-call(s32[1]{0:T(128)} %bitcast.1.place_ref, bf16[1,256,1280]{2,1,0:T(8,128)(2,1)S(1)} %collective-permute-done.4.query_ref.key_ref.value_ref, bf16[1,256,1280]{2,1,0:T(8,128)(2,1)S(1)} %collective-permute-done.4.query_ref.key_ref.value_ref, ...), custom_call_target="tpu_custom_call" | custom-call | tf_op jit(solution)/shard_map/softmax_finish/pallas_call | solution.py:264
  48.6 6.5 %collective-permute-done.5.block_ref = bf16[1,256,1024]{2,1,0:T(8,128)(2,1)S(1)} collective-permute-done((bf16[1,256,1024]{2,1,0:T(8,128)(2,1)S(1)}, bf16[1,256,1024]{2,1,0:T(8,128)(2,1)S(1)}, u32[]{:S(2)}, u32[]{:S(2)}) %collective-permute-start.5) | collective-permute-done | bytes 524320 | tf_op jit(solution)/shard_map/ppermute | solution.py:25
  55.1 0.8 %placed.2.refs_0_ = bf16[1,256,2048]{2,1,0:T(8,128)(2,1)} custom-call(bf16[1,256,1024]{2,1,0:T(8,128)(2,1)S(1)} %collective-permute-done.5.block_ref), custom_call_target="tpu_custom_call" | custom-call | tf_op jit(solution)/shard_map/placed/pallas_call | solution.py:295
  55.9 7.8 %collective-permute-done.2.block_ref = bf16[1,256,1024]{2,1,0:T(8,128)(2,1)S(1)} collective-permute-done((bf16[1,256,1024]{2,1,0:T(8,128)(2,1)S(1)}, bf16[1,256,1024]{2,1,0:T(8,128)(2,1)S(1)}, u32[]{:S(2)}, u32[]{:S(2)}) %collective-permute-start.2) | collective-permute-done | bytes 524320 | tf_op jit(solution)/shard_map/ppermute | solution.py:25
  63.7 0.8 %placed.3 = bf16[1,256,2048]{2,1,0:T(8,128)(2,1)} custom-call(bf16[1,256,1024]{2,1,0:T(8,128)(2,1)S(1)} %collective-permute-done.2.block_ref, bf16[1,256,2048]{2,1,0:T(8,128)(2,1)} %placed.2.refs_0_), custom_call_target="tpu_custom_call", output_to_operand_aliasing={{}: (1, {})} | custom-call | tf_op jit(solution)/shard_map/placed/pallas_call | solution.py:295
  (12 shorter events, 0.0 us)
Async XLA Ops:
  0.6 11.4 %copy-start = (bf16[1,256,2048]{2,1,0:T(8,128)(2,1)S(1)}, bf16[1,256,2048]{2,1,0:T(8,128)(2,1)}, u32[]{:S(2)}) copy-start(bf16[1,256,2048]{2,1,0:T(8,128)(2,1)} %key_ref.5) | copy-start | bytes 3145732
  0.6 11.4 %copy-start.7 = (f32[1,256,16]{1,2,0:T(8,128)S(1)}, f32[1,256,16]{1,2,0:T(8,128)}, u32[]{:S(2)}) copy-start(f32[1,256,16]{1,2,0:T(8,128)} %param.12) | copy-start | bytes 49156
  2.8 26.0 %collective-permute-start.4 = (bf16[1,256,1280]{2,1,0:T(8,128)(2,1)}, bf16[1,256,1280]{2,1,0:T(8,128)(2,1)S(1)}, u32[]{:S(2)}, u32[]{:S(2)}) collective-permute-start(bf16[1,256,1280]{2,1,0:T(8,128)(2,1)} %get-tuple-element.11), channel_id=1, source_target_pairs={{3,0},{0,1},{1,2},{2,3},{7,4},{4,5},{5,6},{6,7},{11,8},{8,9},{9,10... | collective-permute-start | bytes 1966088 | tf_op jit(solution)/shard_map/ppermute | solution.py:25
  5.8 6.2 %collective-permute-start = (bf16[1,256,256]{2,1,0:T(8,128)(2,1)}, bf16[1,256,256]{2,1,0:T(8,128)(2,1)S(1)}, u32[]{:S(2)}, u32[]{:S(2)}) collective-permute-start(bf16[1,256,256]{2,1,0:T(8,128)(2,1)} %get-tuple-element.8.key_ref.value_ref), channel_id=1, source_target_pairs={{0,16},{1,17},{2,18},{3,19},{4,20},{5,21},{6,22},{7,23},{8,24},{9,... | collective-permute-start | bytes 393224 | tf_op jit(solution)/shard_map/ppermute | solution.py:310
  12.1 1.2 %copy-start.1 = (bf16[1,256,2048]{2,1,0:T(8,128)(2,1)S(1)}, bf16[1,256,2048]{2,1,0:T(8,128)(2,1)}, u32[]{:S(2)}) copy-start(bf16[1,256,2048]{2,1,0:T(8,128)(2,1)} %value_ref.5) | copy-start | bytes 3145732
  15.4 7.9 %copy-start.6 = (bf16[1,256,256]{2,1,0:T(8,128)(2,1)S(1)}, bf16[1,256,256]{2,1,0:T(8,128)(2,1)}, u32[]{:S(2)}) copy-start(bf16[1,256,256]{2,1,0:T(8,128)(2,1)} %get-tuple-element.8.key_ref.value_ref) | copy-start | bytes 393220
  15.4 13.4 %collective-permute-start.3 = (bf16[8,128,128]{2,1,0:T(8,128)(2,1)}, bf16[8,128,128]{2,1,0:T(8,128)(2,1)}, u32[]{:S(2)}, u32[]{:S(2)}) collective-permute-start(bf16[8,128,128]{2,1,0:T(8,128)(2,1)} %closing_states.3), channel_id=1, source_target_pairs={{0,16},{1,17},{2,18},{3,19},{4,20},{5,21},{6,22},{7,23},{8,24},{9,... | collective-permute-start | bytes 786440 | tf_op jit(solution)/shard_map/ppermute | solution.py:316
  21.8 7.0 %copy-start.2 = (bf16[1,256,2048]{2,1,0:T(8,128)(2,1)S(1)}, bf16[1,256,2048]{2,1,0:T(8,128)(2,1)}, u32[]{:S(2)}) copy-start(bf16[1,256,2048]{2,1,0:T(8,128)(2,1)} %value_ref.5) | copy-start | bytes 3145732
  21.8 14.3 %collective-permute-start.1 = (bf16[8,128,128]{2,1,0:T(8,128)(2,1)S(1)}, bf16[8,128,128]{2,1,0:T(8,128)(2,1)S(1)}, u32[]{:S(2)}, u32[]{:S(2)}) collective-permute-start(bf16[8,128,128]{2,1,0:T(8,128)(2,1)S(1)} %closing_states.2), channel_id=1, source_target_pairs={{0,16},{1,17},{2,18},{3,19},{4,20},{5,21},{6,22},{7,23},{8,24},{9,... | collective-permute-start | bytes 786440 | tf_op jit(solution)/shard_map/ppermute | solution.py:316
  23.3 1.2 %copy-start.5 = (bf16[1,256,2048]{2,1,0:T(8,128)(2,1)S(1)}, bf16[1,256,2048]{2,1,0:T(8,128)(2,1)}, u32[]{:S(2)}) copy-start(bf16[1,256,2048]{2,1,0:T(8,128)(2,1)} %query_ref.7) | copy-start | bytes 3145732
  24.5 4.3 %copy-start.8 = (f32[1,2048]{1,0:T(1,128)S(1)}, f32[1,2048]{1,0:T(1,128)}, u32[]{:S(2)}) copy-start(f32[1,2048]{1,0:T(1,128)} %gain_ref.3) | copy-start | bytes 24580
  27.1 16.7 %collective-permute-start.7 = (bf16[1,256,1024]{2,1,0:T(8,128)(2,1)S(1)}, bf16[1,256,1024]{2,1,0:T(8,128)(2,1)S(1)}, u32[]{:S(2)}, u32[]{:S(2)}) collective-permute-start(bf16[1,256,1024]{2,1,0:T(8,128)(2,1)S(1)} %softmax_group.1), channel_id=1, source_target_pairs={{3,0},{0,1},{1,2},{2,3},{7,4},{4,5},{5,6},{6,7},{11,8},{8,9},{9,10... | collective-permute-start | bytes 1572872 | tf_op jit(solution)/shard_map/ppermute | solution.py:25
  28.8 1.2 %copy-start.3 = (bf16[1,256,2048]{2,1,0:T(8,128)(2,1)S(1)}, bf16[1,256,2048]{2,1,0:T(8,128)(2,1)}, u32[]{:S(2)}) copy-start(bf16[1,256,2048]{2,1,0:T(8,128)(2,1)} %query_ref.6) | copy-start | bytes 3145732
  30.0 1.2 %copy-start.4 = (bf16[1,256,2048]{2,1,0:T(8,128)(2,1)S(1)}, bf16[1,256,2048]{2,1,0:T(8,128)(2,1)}, u32[]{:S(2)}) copy-start(bf16[1,256,2048]{2,1,0:T(8,128)(2,1)} %gate_ref.3) | copy-start | bytes 3145732
  34.5 20.6 %collective-permute-start.5 = (bf16[1,256,1024]{2,1,0:T(8,128)(2,1)S(1)}, bf16[1,256,1024]{2,1,0:T(8,128)(2,1)S(1)}, u32[]{:S(2)}, u32[]{:S(2)}) collective-permute-start(bf16[1,256,1024]{2,1,0:T(8,128)(2,1)S(1)} %lightning_mix.3), channel_id=1, source_target_pairs={{3,0},{0,1},{1,2},{2,3},{7,4},{4,5},{5,6},{6,7},{11,8},{8,9},{9,10... | collective-permute-start | bytes 1572872 | tf_op jit(solution)/shard_map/ppermute | solution.py:25
  38.4 25.3 %collective-permute-start.2 = (bf16[1,256,1024]{2,1,0:T(8,128)(2,1)S(1)}, bf16[1,256,1024]{2,1,0:T(8,128)(2,1)S(1)}, u32[]{:S(2)}, u32[]{:S(2)}) collective-permute-start(bf16[1,256,1024]{2,1,0:T(8,128)(2,1)S(1)} %lightning_mix.2), channel_id=1, source_target_pairs={{3,0},{0,1},{1,2},{2,3},{7,4},{4,5},{5,6},{6,7},{11,8},{8,9},{9,10... | collective-permute-start | bytes 1572872 | tf_op jit(solution)/shard_map/ppermute | solution.py:25
  38.8 6.2 %collective-permute-start.6 = (bf16[1,256,256]{2,1,0:T(8,128)(2,1)S(1)}, bf16[1,256,256]{2,1,0:T(8,128)(2,1)S(1)}, u32[]{:S(2)}, u32[]{:S(2)}) collective-permute-start(bf16[1,256,256]{2,1,0:T(8,128)(2,1)S(1)} %slice.3), channel_id=1, source_target_pairs={{0,16},{1,17},{2,18},{3,19},{4,20},{5,21},{6,22},{7,23},{8,24},{9,... | collective-permute-start | bytes 393224 | tf_op jit(solution)/shard_map/ppermute | solution.py:310

commit v2 on v1

--- a/solution.py
+++ b/solution.py
@@ -65,7 +65,7 @@
     )(lin_key, lin_value, decay_rows)
 
 
-def mix_kernel(query_ref, key_ref, value_ref, decay_ref, gate_ref, gain_ref, state_ref, out_ref):
+def mix_kernel(place_ref, query_ref, key_ref, value_ref, decay_ref, gate_ref, gain_ref, state_ref, *out_refs):
     running = running_sums(decay_ref[0])
     columns = turned(running)
     lift = jnp.exp(columns)
@@ -73,6 +73,10 @@
         jnp.int32, (HALF, HALF), 1
     )
     turned_dims = (((1,), (1,)), ((), ()))
+    owner = []
+    for out_ref in out_refs:
+        first = len(owner)
+        owner += [(out_ref, first)] * (out_ref.shape[2] // HD)
     for h in range(state_ref.shape[0]):
         lanes = slice(h * HD, (h + 1) * HD)
         queries = query_ref[0, :, lanes]
@@ -81,6 +85,7 @@
         column = columns[:, h : h + 1]
         row = running[h : h + 1, :]
         earlier = jnp.dot(queries, state_ref[h], preferred_element_type=jnp.float32) * lift[:, h : h + 1]
+        earlier = jnp.where(place_ref[0] > 0, earlier, 0.0)
         parts = []
         for b in range(2):
             rows = slice(b * HALF, (b + 1) * HALF)
@@ -102,62 +107,71 @@
         mixture = jnp.concatenate(parts, axis=0) + earlier
         scale = lax.rsqrt(jnp.mean(mixture * mixture, axis=1, keepdims=True) + epsilon)
         gate = jax.nn.sigmoid(gate_ref[0, :, lanes].astype(jnp.float32))
-        out_ref[0, :, lanes] = (mixture * scale * gain_ref[0:1, lanes] * gate).astype(out_ref.dtype)
-
-
-def lightning(lin_query, lin_key, lin_value, decay_rows, out_gate, norm_gain, incoming, part, parts):
+        result = mixture * scale * gain_ref[0:1, lanes] * gate
+        out_ref, first = owner[h]
+        lanes = slice((h - first) * HD, (h - first + 1) * HD)
+        out_ref[0, :, lanes] = result.astype(out_ref.dtype)
+
+
+def lightning(
+    place, lin_query, lin_key, lin_value, decay_rows, out_gate, norm_gain, incoming, part, parts, chunks
+):
     heads = decay_rows.shape[1] // parts
-    wide = pl.BlockSpec((1, BLK, heads * HD), lambda i: (0, 0, part))
+    wide = pl.BlockSpec((1, BLK, heads * HD), lambda i, place: (0, 0, part))
     return pl.pallas_call(
         mix_kernel,
-        grid=(1,),
-        in_specs=[
-            wide,
-            wide,
-            wide,
-            pl.BlockSpec((1, heads, BLK), lambda i: (0, part, 0)),
-            wide,
-            pl.BlockSpec((1, heads * HD), lambda i: (0, part)),
-            pl.BlockSpec((heads, HD, HD), lambda i: (0, 0, 0)),
-        ],
-        out_specs=pl.BlockSpec((1, BLK, heads * HD), lambda i: (0, 0, 0)),
-        out_shape=jax.ShapeDtypeStruct((1, BLK, heads * HD), jnp.bfloat16),
+        grid_spec=pltpu.PrefetchScalarGridSpec(
+            num_scalar_prefetch=1,
+            grid=(1,),
+            in_specs=[
+                wide,
+                wide,
+                wide,
+                pl.BlockSpec((1, heads, BLK), lambda i, place: (0, part, 0)),
+                wide,
+                pl.BlockSpec((1, heads * HD), lambda i, place: (0, part)),
+                pl.BlockSpec((heads, HD, HD), lambda i, place: (0, 0, 0)),
+            ],
+            out_specs=[pl.BlockSpec((1, BLK, n * HD), lambda i, place: (0, 0, 0)) for n in chunks],
+        ),
+        out_shape=[jax.ShapeDtypeStruct((1, BLK, n * HD), jnp.bfloat16) for n in chunks],
         compiler_params=pltpu.CompilerParams(vmem_limit_bytes=20 * MIB),
         name="lightning_mix",
-    )(lin_query, lin_key, lin_value, decay_rows, out_gate, norm_gain, incoming)
+    )(place, lin_query, lin_key, lin_value, decay_rows, out_gate, norm_gain, incoming)
+
+
+def copied(pieces, sems):
+    copies = [pltpu.make_async_copy(a, b, sems.at[i]) for i, (a, b) in enumerate(pieces)]
+    for copy in copies:
+        copy.start()
+    for copy in copies:
+        copy.wait()
 
 
 def pack_kernel(query_ref, key_ref, value_ref, raw_ref, *refs):
-    pair_refs, sems = refs[:-1], refs[-1]
     width = GROUP * HD
-    copies = [
+    pieces = [
+        (query_ref.at[:, :, pl.ds(0, width)], raw_ref.at[:, :, pl.ds(0, width)]),
         (key_ref.at[:, :, pl.ds(0, HD)], raw_ref.at[:, :, pl.ds(width, HD)]),
         (value_ref.at[:, :, pl.ds(0, HD)], raw_ref.at[:, :, pl.ds(width + HD, HD)]),
-        (query_ref.at[:, :, pl.ds(0, width)], raw_ref.at[:, :, pl.ds(0, width)]),
     ]
-    for i, pair_ref in enumerate(pair_refs):
+    for i, pair_ref in enumerate(refs[:-1]):
         lanes = pl.ds((i + 1) * HD, HD)
-        copies.append((key_ref.at[:, :, lanes], pair_ref.at[:, :, pl.ds(0, HD)]))
-        copies.append((value_ref.at[:, :, lanes], pair_ref.at[:, :, pl.ds(HD, HD)]))
-    started = [pltpu.make_async_copy(a, b, sems.at[i]) for i, (a, b) in enumerate(copies)]
-    for copy in started:
-        copy.start()
-    for copy in started:
-        copy.wait()
+        pieces.append((key_ref.at[:, :, lanes], pair_ref.at[:, :, pl.ds(0, HD)]))
+        pieces.append((value_ref.at[:, :, lanes], pair_ref.at[:, :, pl.ds(HD, HD)]))
+    copied(pieces, refs[-1])
 
 
 def packed(soft_query, soft_key, soft_value):
     kv_count = soft_key.shape[2] // HD
-    in_hbm = pl.BlockSpec(memory_space=pltpu.HBM)
-    in_vmem = pl.BlockSpec(memory_space=pltpu.VMEM)
     widths = [(GROUP + 2) * HD] + [2 * HD] * (kv_count - 1)
     return pl.pallas_call(
         pack_kernel,
-        in_specs=[in_hbm] * 3,
-        out_specs=[in_vmem] * kv_count,
-        out_shape=[jax.ShapeDtypeStruct((1, BLK, width), jnp.bfloat16) for width in widths],
+        in_specs=[pl.BlockSpec(memory_space=pltpu.HBM)] * 3,
+        out_specs=[pl.BlockSpec(memory_space=pltpu.VMEM)] * kv_count,
+        out_shape=[pltpu.VMEM((1, BLK, width), jnp.bfloat16) for width in widths],
         scratch_shapes=[pltpu.SemaphoreType.DMA((1 + 2 * kv_count,))],
-        compiler_params=pltpu.CompilerParams(vmem_limit_bytes=60 * MIB),
+        compiler_params=pltpu.CompilerParams(vmem_limit_bytes=4 * MIB),
         name="packed",
     )(soft_query, soft_key, soft_value)
 
@@ -172,7 +186,7 @@
     def scored(queries, keys):
         return lax.dot_general(queries, keys, turned_dims, preferred_element_type=jnp.float32)
 
-    for h in range(GROUP):
+    for h in range(query_ref.shape[2] // HD):
         lanes = slice(h * HD, (h + 1) * HD)
         queries = query_ref[0, :, lanes]
         own = jnp.where(causal, scored(queries, key_ref[0]), lowest)
@@ -217,61 +231,60 @@
     attend(place_ref[0], query_ref, key_ref, value_ref, before_ref, out_ref)
 
 
-def soft_cost(others):
-    return pl.CostEstimate(
-        flops=4 * GROUP * BLK * BLK * (others + 1) * HD,
-        bytes_accessed=5 * GROUP * BLK * HD,
-        transcendentals=GROUP * BLK * BLK * (others + 1),
-    )
+STEP = 8
 
 
 def softmax_group(place, soft_query, pair, before, group):
     others = before.shape[0]
-    wide = (1, BLK, GROUP * HD)
+    steps = GROUP // STEP
+    wide = (1, BLK, STEP * HD)
     return pl.pallas_call(
         soft_kernel,
         grid_spec=pltpu.PrefetchScalarGridSpec(
             num_scalar_prefetch=1,
-            grid=(1,),
+            grid=(steps,),
             in_specs=[
-                pl.BlockSpec(wide, lambda i, place: (0, 0, group)),
+                pl.BlockSpec(wide, lambda i, place: (0, 0, group * steps + i)),
                 pl.BlockSpec((1, BLK, HD), lambda i, place: (0, 0, 0)),
                 pl.BlockSpec((1, BLK, HD), lambda i, place: (0, 0, 1)),
                 pl.BlockSpec((others, BLK, 2 * HD), lambda i, place: (0, 0, 0)),
             ],
-            out_specs=pl.BlockSpec(wide, lambda i, place: (0, 0, 0)),
+            out_specs=pl.BlockSpec(wide, lambda i, place: (0, 0, i)),
         ),
-        out_shape=jax.ShapeDtypeStruct(wide, jnp.bfloat16),
+        out_shape=jax.ShapeDtypeStruct((1, BLK, GROUP * HD), jnp.bfloat16),
         compiler_params=pltpu.CompilerParams(vmem_limit_bytes=20 * MIB),
         name="softmax_group",
     )(place, soft_query, pair, pair, before)
 
 
 def finish_kernel(place_ref, query_ref, key_ref, value_ref, before_ref, ready_ref, out_ref):
-    @pl.when(pl.program_id(0) == 0)
+    here = pl.program_id(0) < GROUP // STEP
+
+    @pl.when(here)
     def _():
         attend(place_ref[0], query_ref, key_ref, value_ref, before_ref, out_ref)
 
-    @pl.when(pl.program_id(0) > 0)
+    @pl.when(jnp.logical_not(here))
     def _():
         out_ref[...] = ready_ref[...]
 
 
 def softmax_finish(place, raw, before, ready):
     others = before.shape[0]
-    wide = (1, BLK, GROUP * HD)
+    steps = GROUP // STEP
+    wide = (1, BLK, STEP * HD)
     groups = 1 + ready.shape[2] // (GROUP * HD)
     return pl.pallas_call(
         finish_kernel,
         grid_spec=pltpu.PrefetchScalarGridSpec(
             num_scalar_prefetch=1,
-            grid=(groups,),
+            grid=(groups * steps,),
             in_specs=[
-                pl.BlockSpec(wide, lambda i, place: (0, 0, 0)),
+                pl.BlockSpec(wide, lambda i, place: (0, 0, jnp.minimum(i, steps - 1))),
                 pl.BlockSpec((1, BLK, HD), lambda i, place: (0, 0, GROUP)),
                 pl.BlockSpec((1, BLK, HD), lambda i, place: (0, 0, GROUP + 1)),
                 pl.BlockSpec((others, BLK, 2 * HD), lambda i, place: (0, 0, 0)),
-                pl.BlockSpec(wide, lambda i, place: (0, 0, jnp.maximum(i - 1, 0))),
+                pl.BlockSpec(wide, lambda i, place: (0, 0, jnp.maximum(i - steps, 0))),
             ],
             out_specs=pl.BlockSpec(wide, lambda i, place: (0, 0, i)),
         ),
@@ -281,23 +294,20 @@
     )(place, raw, raw, raw, before, ready)
 
 
-def place_kernel(part, block_ref, *refs):
-    whole_ref, sem = refs[-2:]
-    width = block_ref.shape[2]
-    copy = pltpu.make_async_copy(block_ref, whole_ref.at[:, :, pl.ds(part * width, width)], sem)
-    copy.start()
-    copy.wait()
-
-
-def placed(block, part, parts, whole=None):
+def place_kernel(start, block_ref, *refs):
+    whole_ref, sems = refs[-2:]
+    copied([(block_ref, whole_ref.at[:, :, pl.ds(start, block_ref.shape[2])])], sems)
+
+
+def placed(block, start, width, whole=None):
     anywhere = pl.BlockSpec(memory_space=pl.ANY)
     operands = (block,) if whole is None else (block, whole)
     return pl.pallas_call(
-        functools.partial(place_kernel, part),
+        functools.partial(place_kernel, start),
         in_specs=[anywhere] * len(operands),
         out_specs=anywhere,
-        out_shape=jax.ShapeDtypeStruct(block.shape[:2] + (parts * block.shape[2],), block.dtype),
-        scratch_shapes=[pltpu.SemaphoreType.DMA],
+        out_shape=jax.ShapeDtypeStruct(block.shape[:2] + (width,), block.dtype),
+        scratch_shapes=[pltpu.SemaphoreType.DMA((1,))],
         input_output_aliases={} if whole is None else {1: 0},
         compiler_params=pltpu.CompilerParams(vmem_limit_bytes=1 * MIB),
         name="placed",
@@ -307,13 +317,13 @@
 def earlier_blocks(block):
     devices = lax.axis_size("ctx")
     if devices == 2:
-        return lax.ppermute(block, "ctx", [(0, 1)])
+        return passed_along(block, "ctx", 1)
     return lax.all_gather(block, "ctx", axis=0, tiled=True)[: devices - 1]
 
 
 def incoming_states(closing, decay_rows):
     if lax.axis_size("ctx") == 2:
-        return lax.ppermute(closing, "ctx", [(0, 1)])
+        return passed_along(closing, "ctx", 1)
     states = lax.all_gather(closing[None], "ctx", axis=0, tiled=True)
     logs = lax.all_gather(jnp.sum(decay_rows, axis=2), "ctx", axis=0, tiled=True)
     earlier = (lax.iota(jnp.int32, logs.shape[0]) < lax.axis_index("ctx"))[:, None]
@@ -324,43 +334,59 @@
 
 
 PARTS = 2
+LAST = 2
 
 
 def local(
     lin_query, lin_key, lin_value, log_decay, out_gate, norm_gain, soft_query, soft_key, soft_value
 ):
     place = lax.axis_index("ctx").astype(jnp.int32)[None]
+    lin_query, lin_key, lin_value, out_gate, soft_query, soft_key, soft_value = (
+        pltpu.with_memory_space_constraint(x, pltpu.HBM)
+        for x in (lin_query, lin_key, lin_value, out_gate, soft_query, soft_key, soft_value)
+    )
     decay_rows = jnp.swapaxes(log_decay, 1, 2)
     heads = decay_rows.shape[1] // PARTS
     raw, *pairs = packed(soft_query, soft_key, soft_value)
     handed_raw = passed_along(raw, "pp", 1)
     befores = [earlier_blocks(pair) for pair in pairs]
+    lin_key, lin_value, raw = lax.optimization_barrier((lin_key, lin_value, raw))
+    closing = [closing_states(lin_key, lin_value, decay_rows, part, PARTS) for part in range(PARTS)]
+    closing[0], *befores = lax.optimization_barrier((closing[0], *befores))
     ready = [
-        passed_along(softmax_group(place, soft_query, pair, before, g + 1), "pp", 1)
+        softmax_group(place, soft_query, pair, before, g + 1)
         for g, (pair, before) in enumerate(zip(pairs, befores))
     ]
-    ready = ready[0] if len(ready) == 1 else jnp.concatenate(ready, axis=2)
-    lin_key, lin_value, *befores = lax.optimization_barrier((lin_key, lin_value, *befores))
-    incoming = []
-    for part in range(PARTS):
-        closing = closing_states(lin_key, lin_value, decay_rows, part, PARTS)
-        incoming.append(incoming_states(closing, decay_rows[:, part * heads : (part + 1) * heads]))
-    incoming[0], handed_raw = lax.optimization_barrier((incoming[0], handed_raw))
-    lin_parts = [
-        passed_along(
-            lightning(
-                lin_query, lin_key, lin_value, decay_rows, out_gate, norm_gain, incoming[part], part, PARTS
-            ),
-            "pp",
-            1,
-        )
+    incoming = [
+        incoming_states(closing[part], decay_rows[:, part * heads : (part + 1) * heads])
         for part in range(PARTS)
     ]
+    ready = [passed_along(group, "pp", 1) for group in ready]
+    ready = ready[0] if len(ready) == 1 else jnp.concatenate(ready, axis=2)
+    incoming[0], handed_raw = lax.optimization_barrier((incoming[0], handed_raw))
+    chunks = []
+    for part in range(PARTS):
+        chunks += lightning(
+            place,
+            lin_query,
+            lin_key,
+            lin_value,
+            decay_rows,
+            out_gate,
+            norm_gain,
+            incoming[part],
+            part,
+            PARTS,
+            [heads - LAST, LAST] if part == PARTS - 1 else [heads],
+        )
+    chunks = [passed_along(chunk, "pp", 1) for chunk in chunks]
     before = earlier_blocks(handed_raw[:, :, GROUP * HD :])
     soft_handed = softmax_finish(place, handed_raw, before, ready)
     lin_handed = None
-    for part in range(PARTS):
-        lin_handed = placed(lin_parts[part], part, PARTS, lin_handed)
+    start = 0
+    for chunk in chunks:
+        lin_handed = placed(chunk, start, lin_query.shape[2], lin_handed)
+        start += chunk.shape[2]
     return (lin_handed, soft_handed)
 
 

time: 64.9 us -> 56.2 us (0.87)
  starting transfers between devices: 20.3 us -> 13.1 us
  local copies, waits for them, and re-layouts: 4.92 us -> 0.02 us
  Pallas kernels: 18.9 us -> 23.1 us
    ppermute x4 -> x0, starting transfers between devices: 13.6 us -> none  [the longest x2 7.09 us: earlier_blocks(): return lax.ppermute(block, 'ctx', [(0, 1)])]
    ppermute x4 -> x9, starting transfers between devices: 6.67 us -> 13.1 us  [passed_along(): lax.ppermute(block, axis, [((i - distance) % devices, i) for i in range(d...]
    unnamed x18 -> x4, local copies, waits for them, and re-layouts: 4.91 us -> 0.01 us
    ppermute x4 -> x0, waiting for transfers between devices: 3.98 us -> none  [the longest x2 3.97 us: earlier_blocks(): return lax.ppermute(block, 'ctx', [(0, 1)])]
    ppermute x4 -> x9, waiting for transfers between devices: 15.6 us -> 19 us  [passed_along(): lax.ppermute(block, axis, [((i - distance) % devices, i) for i in range(d...]
    pallas_call x2, Pallas kernels: 3.45 us -> 5.11 us  [closing_states(): pl.pallas_call(states_kernel, grid=(1,), in_specs=[wide, wide, pl.BlockSp...]
    pallas_call x5 -> x6, Pallas kernels: 9.28 us -> 10.7 us  [the longest x2 7.4 us: lightning(): pl.pallas_call(mix_kernel, grid_spec=pltpu.PrefetchScalarGridSpec(num_sca...]
    pallas_call x1, Pallas kernels: 2.61 us -> 3.64 us  [softmax_group(): pl.pallas_call(soft_kernel, grid_spec=pltpu.PrefetchScalarGridSpec(num_sc...]
  transfers between devices with their start and end apart: 8 -> 9, of which waited for: 5 -> 7; matrix products, arithmetic and copies ran while one was open for 0% -> 0% of each run, Pallas kernels for 25% -> 38%
where the time goes in v2:
time: 56.2 us; the launch traced here: 56 us
  Pallas kernels  23.1 us (41%)
  waiting for transfers between devices  19 us (34%)
  starting transfers between devices  13.1 us (23%)
  between operations  0.72 us (1%)
    ppermute x9, waiting for transfers between devices, passed_along(): lax.ppermute(block, axis, [((i - distance) % devices, i) for i in range(d...  19 us
    ppermute x9, starting transfers between devices, passed_along(): lax.ppermute(block, axis, [((i - distance) % devices, i) for i in range(d...  13.1 us
    pallas_call x2, Pallas kernels, lightning(): pl.pallas_call(mix_kernel, grid_spec=pltpu.PrefetchScalarGridSpec(num_sca...  7.4 us
    pallas_call x2, Pallas kernels, closing_states(): pl.pallas_call(states_kernel, grid=(1,), in_specs=[wide, wide, pl.BlockSp...  5.11 us
    pallas_call x1, Pallas kernels, softmax_finish(): pl.pallas_call(finish_kernel, grid_spec=pltpu.PrefetchScalarGridSpec(num_...  3.66 us
    pallas_call x1, Pallas kernels, softmax_group(): pl.pallas_call(soft_kernel, grid_spec=pltpu.PrefetchScalarGridSpec(num_sc...  3.64 us
    pallas_call x3, Pallas kernels, placed(): pl.pallas_call(functools.partial(place_kernel, start), in_specs=[anywhere...  2.22 us
  transfers between devices with their start and end apart: 9, of which 7 were waited for; matrix products, arithmetic and copies ran while one was open for 0% of the time, Pallas kernels for 38%

profile of v2, /device:TPU:0, one launch (start us, length us, event | category | flops | bytes accessed | tf_op | source)
XLA Modules:
  0.0 56.0 jit_solution(7571555668594378603)
XLA Ops:
  0.6 0.0 copy-start
  0.6 1.1 %packed.1 = (bf16[1,256,1280]{2,1,0:T(8,128)(2,1)S(1)}, bf16[1,256,256]{2,1,0:T(8,128)(2,1)S(1)}) custom-call(bf16[1,256,2048]{2,1,0:T(8,128)(2,1)} %query_ref.7, bf16[1,256,256]{2,1,0:T(8,128)(2,1)} %key_ref.1, bf16[1,256,256]{2,1,0:T(8,128)(2,1)} %value_ref.1), custom_call_target="tpu_custom_call" | custom-call | tf_op jit(solution)/shard_map/packed/pallas_call | solution.py:168
  1.8 3.1 %collective-permute-start.5 = (bf16[1,256,1280]{2,1,0:T(8,128)(2,1)S(1)}, bf16[1,256,1280]{2,1,0:T(8,128)(2,1)S(1)}, u32[]{:S(2)}, u32[]{:S(2)}) collective-permute-start(bf16[1,256,1280]{2,1,0:T(8,128)(2,1)S(1)} %get-tuple-element.12), channel_id=1, source_target_pairs={{3,0},{0,1},{1,2},{2,3},{7,4},{4,5},{5,6},{6,7},{11,8},{8,9},{9,10... | collective-permute-start | bytes 1966088 | tf_op jit(solution)/shard_map/ppermute | solution.py:25
  4.8 1.5 %collective-permute-start.3 = (bf16[1,256,256]{2,1,0:T(8,128)(2,1)S(1)}, bf16[1,256,256]{2,1,0:T(8,128)(2,1)S(1)}, u32[]{:S(2)}, u32[]{:S(2)}) collective-permute-start(bf16[1,256,256]{2,1,0:T(8,128)(2,1)S(1)} %get-tuple-element.17.key_ref.value_ref), channel_id=1, source_target_pairs={{16,0},{0,16},{17,1},{1,17},{18,2},{2,18},{19,3},{3,19},{20,4},{4,... | collective-permute-start | bytes 393224 | tf_op jit(solution)/shard_map/ppermute | solution.py:25
  6.3 0.0 copy-done
  6.3 2.6 %closing_states.3 = bf16[8,128,128]{2,1,0:T(8,128)(2,1)S(1)} custom-call(bf16[1,256,2048]{2,1,0:T(8,128)(2,1)} %key_ref.5, bf16[1,256,2048]{2,1,0:T(8,128)(2,1)} %value_ref.5, f32[1,16,256]{2,1,0:T(8,128)S(1)} %bitcast.2), custom_call_target="tpu_custom_call" | custom-call | tf_op jit(solution)/shard_map/closing_states/pallas_call | solution.py:57
  8.9 0.9 %collective-permute-done.3.before_ref = bf16[1,256,256]{2,1,0:T(8,128)(2,1)S(1)} collective-permute-done((bf16[1,256,256]{2,1,0:T(8,128)(2,1)S(1)}, bf16[1,256,256]{2,1,0:T(8,128)(2,1)S(1)}, u32[]{:S(2)}, u32[]{:S(2)}) %collective-permute-start.3) | collective-permute-done | bytes 131104 | tf_op jit(solution)/shard_map/ppermute | solution.py:25
  9.8 1.5 %collective-permute-start.4 = (bf16[8,128,128]{2,1,0:T(8,128)(2,1)S(1)}, bf16[8,128,128]{2,1,0:T(8,128)(2,1)S(1)}, u32[]{:S(2)}, u32[]{:S(2)}) collective-permute-start(bf16[8,128,128]{2,1,0:T(8,128)(2,1)S(1)} %closing_states.3), channel_id=1, source_target_pairs={{16,0},{0,16},{17,1},{1,17},{18,2},{2,18},{19,3},{3,19},{20,4},{4,... | collective-permute-start | bytes 786440 | tf_op jit(solution)/shard_map/ppermute | solution.py:25
  11.3 2.6 %closing_states.2 = bf16[8,128,128]{2,1,0:T(8,128)(2,1)S(1)} custom-call(bf16[1,256,2048]{2,1,0:T(8,128)(2,1)} %key_ref.5, bf16[1,256,2048]{2,1,0:T(8,128)(2,1)} %value_ref.5, f32[1,16,256]{2,1,0:T(8,128)S(1)} %bitcast.3), custom_call_target="tpu_custom_call" | custom-call | tf_op jit(solution)/shard_map/closing_states/pallas_call | solution.py:57
  13.9 0.6 %collective-permute-start = (bf16[8,128,128]{2,1,0:T(8,128)(2,1)S(1)}, bf16[8,128,128]{2,1,0:T(8,128)(2,1)S(1)}, u32[]{:S(2)}, u32[]{:S(2)}) collective-permute-start(bf16[8,128,128]{2,1,0:T(8,128)(2,1)S(1)} %closing_states.2), channel_id=1, source_target_pairs={{16,0},{0,16},{17,1},{1,17},{18,2},{2,18},{19,3},{3,19},{20,4},{4,... | collective-permute-start | bytes 786440 | tf_op jit(solution)/shard_map/ppermute | solution.py:25
  14.4 0.0 copy-start.1
  14.5 3.6 %softmax_group.1 = bf16[1,256,1024]{2,1,0:T(8,128)(2,1)S(1)} custom-call(s32[1]{0:T(128)} %bitcast.place_ref, bf16[1,256,2048]{2,1,0:T(8,128)(2,1)} %query_ref.7, bf16[1,256,256]{2,1,0:T(8,128)(2,1)S(1)} %get-tuple-element.17.key_ref.value_ref, bf16[1,256,256]{2,1,0:T(8,128)(2,1)S(1)} %get-tuple-element.17.key_ref.value_ref, ...), custom_call_target="tpu_custom_call" | custom-call | tf_op jit(solution)/shard_map/softmax_group/pallas_call | solution.py:241
  18.1 1.6 %collective-permute-start.8 = (bf16[1,256,1024]{2,1,0:T(8,128)(2,1)S(1)}, bf16[1,256,1024]{2,1,0:T(8,128)(2,1)S(1)}, u32[]{:S(2)}, u32[]{:S(2)}) collective-permute-start(bf16[1,256,1024]{2,1,0:T(8,128)(2,1)S(1)} %softmax_group.1), channel_id=1, source_target_pairs={{3,0},{0,1},{1,2},{2,3},{7,4},{4,5},{5,6},{6,7},{11,8},{8,9},{9,10... | collective-permute-start | bytes 1572872 | tf_op jit(solution)/shard_map/ppermute | solution.py:25
  19.7 0.0 collective-permute-done.4.state_ref
  19.7 2.7 %collective-permute-done.5.query_ref.key_ref.value_ref = bf16[1,256,1280]{2,1,0:T(8,128)(2,1)S(1)} collective-permute-done((bf16[1,256,1280]{2,1,0:T(8,128)(2,1)S(1)}, bf16[1,256,1280]{2,1,0:T(8,128)(2,1)S(1)}, u32[]{:S(2)}, u32[]{:S(2)}) %collective-permute-start.5) | collective-permute-done | bytes 655392 | tf_op jit(solution)/shard_map/ppermute | solution.py:25
  22.4 0.0 copy-done.1
  22.4 3.7 %lightning_mix.3 = bf16[1,256,1024]{2,1,0:T(8,128)(2,1)S(1)} custom-call(s32[1]{0:T(128)} %bitcast.place_ref, bf16[1,256,2048]{2,1,0:T(8,128)(2,1)} %query_ref.6, bf16[1,256,2048]{2,1,0:T(8,128)(2,1)} %key_ref.5, bf16[1,256,2048]{2,1,0:T(8,128)(2,1)} %value_ref.5, f32[1,16,256]{2,1,0:T(8,128)S(1)} %bitcast.4, bf16[1,256,2048]{2,1,0:T(8,128)(2,1)} %gate_ref.3, ...), custom_call_target="tpu_custom_call" | custom-call | tf_op jit(solution)/shard_map/lightning_mix/pallas_call | solution.py:121
  26.1 0.1 collective-permute-start.6
  26.2 0.0 collective-permute-done.state_ref
  26.2 3.7 %lightning_mix.2 = (bf16[1,256,768]{2,1,0:T(8,128)(2,1)S(1)}, bf16[1,256,256]{2,1,0:T(8,128)(2,1)S(1)}) custom-call(s32[1]{0:T(128)} %bitcast.place_ref, bf16[1,256,2048]{2,1,0:T(8,128)(2,1)} %query_ref.6, bf16[1,256,2048]{2,1,0:T(8,128)(2,1)} %key_ref.5, bf16[1,256,2048]{2,1,0:T(8,128)(2,1)} %value_ref.5, f32[1,16,256]{2,1,0:T(8,128)S(1)} %bitcast.5, ...), custom_call_target="tpu_custom_call" | custom-call | tf_op jit(solution)/shard_map/lightning_mix/pallas_call | solution.py:121
  29.9 1.3 %collective-permute-start.2 = (bf16[1,256,768]{2,1,0:T(8,128)(2,1)S(1)}, bf16[1,256,768]{2,1,0:T(8,128)(2,1)S(1)}, u32[]{:S(2)}, u32[]{:S(2)}) collective-permute-start(bf16[1,256,768]{2,1,0:T(8,128)(2,1)S(1)} %get-tuple-element.16), channel_id=1, source_target_pairs={{3,0},{0,1},{1,2},{2,3},{7,4},{4,5},{5,6},{6,7},{11,8},{8,9},{9,10... | collective-permute-start | bytes 1179656 | tf_op jit(solution)/shard_map/ppermute | solution.py:25
  31.2 1.6 %collective-permute-start.7 = (bf16[1,256,256]{2,1,0:T(8,128)(2,1)S(1)}, bf16[1,256,256]{2,1,0:T(8,128)(2,1)S(1)}, u32[]{:S(2)}, u32[]{:S(2)}) collective-permute-start(bf16[1,256,256]{2,1,0:T(8,128)(2,1)S(1)} %slice.3), channel_id=1, source_target_pairs={{16,0},{0,16},{17,1},{1,17},{18,2},{2,18},{19,3},{3,19},{20,4},{4,... | collective-permute-start | bytes 393224 | tf_op jit(solution)/shard_map/ppermute | solution.py:25
  32.7 2.0 %collective-permute-start.1 = (bf16[1,256,256]{2,1,0:T(8,128)(2,1)S(1)}, bf16[1,256,256]{2,1,0:T(8,128)(2,1)S(1)}, u32[]{:S(2)}, u32[]{:S(2)}) collective-permute-start(bf16[1,256,256]{2,1,0:T(8,128)(2,1)S(1)} %get-tuple-element.15), channel_id=1, source_target_pairs={{3,0},{0,1},{1,2},{2,3},{7,4},{4,5},{5,6},{6,7},{11,8},{8,9},{9,10... | collective-permute-start | bytes 393224 | tf_op jit(solution)/shard_map/ppermute | solution.py:25
  34.7 0.1 collective-permute-done.8.ready_ref
  34.8 1.4 %collective-permute-done.7.before_ref = bf16[1,256,256]{2,1,0:T(8,128)(2,1)S(1)} collective-permute-done((bf16[1,256,256]{2,1,0:T(8,128)(2,1)S(1)}, bf16[1,256,256]{2,1,0:T(8,128)(2,1)S(1)}, u32[]{:S(2)}, u32[]{:S(2)}) %collective-permute-start.7) | collective-permute-done | bytes 131104 | tf_op jit(solution)/shard_map/ppermute | solution.py:25
  36.2 3.7 %softmax_finish.1 = bf16[1,256,2048]{2,1,0:T(8,128)(2,1)} custom-call(s32[1]{0:T(128)} %bitcast.place_ref, bf16[1,256,1280]{2,1,0:T(8,128)(2,1)S(1)} %collective-permute-done.5.query_ref.key_ref.value_ref, bf16[1,256,1280]{2,1,0:T(8,128)(2,1)S(1)} %collective-permute-done.5.query_ref.key_ref.value_ref, ...), custom_call_target="tpu_custom_call" | custom-call | tf_op jit(solution)/shard_map/softmax_finish/pallas_call | solution.py:277
  39.9 6.2 %collective-permute-done.6.block_ref = bf16[1,256,1024]{2,1,0:T(8,128)(2,1)S(1)} collective-permute-done((bf16[1,256,1024]{2,1,0:T(8,128)(2,1)S(1)}, bf16[1,256,1024]{2,1,0:T(8,128)(2,1)S(1)}, u32[]{:S(2)}, u32[]{:S(2)}) %collective-permute-start.6) | collective-permute-done | bytes 524320 | tf_op jit(solution)/shard_map/ppermute | solution.py:25
  46.0 0.8 %placed.3.refs_0_ = bf16[1,256,2048]{2,1,0:T(8,128)(2,1)} custom-call(bf16[1,256,1024]{2,1,0:T(8,128)(2,1)S(1)} %collective-permute-done.6.block_ref), custom_call_target="tpu_custom_call" | custom-call | tf_op jit(solution)/shard_map/placed/pallas_call | solution.py:305
  46.9 7.0 %collective-permute-done.2.block_ref = bf16[1,256,768]{2,1,0:T(8,128)(2,1)S(1)} collective-permute-done((bf16[1,256,768]{2,1,0:T(8,128)(2,1)S(1)}, bf16[1,256,768]{2,1,0:T(8,128)(2,1)S(1)}, u32[]{:S(2)}, u32[]{:S(2)}) %collective-permute-start.2) | collective-permute-done | bytes 393248 | tf_op jit(solution)/shard_map/ppermute | solution.py:25
  53.9 0.8 %placed.4.refs_0_ = bf16[1,256,2048]{2,1,0:T(8,128)(2,1)} custom-call(bf16[1,256,768]{2,1,0:T(8,128)(2,1)S(1)} %collective-permute-done.2.block_ref, bf16[1,256,2048]{2,1,0:T(8,128)(2,1)} %placed.3.refs_0_), custom_call_target="tpu_custom_call", output_to_operand_aliasing={{}: (1, {})} | custom-call | tf_op jit(solution)/shard_map/placed/pallas_call | solution.py:305
  54.7 0.6 %collective-permute-done.1.block_ref = bf16[1,256,256]{2,1,0:T(8,128)(2,1)S(1)} collective-permute-done((bf16[1,256,256]{2,1,0:T(8,128)(2,1)S(1)}, bf16[1,256,256]{2,1,0:T(8,128)(2,1)S(1)}, u32[]{:S(2)}, u32[]{:S(2)}) %collective-permute-start.1) | collective-permute-done | bytes 131104 | tf_op jit(solution)/shard_map/ppermute | solution.py:25
  55.3 0.7 %placed.5 = bf16[1,256,2048]{2,1,0:T(8,128)(2,1)} custom-call(bf16[1,256,256]{2,1,0:T(8,128)(2,1)S(1)} %collective-permute-done.1.block_ref, bf16[1,256,2048]{2,1,0:T(8,128)(2,1)} %placed.4.refs_0_), custom_call_target="tpu_custom_call", output_to_operand_aliasing={{}: (1, {})} | custom-call | tf_op jit(solution)/shard_map/placed/pallas_call | solution.py:305
  (1 shorter events, 0.0 us)
Async XLA Ops:
  0.6 5.7 %copy-start = (f32[1,256,16]{1,2,0:T(8,128)S(1)}, f32[1,256,16]{1,2,0:T(8,128)}, u32[]{:S(2)}) copy-start(f32[1,256,16]{1,2,0:T(8,128)} %param.12) | copy-start | bytes 49156
  1.8 20.7 %collective-permute-start.5 = (bf16[1,256,1280]{2,1,0:T(8,128)(2,1)S(1)}, bf16[1,256,1280]{2,1,0:T(8,128)(2,1)S(1)}, u32[]{:S(2)}, u32[]{:S(2)}) collective-permute-start(bf16[1,256,1280]{2,1,0:T(8,128)(2,1)S(1)} %get-tuple-element.12), channel_id=1, source_target_pairs={{3,0},{0,1},{1,2},{2,3},{7,4},{4,5},{5,6},{6,7},{11,8},{8,9},{9,10... | collective-permute-start | bytes 1966088 | tf_op jit(solution)/shard_map/ppermute | solution.py:25
  4.8 5.0 %collective-permute-start.3 = (bf16[1,256,256]{2,1,0:T(8,128)(2,1)S(1)}, bf16[1,256,256]{2,1,0:T(8,128)(2,1)S(1)}, u32[]{:S(2)}, u32[]{:S(2)}) collective-permute-start(bf16[1,256,256]{2,1,0:T(8,128)(2,1)S(1)} %get-tuple-element.17.key_ref.value_ref), channel_id=1, source_target_pairs={{16,0},{0,16},{17,1},{1,17},{18,2},{2,18},{19,3},{3,19},{20,4},{4,... | collective-permute-start | bytes 393224 | tf_op jit(solution)/shard_map/ppermute | solution.py:25
  9.8 9.9 %collective-permute-start.4 = (bf16[8,128,128]{2,1,0:T(8,128)(2,1)S(1)}, bf16[8,128,128]{2,1,0:T(8,128)(2,1)S(1)}, u32[]{:S(2)}, u32[]{:S(2)}) collective-permute-start(bf16[8,128,128]{2,1,0:T(8,128)(2,1)S(1)} %closing_states.3), channel_id=1, source_target_pairs={{16,0},{0,16},{17,1},{1,17},{18,2},{2,18},{19,3},{3,19},{20,4},{4,... | collective-permute-start | bytes 786440 | tf_op jit(solution)/shard_map/ppermute | solution.py:25
  13.9 12.3 %collective-permute-start = (bf16[8,128,128]{2,1,0:T(8,128)(2,1)S(1)}, bf16[8,128,128]{2,1,0:T(8,128)(2,1)S(1)}, u32[]{:S(2)}, u32[]{:S(2)}) collective-permute-start(bf16[8,128,128]{2,1,0:T(8,128)(2,1)S(1)} %closing_states.2), channel_id=1, source_target_pairs={{16,0},{0,16},{17,1},{1,17},{18,2},{2,18},{19,3},{3,19},{20,4},{4,... | collective-permute-start | bytes 786440 | tf_op jit(solution)/shard_map/ppermute | solution.py:25
  14.4 8.0 %copy-start.1 = (f32[1,2048]{1,0:T(1,128)S(1)}, f32[1,2048]{1,0:T(1,128)}, u32[]{:S(2)}) copy-start(f32[1,2048]{1,0:T(1,128)} %gain_ref.3) | copy-start | bytes 24580
  18.1 16.7 %collective-permute-start.8 = (bf16[1,256,1024]{2,1,0:T(8,128)(2,1)S(1)}, bf16[1,256,1024]{2,1,0:T(8,128)(2,1)S(1)}, u32[]{:S(2)}, u32[]{:S(2)}) collective-permute-start(bf16[1,256,1024]{2,1,0:T(8,128)(2,1)S(1)} %softmax_group.1), channel_id=1, source_target_pairs={{3,0},{0,1},{1,2},{2,3},{7,4},{4,5},{5,6},{6,7},{11,8},{8,9},{9,10... | collective-permute-start | bytes 1572872 | tf_op jit(solution)/shard_map/ppermute | solution.py:25
  26.1 19.9 %collective-permute-start.6 = (bf16[1,256,1024]{2,1,0:T(8,128)(2,1)S(1)}, bf16[1,256,1024]{2,1,0:T(8,128)(2,1)S(1)}, u32[]{:S(2)}, u32[]{:S(2)}) collective-permute-start(bf16[1,256,1024]{2,1,0:T(8,128)(2,1)S(1)} %lightning_mix.3), channel_id=1, source_target_pairs={{3,0},{0,1},{1,2},{2,3},{7,4},{4,5},{5,6},{6,7},{11,8},{8,9},{9,10... | collective-permute-start | bytes 1572872 | tf_op jit(solution)/shard_map/ppermute | solution.py:25
  29.9 24.0 %collective-permute-start.2 = (bf16[1,256,768]{2,1,0:T(8,128)(2,1)S(1)}, bf16[1,256,768]{2,1,0:T(8,128)(2,1)S(1)}, u32[]{:S(2)}, u32[]{:S(2)}) collective-permute-start(bf16[1,256,768]{2,1,0:T(8,128)(2,1)S(1)} %get-tuple-element.16), channel_id=1, source_target_pairs={{3,0},{0,1},{1,2},{2,3},{7,4},{4,5},{5,6},{6,7},{11,8},{8,9},{9,10... | collective-permute-start | bytes 1179656 | tf_op jit(solution)/shard_map/ppermute | solution.py:25
  31.2 5.0 %collective-permute-start.7 = (bf16[1,256,256]{2,1,0:T(8,128)(2,1)S(1)}, bf16[1,256,256]{2,1,0:T(8,128)(2,1)S(1)}, u32[]{:S(2)}, u32[]{:S(2)}) collective-permute-start(bf16[1,256,256]{2,1,0:T(8,128)(2,1)S(1)} %slice.3), channel_id=1, source_target_pairs={{16,0},{0,16},{17,1},{1,17},{18,2},{2,18},{19,3},{3,19},{20,4},{4,... | collective-permute-start | bytes 393224 | tf_op jit(solution)/shard_map/ppermute | solution.py:25
  32.7 22.6 %collective-permute-start.1 = (bf16[1,256,256]{2,1,0:T(8,128)(2,1)S(1)}, bf16[1,256,256]{2,1,0:T(8,128)(2,1)S(1)}, u32[]{:S(2)}, u32[]{:S(2)}) collective-permute-start(bf16[1,256,256]{2,1,0:T(8,128)(2,1)S(1)} %get-tuple-element.15), channel_id=1, source_target_pairs={{3,0},{0,1},{1,2},{2,3},{7,4},{4,5},{5,6},{6,7},{11,8},{8,9},{9,10... | collective-permute-start | bytes 393224 | tf_op jit(solution)/shard_map/ppermute | solution.py:25

commit v3 on v2

--- a/solution.py
+++ b/solution.py
@@ -40,26 +40,35 @@
     return jnp.transpose(jnp.concatenate([rows, fill], axis=0))
 
 
-def states_kernel(key_ref, value_ref, decay_ref, state_ref):
+def states_kernel(key_ref, value_ref, decay_ref, *state_refs):
     running = running_sums(decay_ref[0])
     press = turned(jnp.exp(running[:, BLK - 1 :] - running))
-    for h in range(state_ref.shape[0]):
+    states = []
+    for h in range(running.shape[0]):
         lanes = slice(h * HD, (h + 1) * HD)
         pressed = (key_ref[0, :, lanes].astype(jnp.float32) * press[:, h : h + 1]).astype(jnp.bfloat16)
-        state_ref[h] = lax.dot_general(
-            pressed, value_ref[0, :, lanes], (((0,), (0,)), ((), ())), preferred_element_type=jnp.float32
-        ).astype(state_ref.dtype)
-
-
-def closing_states(lin_key, lin_value, decay_rows, part, parts):
+        states.append(
+            lax.dot_general(
+                pressed, value_ref[0, :, lanes], (((0,), (0,)), ((), ())), preferred_element_type=jnp.float32
+            )
+        )
+    for part, state_ref in enumerate(state_refs):
+
+        @pl.when(pl.program_id(0) == part)
+        def _(state_ref=state_ref):
+            for h, state in enumerate(states):
+                state_ref[h] = state.astype(state_ref.dtype)
+
+
+def closing_states(lin_key, lin_value, decay_rows, parts):
     heads = decay_rows.shape[1] // parts
-    wide = pl.BlockSpec((1, BLK, heads * HD), lambda i: (0, 0, part))
+    wide = pl.BlockSpec((1, BLK, heads * HD), lambda i: (0, 0, i))
     return pl.pallas_call(
         states_kernel,
-        grid=(1,),
-        in_specs=[wide, wide, pl.BlockSpec((1, heads, BLK), lambda i: (0, part, 0))],
-        out_specs=pl.BlockSpec((heads, HD, HD), lambda i: (0, 0, 0)),
-        out_shape=jax.ShapeDtypeStruct((heads, HD, HD), jnp.bfloat16),
+        grid=(parts,),
+        in_specs=[wide, wide, pl.BlockSpec((1, heads, BLK), lambda i: (0, i, 0))],
+        out_specs=[pl.BlockSpec((heads, HD, HD), lambda i: (0, 0, 0))] * parts,
+        out_shape=[jax.ShapeDtypeStruct((heads, HD, HD), jnp.bfloat16)] * parts,
         compiler_params=pltpu.CompilerParams(vmem_limit_bytes=16 * MIB),
         name="closing_states",
     )(lin_key, lin_value, decay_rows)
@@ -351,7 +360,7 @@
     handed_raw = passed_along(raw, "pp", 1)
     befores = [earlier_blocks(pair) for pair in pairs]
     lin_key, lin_value, raw = lax.optimization_barrier((lin_key, lin_value, raw))
-    closing = [closing_states(lin_key, lin_value, decay_rows, part, PARTS) for part in range(PARTS)]
+    closing = list(closing_states(lin_key, lin_value, decay_rows, PARTS))
     closing[0], *befores = lax.optimization_barrier((closing[0], *befores))
     ready = [
         softmax_group(place, soft_query, pair, before, g + 1)

time: 56.2 us -> 56.2 us (level)
  Pallas kernels: 23.1 us -> 22 us
  waiting for transfers between devices: 19 us -> 20.1 us
    pallas_call x2 -> x1, Pallas kernels: 5.11 us -> 3.97 us  [closing_states(): pl.pallas_call(states_kernel, grid=(parts,), in_specs=[wide, wide, pl.Blo...]
    ppermute x9, waiting for transfers between devices: 19 us -> 20.1 us  [passed_along(): lax.ppermute(block, axis, [((i - distance) % devices, i) for i in range(d...]
  transfers between devices with their start and end apart: 9 -> 9, of which waited for: 7 -> 6; matrix products, arithmetic and copies ran while one was open for 0% -> 0% of each run, Pallas kernels for 38% -> 36%
where the time goes in v3:
time: 56.2 us; the launch traced here: 56 us
  Pallas kernels  22 us (39%)
  waiting for transfers between devices  20.1 us (36%)
  starting transfers between devices  13.1 us (23%)
  between operations  0.71 us (1%)
    ppermute x9, waiting for transfers between devices, passed_along(): lax.ppermute(block, axis, [((i - distance) % devices, i) for i in range(d...  20.1 us
    ppermute x9, starting transfers between devices, passed_along(): lax.ppermute(block, axis, [((i - distance) % devices, i) for i in range(d...  13.1 us
    pallas_call x2, Pallas kernels, lightning(): pl.pallas_call(mix_kernel, grid_spec=pltpu.PrefetchScalarGridSpec(num_sca...  7.39 us
    pallas_call x1, Pallas kernels, closing_states(): pl.pallas_call(states_kernel, grid=(parts,), in_specs=[wide, wide, pl.Blo...  3.97 us
    pallas_call x1, Pallas kernels, softmax_finish(): pl.pallas_call(finish_kernel, grid_spec=pltpu.PrefetchScalarGridSpec(num_...  3.68 us
    pallas_call x1, Pallas kernels, softmax_group(): pl.pallas_call(soft_kernel, grid_spec=pltpu.PrefetchScalarGridSpec(num_sc...  3.64 us
    pallas_call x3, Pallas kernels, placed(): pl.pallas_call(functools.partial(place_kernel, start), in_specs=[anywhere...  2.22 us
  transfers between devices with their start and end apart: 9, of which 6 were waited for; matrix products, arithmetic and copies ran while one was open for 0% of the time, Pallas kernels for 36%

profile of v3, /device:TPU:0, one launch (start us, length us, event | category | flops | bytes accessed | tf_op | source)
XLA Modules:
  0.0 56.0 jit_solution(2888056694430333061)
XLA Ops:
  0.6 0.0 copy-start
  0.6 1.1 %packed.1 = (bf16[1,256,1280]{2,1,0:T(8,128)(2,1)S(1)}, bf16[1,256,256]{2,1,0:T(8,128)(2,1)S(1)}) custom-call(bf16[1,256,2048]{2,1,0:T(8,128)(2,1)} %query_ref.7, bf16[1,256,256]{2,1,0:T(8,128)(2,1)} %key_ref.1, bf16[1,256,256]{2,1,0:T(8,128)(2,1)} %value_ref.1), custom_call_target="tpu_custom_call" | custom-call | tf_op jit(solution)/shard_map/packed/pallas_call | solution.py:177
  1.8 3.1 %collective-permute-start.5 = (bf16[1,256,1280]{2,1,0:T(8,128)(2,1)S(1)}, bf16[1,256,1280]{2,1,0:T(8,128)(2,1)S(1)}, u32[]{:S(2)}, u32[]{:S(2)}) collective-permute-start(bf16[1,256,1280]{2,1,0:T(8,128)(2,1)S(1)} %get-tuple-element.14), channel_id=1, source_target_pairs={{3,0},{0,1},{1,2},{2,3},{7,4},{4,5},{5,6},{6,7},{11,8},{8,9},{9,10... | collective-permute-start | bytes 1966088 | tf_op jit(solution)/shard_map/ppermute | solution.py:25
  4.8 1.5 %collective-permute-start.3 = (bf16[1,256,256]{2,1,0:T(8,128)(2,1)S(1)}, bf16[1,256,256]{2,1,0:T(8,128)(2,1)S(1)}, u32[]{:S(2)}, u32[]{:S(2)}) collective-permute-start(bf16[1,256,256]{2,1,0:T(8,128)(2,1)S(1)} %get-tuple-element.21.key_ref.value_ref), channel_id=1, source_target_pairs={{16,0},{0,16},{17,1},{1,17},{18,2},{2,18},{19,3},{3,19},{20,4},{4,... | collective-permute-start | bytes 393224 | tf_op jit(solution)/shard_map/ppermute | solution.py:25
  6.3 0.0 copy-done
  6.3 4.0 %closing_states.1 = (bf16[8,128,128]{2,1,0:T(8,128)(2,1)S(1)}, bf16[8,128,128]{2,1,0:T(8,128)(2,1)S(1)}) custom-call(bf16[1,256,2048]{2,1,0:T(8,128)(2,1)} %key_ref.4, bf16[1,256,2048]{2,1,0:T(8,128)(2,1)} %value_ref.4, f32[1,16,256]{2,1,0:T(8,128)S(1)} %bitcast.2), custom_call_target="tpu_custom_call" | custom-call | tf_op jit(solution)/shard_map/closing_states/pallas_call | solution.py:66
  10.3 0.0 collective-permute-done.3.before_ref
  10.3 1.0 %collective-permute-start.4 = (bf16[8,128,128]{2,1,0:T(8,128)(2,1)S(1)}, bf16[8,128,128]{2,1,0:T(8,128)(2,1)S(1)}, u32[]{:S(2)}, u32[]{:S(2)}) collective-permute-start(bf16[8,128,128]{2,1,0:T(8,128)(2,1)S(1)} %get-tuple-element.22), channel_id=1, source_target_pairs={{16,0},{0,16},{17,1},{1,17},{18,2},{2,18},{19,3},{3,19},{20,4},{4,... | collective-permute-start | bytes 786440 | tf_op jit(solution)/shard_map/ppermute | solution.py:25
  11.3 1.1 %collective-permute-start = (bf16[8,128,128]{2,1,0:T(8,128)(2,1)S(1)}, bf16[8,128,128]{2,1,0:T(8,128)(2,1)S(1)}, u32[]{:S(2)}, u32[]{:S(2)}) collective-permute-start(bf16[8,128,128]{2,1,0:T(8,128)(2,1)S(1)} %get-tuple-element.17), channel_id=1, source_target_pairs={{16,0},{0,16},{17,1},{1,17},{18,2},{2,18},{19,3},{3,19},{20,4},{4,... | collective-permute-start | bytes 786440 | tf_op jit(solution)/shard_map/ppermute | solution.py:25
  12.4 0.0 copy-start.1
  12.4 3.6 %softmax_group.1 = bf16[1,256,1024]{2,1,0:T(8,128)(2,1)S(1)} custom-call(s32[1]{0:T(128)} %bitcast.place_ref, bf16[1,256,2048]{2,1,0:T(8,128)(2,1)} %query_ref.7, bf16[1,256,256]{2,1,0:T(8,128)(2,1)S(1)} %get-tuple-element.21.key_ref.value_ref, bf16[1,256,256]{2,1,0:T(8,128)(2,1)S(1)} %get-tuple-element.21.key_ref.value_ref, ...), custom_call_target="tpu_custom_call" | custom-call | tf_op jit(solution)/shard_map/softmax_group/pallas_call | solution.py:250
  16.1 1.6 %collective-permute-start.8 = (bf16[1,256,1024]{2,1,0:T(8,128)(2,1)S(1)}, bf16[1,256,1024]{2,1,0:T(8,128)(2,1)S(1)}, u32[]{:S(2)}, u32[]{:S(2)}) collective-permute-start(bf16[1,256,1024]{2,1,0:T(8,128)(2,1)S(1)} %softmax_group.1), channel_id=1, source_target_pairs={{3,0},{0,1},{1,2},{2,3},{7,4},{4,5},{5,6},{6,7},{11,8},{8,9},{9,10... | collective-permute-start | bytes 1572872 | tf_op jit(solution)/shard_map/ppermute | solution.py:25
  17.7 1.9 %collective-permute-done.4.state_ref = bf16[8,128,128]{2,1,0:T(8,128)(2,1)S(1)} collective-permute-done((bf16[8,128,128]{2,1,0:T(8,128)(2,1)S(1)}, bf16[8,128,128]{2,1,0:T(8,128)(2,1)S(1)}, u32[]{:S(2)}, u32[]{:S(2)}) %collective-permute-start.4) | collective-permute-done | bytes 262176 | tf_op jit(solution)/shard_map/ppermute | solution.py:25
  19.6 2.8 %collective-permute-done.5.query_ref.key_ref.value_ref = bf16[1,256,1280]{2,1,0:T(8,128)(2,1)S(1)} collective-permute-done((bf16[1,256,1280]{2,1,0:T(8,128)(2,1)S(1)}, bf16[1,256,1280]{2,1,0:T(8,128)(2,1)S(1)}, u32[]{:S(2)}, u32[]{:S(2)}) %collective-permute-start.5) | collective-permute-done | bytes 655392 | tf_op jit(solution)/shard_map/ppermute | solution.py:25
  22.4 0.0 copy-done.1
  22.4 3.7 %lightning_mix.3 = bf16[1,256,1024]{2,1,0:T(8,128)(2,1)S(1)} custom-call(s32[1]{0:T(128)} %bitcast.place_ref, bf16[1,256,2048]{2,1,0:T(8,128)(2,1)} %query_ref.6, bf16[1,256,2048]{2,1,0:T(8,128)(2,1)} %key_ref.4, bf16[1,256,2048]{2,1,0:T(8,128)(2,1)} %value_ref.4, f32[1,16,256]{2,1,0:T(8,128)S(1)} %bitcast.3, bf16[1,256,2048]{2,1,0:T(8,128)(2,1)} %gate_ref.3, ...), custom_call_target="tpu_custom_call" | custom-call | tf_op jit(solution)/shard_map/lightning_mix/pallas_call | solution.py:130
  26.1 0.1 collective-permute-start.6
  26.2 0.0 collective-permute-done.state_ref
  26.2 3.7 %lightning_mix.2 = (bf16[1,256,768]{2,1,0:T(8,128)(2,1)S(1)}, bf16[1,256,256]{2,1,0:T(8,128)(2,1)S(1)}) custom-call(s32[1]{0:T(128)} %bitcast.place_ref, bf16[1,256,2048]{2,1,0:T(8,128)(2,1)} %query_ref.6, bf16[1,256,2048]{2,1,0:T(8,128)(2,1)} %key_ref.4, bf16[1,256,2048]{2,1,0:T(8,128)(2,1)} %value_ref.4, f32[1,16,256]{2,1,0:T(8,128)S(1)} %bitcast.4, ...), custom_call_target="tpu_custom_call" | custom-call | tf_op jit(solution)/shard_map/lightning_mix/pallas_call | solution.py:130
  29.9 1.6 %collective-permute-start.2 = (bf16[1,256,768]{2,1,0:T(8,128)(2,1)S(1)}, bf16[1,256,768]{2,1,0:T(8,128)(2,1)S(1)}, u32[]{:S(2)}, u32[]{:S(2)}) collective-permute-start(bf16[1,256,768]{2,1,0:T(8,128)(2,1)S(1)} %get-tuple-element.19), channel_id=1, source_target_pairs={{3,0},{0,1},{1,2},{2,3},{7,4},{4,5},{5,6},{6,7},{11,8},{8,9},{9,10... | collective-permute-start | bytes 1179656 | tf_op jit(solution)/shard_map/ppermute | solution.py:25
  31.6 1.6 %collective-permute-start.7 = (bf16[1,256,256]{2,1,0:T(8,128)(2,1)S(1)}, bf16[1,256,256]{2,1,0:T(8,128)(2,1)S(1)}, u32[]{:S(2)}, u32[]{:S(2)}) collective-permute-start(bf16[1,256,256]{2,1,0:T(8,128)(2,1)S(1)} %slice.3), channel_id=1, source_target_pairs={{16,0},{0,16},{17,1},{1,17},{18,2},{2,18},{19,3},{3,19},{20,4},{4,... | collective-permute-start | bytes 393224 | tf_op jit(solution)/shard_map/ppermute | solution.py:25
  33.1 1.6 %collective-permute-start.1 = (bf16[1,256,256]{2,1,0:T(8,128)(2,1)S(1)}, bf16[1,256,256]{2,1,0:T(8,128)(2,1)S(1)}, u32[]{:S(2)}, u32[]{:S(2)}) collective-permute-start(bf16[1,256,256]{2,1,0:T(8,128)(2,1)S(1)} %get-tuple-element.18), channel_id=1, source_target_pairs={{3,0},{0,1},{1,2},{2,3},{7,4},{4,5},{5,6},{6,7},{11,8},{8,9},{9,10... | collective-permute-start | bytes 393224 | tf_op jit(solution)/shard_map/ppermute | solution.py:25
  34.7 0.0 collective-permute-done.8.ready_ref
  34.7 1.9 %collective-permute-done.7.before_ref = bf16[1,256,256]{2,1,0:T(8,128)(2,1)S(1)} collective-permute-done((bf16[1,256,256]{2,1,0:T(8,128)(2,1)S(1)}, bf16[1,256,256]{2,1,0:T(8,128)(2,1)S(1)}, u32[]{:S(2)}, u32[]{:S(2)}) %collective-permute-start.7) | collective-permute-done | bytes 131104 | tf_op jit(solution)/shard_map/ppermute | solution.py:25
  36.6 3.7 %softmax_finish.1 = bf16[1,256,2048]{2,1,0:T(8,128)(2,1)} custom-call(s32[1]{0:T(128)} %bitcast.place_ref, bf16[1,256,1280]{2,1,0:T(8,128)(2,1)S(1)} %collective-permute-done.5.query_ref.key_ref.value_ref, bf16[1,256,1280]{2,1,0:T(8,128)(2,1)S(1)} %collective-permute-done.5.query_ref.key_ref.value_ref, ...), custom_call_target="tpu_custom_call" | custom-call | tf_op jit(solution)/shard_map/softmax_finish/pallas_call | solution.py:286
  40.3 4.6 %collective-permute-done.6.block_ref = bf16[1,256,1024]{2,1,0:T(8,128)(2,1)S(1)} collective-permute-done((bf16[1,256,1024]{2,1,0:T(8,128)(2,1)S(1)}, bf16[1,256,1024]{2,1,0:T(8,128)(2,1)S(1)}, u32[]{:S(2)}, u32[]{:S(2)}) %collective-permute-start.6) | collective-permute-done | bytes 524320 | tf_op jit(solution)/shard_map/ppermute | solution.py:25
  44.9 0.8 %placed.3.refs_0_ = bf16[1,256,2048]{2,1,0:T(8,128)(2,1)} custom-call(bf16[1,256,1024]{2,1,0:T(8,128)(2,1)S(1)} %collective-permute-done.6.block_ref), custom_call_target="tpu_custom_call" | custom-call | tf_op jit(solution)/shard_map/placed/pallas_call | solution.py:314
  45.7 7.6 %collective-permute-done.2.block_ref = bf16[1,256,768]{2,1,0:T(8,128)(2,1)S(1)} collective-permute-done((bf16[1,256,768]{2,1,0:T(8,128)(2,1)S(1)}, bf16[1,256,768]{2,1,0:T(8,128)(2,1)S(1)}, u32[]{:S(2)}, u32[]{:S(2)}) %collective-permute-start.2) | collective-permute-done | bytes 393248 | tf_op jit(solution)/shard_map/ppermute | solution.py:25
  53.3 0.8 %placed.4.refs_0_ = bf16[1,256,2048]{2,1,0:T(8,128)(2,1)} custom-call(bf16[1,256,768]{2,1,0:T(8,128)(2,1)S(1)} %collective-permute-done.2.block_ref, bf16[1,256,2048]{2,1,0:T(8,128)(2,1)} %placed.3.refs_0_), custom_call_target="tpu_custom_call", output_to_operand_aliasing={{}: (1, {})} | custom-call | tf_op jit(solution)/shard_map/placed/pallas_call | solution.py:314
  54.1 1.2 %collective-permute-done.1.block_ref = bf16[1,256,256]{2,1,0:T(8,128)(2,1)S(1)} collective-permute-done((bf16[1,256,256]{2,1,0:T(8,128)(2,1)S(1)}, bf16[1,256,256]{2,1,0:T(8,128)(2,1)S(1)}, u32[]{:S(2)}, u32[]{:S(2)}) %collective-permute-start.1) | collective-permute-done | bytes 131104 | tf_op jit(solution)/shard_map/ppermute | solution.py:25
  55.3 0.7 %placed.5 = bf16[1,256,2048]{2,1,0:T(8,128)(2,1)} custom-call(bf16[1,256,256]{2,1,0:T(8,128)(2,1)S(1)} %collective-permute-done.1.block_ref, bf16[1,256,2048]{2,1,0:T(8,128)(2,1)} %placed.4.refs_0_), custom_call_target="tpu_custom_call", output_to_operand_aliasing={{}: (1, {})} | custom-call | tf_op jit(solution)/shard_map/placed/pallas_call | solution.py:314
  (1 shorter events, 0.0 us)
Async XLA Ops:
  0.6 5.7 %copy-start = (f32[1,256,16]{1,2,0:T(8,128)S(1)}, f32[1,256,16]{1,2,0:T(8,128)}, u32[]{:S(2)}) copy-start(f32[1,256,16]{1,2,0:T(8,128)} %param.12) | copy-start | bytes 49156
  1.8 20.7 %collective-permute-start.5 = (bf16[1,256,1280]{2,1,0:T(8,128)(2,1)S(1)}, bf16[1,256,1280]{2,1,0:T(8,128)(2,1)S(1)}, u32[]{:S(2)}, u32[]{:S(2)}) collective-permute-start(bf16[1,256,1280]{2,1,0:T(8,128)(2,1)S(1)} %get-tuple-element.14), channel_id=1, source_target_pairs={{3,0},{0,1},{1,2},{2,3},{7,4},{4,5},{5,6},{6,7},{11,8},{8,9},{9,10... | collective-permute-start | bytes 1966088 | tf_op jit(solution)/shard_map/ppermute | solution.py:25
  4.8 5.5 %collective-permute-start.3 = (bf16[1,256,256]{2,1,0:T(8,128)(2,1)S(1)}, bf16[1,256,256]{2,1,0:T(8,128)(2,1)S(1)}, u32[]{:S(2)}, u32[]{:S(2)}) collective-permute-start(bf16[1,256,256]{2,1,0:T(8,128)(2,1)S(1)} %get-tuple-element.21.key_ref.value_ref), channel_id=1, source_target_pairs={{16,0},{0,16},{17,1},{1,17},{18,2},{2,18},{19,3},{3,19},{20,4},{4,... | collective-permute-start | bytes 393224 | tf_op jit(solution)/shard_map/ppermute | solution.py:25
  10.3 9.3 %collective-permute-start.4 = (bf16[8,128,128]{2,1,0:T(8,128)(2,1)S(1)}, bf16[8,128,128]{2,1,0:T(8,128)(2,1)S(1)}, u32[]{:S(2)}, u32[]{:S(2)}) collective-permute-start(bf16[8,128,128]{2,1,0:T(8,128)(2,1)S(1)} %get-tuple-element.22), channel_id=1, source_target_pairs={{16,0},{0,16},{17,1},{1,17},{18,2},{2,18},{19,3},{3,19},{20,4},{4,... | collective-permute-start | bytes 786440 | tf_op jit(solution)/shard_map/ppermute | solution.py:25
  11.3 14.9 %collective-permute-start = (bf16[8,128,128]{2,1,0:T(8,128)(2,1)S(1)}, bf16[8,128,128]{2,1,0:T(8,128)(2,1)S(1)}, u32[]{:S(2)}, u32[]{:S(2)}) collective-permute-start(bf16[8,128,128]{2,1,0:T(8,128)(2,1)S(1)} %get-tuple-element.17), channel_id=1, source_target_pairs={{16,0},{0,16},{17,1},{1,17},{18,2},{2,18},{19,3},{3,19},{20,4},{4,... | collective-permute-start | bytes 786440 | tf_op jit(solution)/shard_map/ppermute | solution.py:25
  12.4 10.0 %copy-start.1 = (f32[1,2048]{1,0:T(1,128)S(1)}, f32[1,2048]{1,0:T(1,128)}, u32[]{:S(2)}) copy-start(f32[1,2048]{1,0:T(1,128)} %gain_ref.3) | copy-start | bytes 24580
  16.1 18.6 %collective-permute-start.8 = (bf16[1,256,1024]{2,1,0:T(8,128)(2,1)S(1)}, bf16[1,256,1024]{2,1,0:T(8,128)(2,1)S(1)}, u32[]{:S(2)}, u32[]{:S(2)}) collective-permute-start(bf16[1,256,1024]{2,1,0:T(8,128)(2,1)S(1)} %softmax_group.1), channel_id=1, source_target_pairs={{3,0},{0,1},{1,2},{2,3},{7,4},{4,5},{5,6},{6,7},{11,8},{8,9},{9,10... | collective-permute-start | bytes 1572872 | tf_op jit(solution)/shard_map/ppermute | solution.py:25
  26.1 18.8 %collective-permute-start.6 = (bf16[1,256,1024]{2,1,0:T(8,128)(2,1)S(1)}, bf16[1,256,1024]{2,1,0:T(8,128)(2,1)S(1)}, u32[]{:S(2)}, u32[]{:S(2)}) collective-permute-start(bf16[1,256,1024]{2,1,0:T(8,128)(2,1)S(1)} %lightning_mix.3), channel_id=1, source_target_pairs={{3,0},{0,1},{1,2},{2,3},{7,4},{4,5},{5,6},{6,7},{11,8},{8,9},{9,10... | collective-permute-start | bytes 1572872 | tf_op jit(solution)/shard_map/ppermute | solution.py:25
  29.9 23.4 %collective-permute-start.2 = (bf16[1,256,768]{2,1,0:T(8,128)(2,1)S(1)}, bf16[1,256,768]{2,1,0:T(8,128)(2,1)S(1)}, u32[]{:S(2)}, u32[]{:S(2)}) collective-permute-start(bf16[1,256,768]{2,1,0:T(8,128)(2,1)S(1)} %get-tuple-element.19), channel_id=1, source_target_pairs={{3,0},{0,1},{1,2},{2,3},{7,4},{4,5},{5,6},{6,7},{11,8},{8,9},{9,10... | collective-permute-start | bytes 1179656 | tf_op jit(solution)/shard_map/ppermute | solution.py:25
  31.6 5.0 %collective-permute-start.7 = (bf16[1,256,256]{2,1,0:T(8,128)(2,1)S(1)}, bf16[1,256,256]{2,1,0:T(8,128)(2,1)S(1)}, u32[]{:S(2)}, u32[]{:S(2)}) collective-permute-start(bf16[1,256,256]{2,1,0:T(8,128)(2,1)S(1)} %slice.3), channel_id=1, source_target_pairs={{16,0},{0,16},{17,1},{1,17},{18,2},{2,18},{19,3},{3,19},{20,4},{4,... | collective-permute-start | bytes 393224 | tf_op jit(solution)/shard_map/ppermute | solution.py:25
  33.1 22.2 %collective-permute-start.1 = (bf16[1,256,256]{2,1,0:T(8,128)(2,1)S(1)}, bf16[1,256,256]{2,1,0:T(8,128)(2,1)S(1)}, u32[]{:S(2)}, u32[]{:S(2)}) collective-permute-start(bf16[1,256,256]{2,1,0:T(8,128)(2,1)S(1)} %get-tuple-element.18), channel_id=1, source_target_pairs={{3,0},{0,1},{1,2},{2,3},{7,4},{4,5},{5,6},{6,7},{11,8},{8,9},{9,10... | collective-permute-start | bytes 393224 | tf_op jit(solution)/shard_map/ppermute | solution.py:25

commit v4 on v3

--- a/solution.py
+++ b/solution.py
@@ -185,12 +185,11 @@
     )(soft_query, soft_key, soft_value)
 
 
-def attend(place, query_ref, key_ref, value_ref, before_ref, out_ref):
-    others = before_ref.shape[0]
+def attend(place, query_ref, key_ref, value_ref, before_key_ref, before_value_ref, out_ref):
+    others = before_key_ref.shape[0]
     factor = HD ** (-0.5) * LOG2E
     causal = lax.broadcasted_iota(jnp.int32, (BLK, BLK), 0) >= lax.broadcasted_iota(jnp.int32, (BLK, BLK), 1)
     turned_dims = (((1,), (1,)), ((), ()))
-    keys, values = slice(0, HD), slice(HD, 2 * HD)
 
     def scored(queries, keys):
         return lax.dot_general(queries, keys, turned_dims, preferred_element_type=jnp.float32)
@@ -201,7 +200,7 @@
         own = jnp.where(causal, scored(queries, key_ref[0]), lowest)
         peak = jnp.max(own, axis=1, keepdims=True)
         if others == 1:
-            before = jnp.where(place > 0, scored(queries, before_ref[0, :, keys]), lowest)
+            before = jnp.where(place > 0, scored(queries, before_key_ref[0]), lowest)
             peak = jnp.maximum(peak, jnp.max(before, axis=1, keepdims=True))
             own = jnp.exp2((own - peak) * factor)
             before = jnp.exp2((before - peak) * factor)
@@ -209,7 +208,7 @@
             weighted = jnp.dot(
                 own.astype(jnp.bfloat16), value_ref[0], preferred_element_type=jnp.float32
             ) + jnp.dot(
-                before.astype(jnp.bfloat16), before_ref[0, :, values], preferred_element_type=jnp.float32
+                before.astype(jnp.bfloat16), before_value_ref[0], preferred_element_type=jnp.float32
             )
         else:
             own = jnp.exp2((own - peak) * factor)
@@ -220,14 +219,14 @@
 
             def absorb(turn, kept):
                 peak, totals, weighted = kept
-                scores = scored(queries, before_ref[turn, :, keys])
+                scores = scored(queries, before_key_ref[turn])
                 new_peak = jnp.maximum(peak, jnp.max(scores, axis=1, keepdims=True))
                 shrink = jnp.exp2((peak - new_peak) * factor)
                 scores = jnp.exp2((scores - new_peak) * factor)
                 totals = totals * shrink + jnp.sum(scores, axis=1, keepdims=True)
                 weighted = weighted * shrink + jnp.dot(
                     scores.astype(jnp.bfloat16),
-                    before_ref[turn, :, values],
+                    before_value_ref[turn],
                     preferred_element_type=jnp.float32,
                 )
                 return (new_peak, totals, weighted)
@@ -236,42 +235,71 @@
         out_ref[0, :, lanes] = (weighted / totals).astype(out_ref.dtype)
 
 
-def soft_kernel(place_ref, query_ref, key_ref, value_ref, before_ref, out_ref):
-    attend(place_ref[0], query_ref, key_ref, value_ref, before_ref, out_ref)
-
-
-STEP = 8
-
-
-def softmax_group(place, soft_query, pair, before, group):
-    others = before.shape[0]
-    steps = GROUP // STEP
-    wide = (1, BLK, STEP * HD)
+def soft_kernel(place_ref, query_ref, key_ref, value_ref, before_key_ref, before_value_ref, out_ref):
+    attend(place_ref[0], query_ref, key_ref, value_ref, before_key_ref, before_value_ref, out_ref)
+
+
+def lanes_at(rows, width, index):
+    return pl.BlockSpec((rows, BLK, width), lambda i, place: (0, 0, index))
+
+
+def softmax_heads(place, soft_query, first, count, key, value, before_key, before_value):
+    others = before_key[0].shape[0]
     return pl.pallas_call(
         soft_kernel,
         grid_spec=pltpu.PrefetchScalarGridSpec(
             num_scalar_prefetch=1,
-            grid=(steps,),
+            grid=(1,),
             in_specs=[
-                pl.BlockSpec(wide, lambda i, place: (0, 0, group * steps + i)),
-                pl.BlockSpec((1, BLK, HD), lambda i, place: (0, 0, 0)),
-                pl.BlockSpec((1, BLK, HD), lambda i, place: (0, 0, 1)),
-                pl.BlockSpec((others, BLK, 2 * HD), lambda i, place: (0, 0, 0)),
+                lanes_at(1, count * HD, first // count),
+                lanes_at(1, HD, key[1]),
+                lanes_at(1, HD, value[1]),
+                lanes_at(others, HD, before_key[1]),
+                lanes_at(others, HD, before_value[1]),
             ],
-            out_specs=pl.BlockSpec(wide, lambda i, place: (0, 0, i)),
+            out_specs=lanes_at(1, count * HD, 0),
         ),
-        out_shape=jax.ShapeDtypeStruct((1, BLK, GROUP * HD), jnp.bfloat16),
+        out_shape=jax.ShapeDtypeStruct((1, BLK, count * HD), jnp.bfloat16),
         compiler_params=pltpu.CompilerParams(vmem_limit_bytes=20 * MIB),
-        name="softmax_group",
-    )(place, soft_query, pair, pair, before)
-
-
-def finish_kernel(place_ref, query_ref, key_ref, value_ref, before_ref, ready_ref, out_ref):
-    here = pl.program_id(0) < GROUP // STEP
+        name="softmax_heads",
+    )(place, soft_query, key[0], value[0], before_key[0], before_value[0])
+
+
+def softmax_all(place, query, key, value, before_key, before_value):
+    groups = key.shape[2] // HD
+    others = before_key.shape[0]
+
+    def by_group(rows, width):
+        return pl.BlockSpec((rows, BLK, width), lambda i, place: (0, 0, i))
+
+    return pl.pallas_call(
+        soft_kernel,
+        grid_spec=pltpu.PrefetchScalarGridSpec(
+            num_scalar_prefetch=1,
+            grid=(groups,),
+            in_specs=[
+                by_group(1, GROUP * HD),
+                by_group(1, HD),
+                by_group(1, HD),
+                by_group(others, HD),
+                by_group(others, HD),
+            ],
+            out_specs=by_group(1, GROUP * HD),
+        ),
+        out_shape=pltpu.HBM(query.shape, jnp.bfloat16),
+        compiler_params=pltpu.CompilerParams(vmem_limit_bytes=20 * MIB),
+        name="softmax_all",
+    )(place, query, key, value, before_key, before_value)
+
+
+def finish_kernel(
+    place_ref, query_ref, key_ref, value_ref, before_key_ref, before_value_ref, ready_ref, out_ref
+):
+    here = pl.program_id(0) == 0
 
     @pl.when(here)
     def _():
-        attend(place_ref[0], query_ref, key_ref, value_ref, before_ref, out_ref)
+        attend(place_ref[0], query_ref, key_ref, value_ref, before_key_ref, before_value_ref, out_ref)
 
     @pl.when(jnp.logical_not(here))
     def _():
@@ -280,27 +308,27 @@
 
 def softmax_finish(place, raw, before, ready):
     others = before.shape[0]
-    steps = GROUP // STEP
-    wide = (1, BLK, STEP * HD)
-    groups = 1 + ready.shape[2] // (GROUP * HD)
+    width = GROUP * HD
+    groups = 1 + ready.shape[2] // width
     return pl.pallas_call(
         finish_kernel,
         grid_spec=pltpu.PrefetchScalarGridSpec(
             num_scalar_prefetch=1,
-            grid=(groups * steps,),
+            grid=(groups,),
             in_specs=[
-                pl.BlockSpec(wide, lambda i, place: (0, 0, jnp.minimum(i, steps - 1))),
-                pl.BlockSpec((1, BLK, HD), lambda i, place: (0, 0, GROUP)),
-                pl.BlockSpec((1, BLK, HD), lambda i, place: (0, 0, GROUP + 1)),
-                pl.BlockSpec((others, BLK, 2 * HD), lambda i, place: (0, 0, 0)),
-                pl.BlockSpec(wide, lambda i, place: (0, 0, jnp.maximum(i - steps, 0))),
+                lanes_at(1, width, 0),
+                lanes_at(1, HD, GROUP),
+                lanes_at(1, HD, GROUP + 1),
+                lanes_at(others, HD, 0),
+                lanes_at(others, HD, 1),
+                pl.BlockSpec((1, BLK, width), lambda i, place: (0, 0, jnp.maximum(i - 1, 0))),
             ],
-            out_specs=pl.BlockSpec(wide, lambda i, place: (0, 0, i)),
+            out_specs=pl.BlockSpec((1, BLK, width), lambda i, place: (0, 0, i)),
         ),
-        out_shape=jax.ShapeDtypeStruct((1, BLK, groups * GROUP * HD), jnp.bfloat16),
+        out_shape=pltpu.HBM((1, BLK, groups * width), jnp.bfloat16),
         compiler_params=pltpu.CompilerParams(vmem_limit_bytes=20 * MIB),
         name="softmax_finish",
-    )(place, raw, raw, raw, before, ready)
+    )(place, raw, raw, raw, before, before, ready)
 
 
 def place_kernel(start, block_ref, *refs):
@@ -310,12 +338,13 @@
 
 def placed(block, start, width, whole=None):
     anywhere = pl.BlockSpec(memory_space=pl.ANY)
+    in_hbm = pl.BlockSpec(memory_space=pltpu.HBM)
     operands = (block,) if whole is None else (block, whole)
     return pl.pallas_call(
         functools.partial(place_kernel, start),
-        in_specs=[anywhere] * len(operands),
-        out_specs=anywhere,
-        out_shape=jax.ShapeDtypeStruct(block.shape[:2] + (width,), block.dtype),
+        in_specs=[anywhere] + [in_hbm] * (len(operands) - 1),
+        out_specs=in_hbm,
+        out_shape=pltpu.HBM(block.shape[:2] + (width,), block.dtype),
         scratch_shapes=[pltpu.SemaphoreType.DMA((1,))],
         input_output_aliases={} if whole is None else {1: 0},
         compiler_params=pltpu.CompilerParams(vmem_limit_bytes=1 * MIB),
@@ -330,11 +359,11 @@
     return lax.all_gather(block, "ctx", axis=0, tiled=True)[: devices - 1]
 
 
-def incoming_states(closing, decay_rows):
+def incoming_states(closing, device_log):
     if lax.axis_size("ctx") == 2:
         return passed_along(closing, "ctx", 1)
     states = lax.all_gather(closing[None], "ctx", axis=0, tiled=True)
-    logs = lax.all_gather(jnp.sum(decay_rows, axis=2), "ctx", axis=0, tiled=True)
+    logs = lax.all_gather(device_log, "ctx", axis=0, tiled=True)
     earlier = (lax.iota(jnp.int32, logs.shape[0]) < lax.axis_index("ctx"))[:, None]
     reached = jnp.sum(jnp.where(earlier, logs, 0.0), axis=0)
     rising = jnp.cumsum(logs, axis=0)
@@ -346,16 +375,37 @@
 LAST = 2
 
 
-def local(
-    lin_query, lin_key, lin_value, log_decay, out_gate, norm_gain, soft_query, soft_key, soft_value
+def joined(chunks, width):
+    whole = None
+    start = 0
+    for chunk in chunks:
+        whole = placed(chunk, start, width, whole)
+        start += chunk.shape[2]
+    return whole
+
+
+def lightning_chunks(place, arrays, incoming):
+    heads = incoming[0].shape[0]
+    chunks = []
+    for part in range(PARTS):
+        sizes = [heads - LAST, LAST] if part == PARTS - 1 else [heads]
+        chunks += lightning(place, *arrays, incoming[part], part, PARTS, sizes)
+    return [passed_along(chunk, "pp", 1) for chunk in chunks]
+
+
+def ahead(
+    device_logs,
+    lin_query,
+    lin_key,
+    lin_value,
+    decay_rows,
+    out_gate,
+    norm_gain,
+    soft_query,
+    soft_key,
+    soft_value,
+    place,
 ):
-    place = lax.axis_index("ctx").astype(jnp.int32)[None]
-    lin_query, lin_key, lin_value, out_gate, soft_query, soft_key, soft_value = (
-        pltpu.with_memory_space_constraint(x, pltpu.HBM)
-        for x in (lin_query, lin_key, lin_value, out_gate, soft_query, soft_key, soft_value)
-    )
-    decay_rows = jnp.swapaxes(log_decay, 1, 2)
-    heads = decay_rows.shape[1] // PARTS
     raw, *pairs = packed(soft_query, soft_key, soft_value)
     handed_raw = passed_along(raw, "pp", 1)
     befores = [earlier_blocks(pair) for pair in pairs]
@@ -363,40 +413,114 @@
     closing = list(closing_states(lin_key, lin_value, decay_rows, PARTS))
     closing[0], *befores = lax.optimization_barrier((closing[0], *befores))
     ready = [
-        softmax_group(place, soft_query, pair, before, g + 1)
+        softmax_heads(
+            place, soft_query, (g + 1) * GROUP, GROUP, (pair, 0), (pair, 1), (before, 0), (before, 1)
+        )
         for g, (pair, before) in enumerate(zip(pairs, befores))
     ]
-    incoming = [
-        incoming_states(closing[part], decay_rows[:, part * heads : (part + 1) * heads])
-        for part in range(PARTS)
-    ]
+    incoming = [incoming_states(closing[part], device_logs[part]) for part in range(PARTS)]
     ready = [passed_along(group, "pp", 1) for group in ready]
     ready = ready[0] if len(ready) == 1 else jnp.concatenate(ready, axis=2)
     incoming[0], handed_raw = lax.optimization_barrier((incoming[0], handed_raw))
-    chunks = []
-    for part in range(PARTS):
-        chunks += lightning(
-            place,
-            lin_query,
-            lin_key,
-            lin_value,
-            decay_rows,
-            out_gate,
-            norm_gain,
-            incoming[part],
-            part,
-            PARTS,
-            [heads - LAST, LAST] if part == PARTS - 1 else [heads],
-        )
-    chunks = [passed_along(chunk, "pp", 1) for chunk in chunks]
+    arrays = (lin_query, lin_key, lin_value, decay_rows, out_gate, norm_gain)
+    chunks = lightning_chunks(place, arrays, incoming)
     before = earlier_blocks(handed_raw[:, :, GROUP * HD :])
     soft_handed = softmax_finish(place, handed_raw, before, ready)
-    lin_handed = None
-    start = 0
-    for chunk in chunks:
-        lin_handed = placed(chunk, start, lin_query.shape[2], lin_handed)
-        start += chunk.shape[2]
-    return (lin_handed, soft_handed)
+    return (joined(chunks, lin_query.shape[2]), soft_handed)
+
+
+def raw_first(
+    device_logs,
+    lin_query,
+    lin_key,
+    lin_value,
+    decay_rows,
+    out_gate,
+    norm_gain,
+    soft_query,
+    soft_key,
+    soft_value,
+    place,
+):
+    handed_key = passed_along(soft_key, "pp", 1)
+    handed_value = passed_along(soft_value, "pp", 1)
+    handed_query = passed_along(soft_query, "pp", 1)
+    closing = closing_states(lin_key, lin_value, decay_rows, PARTS)
+    incoming = [incoming_states(closing[part], device_logs[part]) for part in range(PARTS)]
+    incoming[-1], handed_query, handed_key, handed_value = lax.optimization_barrier(
+        (incoming[-1], handed_query, handed_key, handed_value)
+    )
+    befores = (earlier_blocks(handed_key), earlier_blocks(handed_value))
+    arrays = (lin_query, lin_key, lin_value, decay_rows, out_gate, norm_gain)
+    chunks = lightning_chunks(place, arrays, incoming)
+    soft_handed = softmax_all(place, handed_query, handed_key, handed_value, *befores)
+    return (joined(chunks, lin_query.shape[2]), soft_handed)
+
+
+def worked_out_first(
+    device_logs,
+    lin_query,
+    lin_key,
+    lin_value,
+    decay_rows,
+    out_gate,
+    norm_gain,
+    soft_query,
+    soft_key,
+    soft_value,
+    place,
+):
+    kv_count = soft_key.shape[2] // HD
+    befores = (earlier_blocks(soft_key), earlier_blocks(soft_value))
+    closing = list(closing_states(lin_key, lin_value, decay_rows, PARTS))
+    closing[0], *befores = lax.optimization_barrier((closing[0], *befores))
+    incoming = [incoming_states(closing[part], device_logs[part]) for part in range(PARTS)]
+    groups = []
+    for g in range(kv_count):
+        if groups:
+            soft_query, groups[-1] = lax.optimization_barrier((soft_query, groups[-1]))
+        groups.append(
+            softmax_heads(
+                place,
+                soft_query,
+                g * GROUP,
+                GROUP,
+                (soft_key, g),
+                (soft_value, g),
+                (befores[0], g),
+                (befores[1], g),
+            )
+        )
+    groups = [passed_along(group, "pp", 1) for group in groups]
+    for part in range(min(PARTS, kv_count)):
+        incoming[part], groups[part] = lax.optimization_barrier((incoming[part], groups[part]))
+    arrays = (lin_query, lin_key, lin_value, decay_rows, out_gate, norm_gain)
+    chunks = lightning_chunks(place, arrays, incoming)
+    soft_handed = joined(groups, soft_query.shape[2])
+    return (joined(chunks, lin_query.shape[2]), soft_handed)
+
+
+def local(
+    lin_query, lin_key, lin_value, log_decay, out_gate, norm_gain, soft_query, soft_key, soft_value
+):
+    arrays = (
+        lin_query,
+        lin_key,
+        lin_value,
+        jnp.swapaxes(log_decay, 1, 2),
+        out_gate,
+        norm_gain,
+        soft_query,
+        soft_key,
+        soft_value,
+    )
+    arrays = tuple(pltpu.with_memory_space_constraint(x, pltpu.HBM) for x in arrays)
+    place = lax.axis_index("ctx").astype(jnp.int32)[None]
+    if lax.axis_size("ctx") > 2:
+        return ahead(jnp.split(jnp.sum(log_decay, axis=1), PARTS, axis=1), *arrays, place)
+    turn = lax.axis_index("tp") & 1
+    unused = [None] * PARTS
+    return lax.cond(turn == 0, functools.partial(raw_first, unused), functools.partial(worked_out_first, unused), *arrays, place)
 
 
 def solution(mesh):

time: 56.2 us -> 55.9 us (level)
  the two profiles are of different devices: /device:TPU:0 before, /device:TPU:1 now
where the time goes in v4:
time: 55.9 us; the launch traced here: 55.7 us
  waiting for transfers between devices  23.6 us (42%)
  Pallas kernels  22.6 us (40%)
  starting transfers between devices  7.6 us (14%)
  between operations  0.82 us (1%)
  local copies, waits for them, and re-layouts  0.67 us (1%)
    ppermute x9, waiting for transfers between devices, passed_along(): lax.ppermute(block, axis, [((i - distance) % devices, i) for i in range(d...  23.6 us
    ppermute x9, starting transfers between devices, passed_along(): lax.ppermute(block, axis, [((i - distance) % devices, i) for i in range(d...  7.6 us
    pallas_call x2, Pallas kernels, lightning(): pl.pallas_call(mix_kernel, grid_spec=pltpu.PrefetchScalarGridSpec(num_sca...  7.41 us
    pallas_call x2, Pallas kernels, softmax_heads(): pl.pallas_call(soft_kernel, grid_spec=pltpu.PrefetchScalarGridSpec(num_sc...  7.4 us
    pallas_call x1, Pallas kernels, closing_states(): pl.pallas_call(states_kernel, grid=(parts,), in_specs=[wide, wide, pl.Blo...  3.98 us
    pallas_call x5, Pallas kernels, placed(): pl.pallas_call(functools.partial(place_kernel, start), in_specs=[anywhere...  3.82 us
  transfers between devices with their start and end apart: 9, of which 6 were waited for; matrix products, arithmetic and copies ran while one was open for 0% of the time, Pallas kernels for 33%

profile of v4, /device:TPU:1, one launch (start us, length us, event | category | flops | bytes accessed | tf_op | source)
XLA Modules:
  0.0 55.7 jit_solution(5451082637305434278)
XLA Ops:
  0.6 54.9 %conditional.1 = (bf16[1,256,2048]{2,1,0:T(8,128)(2,1)}, bf16[1,256,2048]{2,1,0:T(8,128)(2,1)}) conditional(s32[]{:T(128)} %convert_element_type.3, (bf16[1,256,2048]{2,1,0:T(8,128)(2,1)}, bf16[1,256,2048]{2,1,0:T(8,128)(2,1)}, f32[1,16,256]{2,1,0:T(8,128)}, bf16[1,256,256]{2,1,0:T(8,128)(2,1)}, bf16[1,256,256]{2,1,0:T(8,128)(2,1)}, ...), branch_computations={%region_0.0_spmd, %region_1.0_spmd} | conditional | bytes 19923556 | solution.py:523
  0.6 2.1 %collective-permute-start.1 = (bf16[1,256,256]{2,1,0:T(8,128)(2,1)}, bf16[1,256,256]{2,1,0:T(8,128)(2,1)S(1)}, u32[]{:S(2)}, u32[]{:S(2)}) collective-permute-start(bf16[1,256,256]{2,1,0:T(8,128)(2,1)} %get-tuple-element.49.key_ref), channel_id=1, source_target_pairs={{16,0},{0,16},{17,1},{1,17},{18,2},{2,18},{19,3},{3,19},{20,4},{4,... | collective-permute-start | bytes 393224 | tf_op jit(solution)/shard_map/cond/branch_0_fun/ppermute | solution.py:25
  2.8 0.1 collective-permute-start.2
  2.8 4.0 %closing_states.2 = (bf16[8,128,128]{2,1,0:T(8,128)(2,1)S(1)}, bf16[8,128,128]{2,1,0:T(8,128)(2,1)S(1)}) custom-call(bf16[1,256,2048]{2,1,0:T(8,128)(2,1)} %get-tuple-element.42.key_ref, bf16[1,256,2048]{2,1,0:T(8,128)(2,1)} %get-tuple-element.43.value_ref, f32[1,16,256]{2,1,0:T(8,128)} %get-tuple-element.44.decay_ref), custom_call_target="tpu_custom_call" | custom-call | tf_op jit(solution)/shard_map/cond/branch_0_fun/closing_states/pallas_call | solution.py:66
  6.8 0.0 collective-permute-done.1.before_key_ref
  6.8 0.0 copy-start.3
  6.9 0.0 copy-start.4
  6.9 0.6 %copy-done.3 = bf16[1,256,256]{2,1,0:T(8,128)(2,1)} copy-done((bf16[1,256,256]{2,1,0:T(8,128)(2,1)}, bf16[1,256,256]{2,1,0:T(8,128)(2,1)S(1)}, u32[]{:S(2)}) %copy-start.3) | copy-done | bytes 131096 | tf_op jit(solution)/shard_map/cond
  7.5 0.0 copy-done.4
  7.5 3.7 %softmax_heads.2 = bf16[1,256,1024]{2,1,0:T(8,128)(2,1)S(1)} custom-call(s32[1]{0:T(128)} %get-tuple-element.40.place_ref, bf16[1,256,2048]{2,1,0:T(8,128)(2,1)} %get-tuple-element.54.query_ref, bf16[1,256,256]{2,1,0:T(8,128)(2,1)} %get-tuple-element.49.key_ref, bf16[1,256,256]{2,1,0:T(8,128)(2,1)} %get-tuple-element.50.value_ref, ...), custom_call_target="tpu_custom_call" | custom-call | tf_op jit(solution)/shard_map/cond/branch_0_fun/softmax_heads/pallas_call | solution.py:248
  11.2 1.7 %collective-permute-start.7 = (bf16[1,256,1024]{2,1,0:T(8,128)(2,1)S(1)}, bf16[1,256,1024]{2,1,0:T(8,128)(2,1)S(1)}, u32[]{:S(2)}, u32[]{:S(2)}) collective-permute-start(bf16[1,256,1024]{2,1,0:T(8,128)(2,1)S(1)} %softmax_heads.2), channel_id=1, source_target_pairs={{3,0},{0,1},{1,2},{2,3},{7,4},{4,5},{5,6},{6,7},{11,8},{8,9},{9,10... | collective-permute-start | bytes 1572872 | tf_op jit(solution)/shard_map/cond/branch_0_fun/ppermute | solution.py:25
  13.0 3.7 %softmax_heads.3 = bf16[1,256,1024]{2,1,0:T(8,128)(2,1)S(1)} custom-call(s32[1]{0:T(128)} %get-tuple-element.40.place_ref, bf16[1,256,2048]{2,1,0:T(8,128)(2,1)} %get-tuple-element.54.query_ref, bf16[1,256,256]{2,1,0:T(8,128)(2,1)} %get-tuple-element.49.key_ref, bf16[1,256,256]{2,1,0:T(8,128)(2,1)} %get-tuple-element.50.value_ref, ...), custom_call_target="tpu_custom_call" | custom-call | tf_op jit(solution)/shard_map/cond/branch_0_fun/softmax_heads/pallas_call | solution.py:248
  16.7 1.4 %collective-permute-start.3 = (bf16[1,256,1024]{2,1,0:T(8,128)(2,1)S(1)}, bf16[1,256,1024]{2,1,0:T(8,128)(2,1)S(1)}, u32[]{:S(2)}, u32[]{:S(2)}) collective-permute-start(bf16[1,256,1024]{2,1,0:T(8,128)(2,1)S(1)} %softmax_heads.3), channel_id=1, source_target_pairs={{3,0},{0,1},{1,2},{2,3},{7,4},{4,5},{5,6},{6,7},{11,8},{8,9},{9,10... | collective-permute-start | bytes 1572872 | tf_op jit(solution)/shard_map/cond/branch_0_fun/ppermute | solution.py:25
  18.0 1.2 %collective-permute-start.6 = (bf16[8,128,128]{2,1,0:T(8,128)(2,1)S(1)}, bf16[8,128,128]{2,1,0:T(8,128)(2,1)S(1)}, u32[]{:S(2)}, u32[]{:S(2)}) collective-permute-start(bf16[8,128,128]{2,1,0:T(8,128)(2,1)S(1)} %get-tuple-element.58), channel_id=1, source_target_pairs={{16,0},{0,16},{17,1},{1,17},{18,2},{2,18},{19,3},{3,19},{20,4},{4,... | collective-permute-start | bytes 786440 | tf_op jit(solution)/shard_map/cond/branch_0_fun/ppermute | solution.py:25
  19.3 0.3 collective-permute-start
  19.5 4.1 %collective-permute-done.6.state_ref = bf16[8,128,128]{2,1,0:T(8,128)(2,1)S(1)} collective-permute-done((bf16[8,128,128]{2,1,0:T(8,128)(2,1)S(1)}, bf16[8,128,128]{2,1,0:T(8,128)(2,1)S(1)}, u32[]{:S(2)}, u32[]{:S(2)}) %collective-permute-start.6) | collective-permute-done | bytes 262176 | tf_op jit(solution)/shard_map/cond/branch_0_fun/ppermute | solution.py:25
  23.6 4.0 %collective-permute-done.7.block_ref = bf16[1,256,1024]{2,1,0:T(8,128)(2,1)S(1)} collective-permute-done((bf16[1,256,1024]{2,1,0:T(8,128)(2,1)S(1)}, bf16[1,256,1024]{2,1,0:T(8,128)(2,1)S(1)}, u32[]{:S(2)}, u32[]{:S(2)}) %collective-permute-start.7) | collective-permute-done | bytes 524320 | tf_op jit(solution)/shard_map/cond/branch_0_fun/ppermute | solution.py:25
  27.6 3.7 %lightning_mix.5 = bf16[1,256,1024]{2,1,0:T(8,128)(2,1)S(1)} custom-call(s32[1]{0:T(128)} %get-tuple-element.40.place_ref, bf16[1,256,2048]{2,1,0:T(8,128)(2,1)} %get-tuple-element.41.query_ref, bf16[1,256,2048]{2,1,0:T(8,128)(2,1)} %get-tuple-element.42.key_ref, bf16[1,256,2048]{2,1,0:T(8,128)(2,1)} %get-tuple-element.43.value_ref, ...), custom_call_target="tpu_custom_call" | custom-call | tf_op jit(solution)/shard_map/cond/branch_0_fun/lightning_mix/pallas_call | solution.py:130
  31.3 0.1 collective-permute-start.8
  31.3 0.0 collective-permute-done.state_ref
  31.3 7.4 %collective-permute-done.3.block_ref = bf16[1,256,1024]{2,1,0:T(8,128)(2,1)S(1)} collective-permute-done((bf16[1,256,1024]{2,1,0:T(8,128)(2,1)S(1)}, bf16[1,256,1024]{2,1,0:T(8,128)(2,1)S(1)}, u32[]{:S(2)}, u32[]{:S(2)}) %collective-permute-start.3) | collective-permute-done | bytes 524320 | tf_op jit(solution)/shard_map/cond/branch_0_fun/ppermute | solution.py:25
  38.8 3.7 %lightning_mix.4 = (bf16[1,256,768]{2,1,0:T(8,128)(2,1)S(1)}, bf16[1,256,256]{2,1,0:T(8,128)(2,1)S(1)}) custom-call(s32[1]{0:T(128)} %get-tuple-element.40.place_ref, bf16[1,256,2048]{2,1,0:T(8,128)(2,1)} %get-tuple-element.41.query_ref, bf16[1,256,2048]{2,1,0:T(8,128)(2,1)} %get-tuple-element.42.key_ref, bf16[1,256,2048]{2,1,0:T(8,128)(2,1)} %get-tuple-element.43.value_ref, ...), custom_call_target="tpu_custom_call" | custom-call | tf_op jit(solution)/shard_map/cond/branch_0_fun/lightning_mix/pallas_call | solution.py:130
  42.5 0.1 collective-permute-start.5
  42.6 0.7 %collective-permute-start.4 = (bf16[1,256,256]{2,1,0:T(8,128)(2,1)S(1)}, bf16[1,256,256]{2,1,0:T(8,128)(2,1)S(1)}, u32[]{:S(2)}, u32[]{:S(2)}) collective-permute-start(bf16[1,256,256]{2,1,0:T(8,128)(2,1)S(1)} %get-tuple-element.56), channel_id=1, source_target_pairs={{3,0},{0,1},{1,2},{2,3},{7,4},{4,5},{5,6},{6,7},{11,8},{8,9},{9,10... | collective-permute-start | bytes 393224 | tf_op jit(solution)/shard_map/cond/branch_0_fun/ppermute | solution.py:25
  43.3 0.8 %placed.11.refs_0_ = bf16[1,256,2048]{2,1,0:T(8,128)(2,1)} custom-call(bf16[1,256,1024]{2,1,0:T(8,128)(2,1)S(1)} %collective-permute-done.7.block_ref), custom_call_target="tpu_custom_call" | custom-call | tf_op jit(solution)/shard_map/cond/branch_0_fun/placed/pallas_call | solution.py:343
  44.1 0.8 %placed.12 = bf16[1,256,2048]{2,1,0:T(8,128)(2,1)} custom-call(bf16[1,256,1024]{2,1,0:T(8,128)(2,1)S(1)} %collective-permute-done.3.block_ref, bf16[1,256,2048]{2,1,0:T(8,128)(2,1)} %placed.11.refs_0_), custom_call_target="tpu_custom_call", output_to_operand_aliasing={{}: (1, {})} | custom-call | tf_op jit(solution)/shard_map/cond/branch_0_fun/placed/pallas_call | solution.py:343
  44.9 4.1 %collective-permute-done.8.block_ref = bf16[1,256,1024]{2,1,0:T(8,128)(2,1)S(1)} collective-permute-done((bf16[1,256,1024]{2,1,0:T(8,128)(2,1)S(1)}, bf16[1,256,1024]{2,1,0:T(8,128)(2,1)S(1)}, u32[]{:S(2)}, u32[]{:S(2)}) %collective-permute-start.8) | collective-permute-done | bytes 524320 | tf_op jit(solution)/shard_map/cond/branch_0_fun/ppermute | solution.py:25
  49.0 0.8 %placed.8.refs_0_ = bf16[1,256,2048]{2,1,0:T(8,128)(2,1)} custom-call(bf16[1,256,1024]{2,1,0:T(8,128)(2,1)S(1)} %collective-permute-done.8.block_ref), custom_call_target="tpu_custom_call" | custom-call | tf_op jit(solution)/shard_map/cond/branch_0_fun/placed/pallas_call | solution.py:343
  49.8 3.4 %collective-permute-done.5.block_ref = bf16[1,256,768]{2,1,0:T(8,128)(2,1)S(1)} collective-permute-done((bf16[1,256,768]{2,1,0:T(8,128)(2,1)S(1)}, bf16[1,256,768]{2,1,0:T(8,128)(2,1)S(1)}, u32[]{:S(2)}, u32[]{:S(2)}) %collective-permute-start.5) | collective-permute-done | bytes 393248 | tf_op jit(solution)/shard_map/cond/branch_0_fun/ppermute | solution.py:25
  53.2 0.8 %placed.9.refs_0_ = bf16[1,256,2048]{2,1,0:T(8,128)(2,1)} custom-call(bf16[1,256,768]{2,1,0:T(8,128)(2,1)S(1)} %collective-permute-done.5.block_ref, bf16[1,256,2048]{2,1,0:T(8,128)(2,1)} %placed.8.refs_0_), custom_call_target="tpu_custom_call", output_to_operand_aliasing={{}: (1, {})} | custom-call | tf_op jit(solution)/shard_map/cond/branch_0_fun/placed/pallas_call | solution.py:343
  54.0 0.6 %collective-permute-done.4.block_ref = bf16[1,256,256]{2,1,0:T(8,128)(2,1)S(1)} collective-permute-done((bf16[1,256,256]{2,1,0:T(8,128)(2,1)S(1)}, bf16[1,256,256]{2,1,0:T(8,128)(2,1)S(1)}, u32[]{:S(2)}, u32[]{:S(2)}) %collective-permute-start.4) | collective-permute-done | bytes 131104 | tf_op jit(solution)/shard_map/cond/branch_0_fun/ppermute | solution.py:25
  54.6 0.7 %placed.10 = bf16[1,256,2048]{2,1,0:T(8,128)(2,1)} custom-call(bf16[1,256,256]{2,1,0:T(8,128)(2,1)S(1)} %collective-permute-done.4.block_ref, bf16[1,256,2048]{2,1,0:T(8,128)(2,1)} %placed.9.refs_0_), custom_call_target="tpu_custom_call", output_to_operand_aliasing={{}: (1, {})} | custom-call | tf_op jit(solution)/shard_map/cond/branch_0_fun/placed/pallas_call | solution.py:343
  (1 shorter events, 0.0 us)
Async XLA Ops:
  0.6 6.2 %collective-permute-start.1 = (bf16[1,256,256]{2,1,0:T(8,128)(2,1)}, bf16[1,256,256]{2,1,0:T(8,128)(2,1)S(1)}, u32[]{:S(2)}, u32[]{:S(2)}) collective-permute-start(bf16[1,256,256]{2,1,0:T(8,128)(2,1)} %get-tuple-element.49.key_ref), channel_id=1, source_target_pairs={{16,0},{0,16},{17,1},{1,17},{18,2},{2,18},{19,3},{3,19},{20,4},{4,... | collective-permute-start | bytes 393224 | tf_op jit(solution)/shard_map/cond/branch_0_fun/ppermute | solution.py:25
  2.8 4.1 %collective-permute-start.2 = (bf16[1,256,256]{2,1,0:T(8,128)(2,1)}, bf16[1,256,256]{2,1,0:T(8,128)(2,1)S(1)}, u32[]{:S(2)}, u32[]{:S(2)}) collective-permute-start(bf16[1,256,256]{2,1,0:T(8,128)(2,1)} %get-tuple-element.50.value_ref), channel_id=1, source_target_pairs={{16,0},{0,16},{17,1},{1,17},{18,2},{2,18},{19,3},{3,19},{20,4},{4,... | collective-permute-start | bytes 393224 | tf_op jit(solution)/shard_map/cond/branch_0_fun/ppermute | solution.py:25
  6.8 0.7 %copy-start.3 = (bf16[1,256,256]{2,1,0:T(8,128)(2,1)}, bf16[1,256,256]{2,1,0:T(8,128)(2,1)S(1)}, u32[]{:S(2)}) copy-start(bf16[1,256,256]{2,1,0:T(8,128)(2,1)S(1)} %collective-permute-done.1.before_key_ref) | copy-start | bytes 393220 | tf_op jit(solution)/shard_map/cond
  6.9 0.7 %copy-start.4 = (bf16[1,256,256]{2,1,0:T(8,128)(2,1)}, bf16[1,256,256]{2,1,0:T(8,128)(2,1)S(1)}, u32[]{:S(2)}) copy-start(bf16[1,256,256]{2,1,0:T(8,128)(2,1)S(1)} %collective-permute-done.2.before_value_ref) | copy-start | bytes 393220 | tf_op jit(solution)/shard_map/cond
  11.2 16.3 %collective-permute-start.7 = (bf16[1,256,1024]{2,1,0:T(8,128)(2,1)S(1)}, bf16[1,256,1024]{2,1,0:T(8,128)(2,1)S(1)}, u32[]{:S(2)}, u32[]{:S(2)}) collective-permute-start(bf16[1,256,1024]{2,1,0:T(8,128)(2,1)S(1)} %softmax_heads.2), channel_id=1, source_target_pairs={{3,0},{0,1},{1,2},{2,3},{7,4},{4,5},{5,6},{6,7},{11,8},{8,9},{9,10... | collective-permute-start | bytes 1572872 | tf_op jit(solution)/shard_map/cond/branch_0_fun/ppermute | solution.py:25
  16.7 22.1 %collective-permute-start.3 = (bf16[1,256,1024]{2,1,0:T(8,128)(2,1)S(1)}, bf16[1,256,1024]{2,1,0:T(8,128)(2,1)S(1)}, u32[]{:S(2)}, u32[]{:S(2)}) collective-permute-start(bf16[1,256,1024]{2,1,0:T(8,128)(2,1)S(1)} %softmax_heads.3), channel_id=1, source_target_pairs={{3,0},{0,1},{1,2},{2,3},{7,4},{4,5},{5,6},{6,7},{11,8},{8,9},{9,10... | collective-permute-start | bytes 1572872 | tf_op jit(solution)/shard_map/cond/branch_0_fun/ppermute | solution.py:25
  18.0 5.5 %collective-permute-start.6 = (bf16[8,128,128]{2,1,0:T(8,128)(2,1)S(1)}, bf16[8,128,128]{2,1,0:T(8,128)(2,1)S(1)}, u32[]{:S(2)}, u32[]{:S(2)}) collective-permute-start(bf16[8,128,128]{2,1,0:T(8,128)(2,1)S(1)} %get-tuple-element.58), channel_id=1, source_target_pairs={{16,0},{0,16},{17,1},{1,17},{18,2},{2,18},{19,3},{3,19},{20,4},{4,... | collective-permute-start | bytes 786440 | tf_op jit(solution)/shard_map/cond/branch_0_fun/ppermute | solution.py:25
  19.3 12.1 %collective-permute-start = (bf16[8,128,128]{2,1,0:T(8,128)(2,1)S(1)}, bf16[8,128,128]{2,1,0:T(8,128)(2,1)S(1)}, u32[]{:S(2)}, u32[]{:S(2)}) collective-permute-start(bf16[8,128,128]{2,1,0:T(8,128)(2,1)S(1)} %get-tuple-element.47), channel_id=1, source_target_pairs={{16,0},{0,16},{17,1},{1,17},{18,2},{2,18},{19,3},{3,19},{20,4},{4,... | collective-permute-start | bytes 786440 | tf_op jit(solution)/shard_map/cond/branch_0_fun/ppermute | solution.py:25
  31.3 17.8 %collective-permute-start.8 = (bf16[1,256,1024]{2,1,0:T(8,128)(2,1)S(1)}, bf16[1,256,1024]{2,1,0:T(8,128)(2,1)S(1)}, u32[]{:S(2)}, u32[]{:S(2)}) collective-permute-start(bf16[1,256,1024]{2,1,0:T(8,128)(2,1)S(1)} %lightning_mix.5), channel_id=1, source_target_pairs={{3,0},{0,1},{1,2},{2,3},{7,4},{4,5},{5,6},{6,7},{11,8},{8,9},{9,10... | collective-permute-start | bytes 1572872 | tf_op jit(solution)/shard_map/cond/branch_0_fun/ppermute | solution.py:25
  42.5 10.7 %collective-permute-start.5 = (bf16[1,256,768]{2,1,0:T(8,128)(2,1)S(1)}, bf16[1,256,768]{2,1,0:T(8,128)(2,1)S(1)}, u32[]{:S(2)}, u32[]{:S(2)}) collective-permute-start(bf16[1,256,768]{2,1,0:T(8,128)(2,1)S(1)} %get-tuple-element.57), channel_id=1, source_target_pairs={{3,0},{0,1},{1,2},{2,3},{7,4},{4,5},{5,6},{6,7},{11,8},{8,9},{9,10... | collective-permute-start | bytes 1179656 | tf_op jit(solution)/shard_map/cond/branch_0_fun/ppermute | solution.py:25
  42.6 12.1 %collective-permute-start.4 = (bf16[1,256,256]{2,1,0:T(8,128)(2,1)S(1)}, bf16[1,256,256]{2,1,0:T(8,128)(2,1)S(1)}, u32[]{:S(2)}, u32[]{:S(2)}) collective-permute-start(bf16[1,256,256]{2,1,0:T(8,128)(2,1)S(1)} %get-tuple-element.56), channel_id=1, source_target_pairs={{3,0},{0,1},{1,2},{2,3},{7,4},{4,5},{5,6},{6,7},{11,8},{8,9},{9,10... | collective-permute-start | bytes 393224 | tf_op jit(solution)/shard_map/cond/branch_0_fun/ppermute | solution.py:25

commit v5 on v4

--- a/solution.py
+++ b/solution.py
@@ -265,12 +265,12 @@
     )(place, soft_query, key[0], value[0], before_key[0], before_value[0])
 
 
-def softmax_all(place, query, key, value, before_key, before_value):
-    groups = key.shape[2] // HD
-    others = before_key.shape[0]
-
-    def by_group(rows, width):
-        return pl.BlockSpec((rows, BLK, width), lambda i, place: (0, 0, i))
+def softmax_all(place, query, pair, before):
+    groups = pair.shape[2] // (2 * HD)
+    others = before.shape[0]
+
+    def by_group(rows, width, start=0):
+        return pl.BlockSpec((rows, BLK, width), lambda i, place: (0, 0, start + i))
 
     return pl.pallas_call(
         soft_kernel,
@@ -280,16 +280,39 @@
             in_specs=[
                 by_group(1, GROUP * HD),
                 by_group(1, HD),
-                by_group(1, HD),
+                by_group(1, HD, groups),
                 by_group(others, HD),
-                by_group(others, HD),
+                by_group(others, HD, groups),
             ],
             out_specs=by_group(1, GROUP * HD),
         ),
         out_shape=pltpu.HBM(query.shape, jnp.bfloat16),
         compiler_params=pltpu.CompilerParams(vmem_limit_bytes=20 * MIB),
         name="softmax_all",
-    )(place, query, key, value, before_key, before_value)
+    )(place, query, pair, pair, before, before)
+
+
+def joined_kernel(key_ref, value_ref, out_ref, sems):
+    width = key_ref.shape[2]
+    copied(
+        [
+            (key_ref, out_ref.at[:, :, pl.ds(0, width)]),
+            (value_ref, out_ref.at[:, :, pl.ds(width, width)]),
+        ],
+        sems,
+    )
+
+
+def side_by_side(soft_key, soft_value):
+    return pl.pallas_call(
+        joined_kernel,
+        in_specs=[pl.BlockSpec(memory_space=pltpu.HBM)] * 2,
+        out_specs=pl.BlockSpec(memory_space=pltpu.VMEM),
+        out_shape=pltpu.VMEM((1, BLK, 2 * soft_key.shape[2]), jnp.bfloat16),
+        scratch_shapes=[pltpu.SemaphoreType.DMA((2,))],
+        compiler_params=pltpu.CompilerParams(vmem_limit_bytes=2 * MIB),
+        name="side_by_side",
+    )(soft_key, soft_value)
 
 
 def finish_kernel(
@@ -442,18 +465,16 @@
     soft_value,
     place,
 ):
-    handed_key = passed_along(soft_key, "pp", 1)
-    handed_value = passed_along(soft_value, "pp", 1)
     handed_query = passed_along(soft_query, "pp", 1)
+    pair = side_by_side(soft_key, soft_value)
+    lin_key, lin_value, pair = lax.optimization_barrier((lin_key, lin_value, pair))
+    handed_pair = passed_along(pair, "pp", 1)
     closing = closing_states(lin_key, lin_value, decay_rows, PARTS)
     incoming = [incoming_states(closing[part], device_logs[part]) for part in range(PARTS)]
-    incoming[-1], handed_query, handed_key, handed_value = lax.optimization_barrier(
-        (incoming[-1], handed_query, handed_key, handed_value)
-    )
-    befores = (earlier_blocks(handed_key), earlier_blocks(handed_value))
+    incoming[-1], handed_query, handed_pair = lax.optimization_barrier((incoming[-1], handed_query, handed_pair))
     arrays = (lin_query, lin_key, lin_value, decay_rows, out_gate, norm_gain)
     chunks = lightning_chunks(place, arrays, incoming)
-    soft_handed = softmax_all(place, handed_query, handed_key, handed_value, *befores)
+    soft_handed = softmax_all(place, handed_query, handed_pair, earlier_blocks(handed_pair))
     return (joined(chunks, lin_query.shape[2]), soft_handed)
 
 

time: 55.9 us -> 56 us (level)
  no operation moved by 1% of the time
where the time goes in v5:
time: 56 us; the launch traced here: 55.7 us
  waiting for transfers between devices  23.6 us (42%)
  Pallas kernels  22.6 us (40%)
  starting transfers between devices  7.6 us (14%)
  between operations  0.82 us (1%)
  local copies, waits for them, and re-layouts  0.67 us (1%)
    ppermute x9, waiting for transfers between devices, passed_along(): lax.ppermute(block, axis, [((i - distance) % devices, i) for i in range(d...  23.6 us
    ppermute x9, starting transfers between devices, passed_along(): lax.ppermute(block, axis, [((i - distance) % devices, i) for i in range(d...  7.6 us
    pallas_call x2, Pallas kernels, lightning(): pl.pallas_call(mix_kernel, grid_spec=pltpu.PrefetchScalarGridSpec(num_sca...  7.41 us
    pallas_call x2, Pallas kernels, softmax_heads(): pl.pallas_call(soft_kernel, grid_spec=pltpu.PrefetchScalarGridSpec(num_sc...  7.4 us
    pallas_call x1, Pallas kernels, closing_states(): pl.pallas_call(states_kernel, grid=(parts,), in_specs=[wide, wide, pl.Blo...  3.98 us
    pallas_call x5, Pallas kernels, placed(): pl.pallas_call(functools.partial(place_kernel, start), in_specs=[anywhere...  3.82 us
  transfers between devices with their start and end apart: 9, of which 6 were waited for; matrix products, arithmetic and copies ran while one was open for 0% of the time, Pallas kernels for 33%

profile of v5, /device:TPU:1, one launch (start us, length us, event | category | flops | bytes accessed | tf_op | source)
XLA Modules:
  0.0 55.7 jit_solution(9767807249432050063)
XLA Ops:
  0.6 54.9 %conditional.1 = (bf16[1,256,2048]{2,1,0:T(8,128)(2,1)}, bf16[1,256,2048]{2,1,0:T(8,128)(2,1)}) conditional(s32[]{:T(128)} %convert_element_type.3, (bf16[1,256,2048]{2,1,0:T(8,128)(2,1)}, bf16[1,256,2048]{2,1,0:T(8,128)(2,1)}, f32[1,16,256]{2,1,0:T(8,128)}, bf16[1,256,256]{2,1,0:T(8,128)(2,1)}, bf16[1,256,256]{2,1,0:T(8,128)(2,1)}, ...), branch_computations={%region_0.0_spmd, %region_1.0_spmd} | conditional | bytes 16777580 | solution.py:544
  0.6 2.1 %collective-permute-start.1 = (bf16[1,256,256]{2,1,0:T(8,128)(2,1)}, bf16[1,256,256]{2,1,0:T(8,128)(2,1)S(1)}, u32[]{:S(2)}, u32[]{:S(2)}) collective-permute-start(bf16[1,256,256]{2,1,0:T(8,128)(2,1)} %get-tuple-element.49.key_ref), channel_id=1, source_target_pairs={{16,0},{0,16},{17,1},{1,17},{18,2},{2,18},{19,3},{3,19},{20,4},{4,... | collective-permute-start | bytes 393224 | tf_op jit(solution)/shard_map/cond/branch_0_fun/ppermute | solution.py:25
  2.8 0.1 collective-permute-start.2
  2.8 4.0 %closing_states.2 = (bf16[8,128,128]{2,1,0:T(8,128)(2,1)S(1)}, bf16[8,128,128]{2,1,0:T(8,128)(2,1)S(1)}) custom-call(bf16[1,256,2048]{2,1,0:T(8,128)(2,1)} %get-tuple-element.42.key_ref, bf16[1,256,2048]{2,1,0:T(8,128)(2,1)} %get-tuple-element.43.value_ref, f32[1,16,256]{2,1,0:T(8,128)} %get-tuple-element.44.decay_ref), custom_call_target="tpu_custom_call" | custom-call | tf_op jit(solution)/shard_map/cond/branch_0_fun/closing_states/pallas_call | solution.py:66
  6.8 0.0 collective-permute-done.1.before_key_ref
  6.8 0.0 copy-start.1
  6.9 0.0 copy-start.2
  6.9 0.6 %copy-done.1 = bf16[1,256,256]{2,1,0:T(8,128)(2,1)} copy-done((bf16[1,256,256]{2,1,0:T(8,128)(2,1)}, bf16[1,256,256]{2,1,0:T(8,128)(2,1)S(1)}, u32[]{:S(2)}) %copy-start.1) | copy-done | bytes 131096 | tf_op jit(solution)/shard_map/cond
  7.5 0.0 copy-done.2
  7.5 3.7 %softmax_heads.2 = bf16[1,256,1024]{2,1,0:T(8,128)(2,1)S(1)} custom-call(s32[1]{0:T(128)} %get-tuple-element.40.place_ref, bf16[1,256,2048]{2,1,0:T(8,128)(2,1)} %get-tuple-element.54.query_ref, bf16[1,256,256]{2,1,0:T(8,128)(2,1)} %get-tuple-element.49.key_ref, bf16[1,256,256]{2,1,0:T(8,128)(2,1)} %get-tuple-element.50.value_ref, ...), custom_call_target="tpu_custom_call" | custom-call | tf_op jit(solution)/shard_map/cond/branch_0_fun/softmax_heads/pallas_call | solution.py:248
  11.2 1.7 %collective-permute-start.7 = (bf16[1,256,1024]{2,1,0:T(8,128)(2,1)S(1)}, bf16[1,256,1024]{2,1,0:T(8,128)(2,1)S(1)}, u32[]{:S(2)}, u32[]{:S(2)}) collective-permute-start(bf16[1,256,1024]{2,1,0:T(8,128)(2,1)S(1)} %softmax_heads.2), channel_id=1, source_target_pairs={{3,0},{0,1},{1,2},{2,3},{7,4},{4,5},{5,6},{6,7},{11,8},{8,9},{9,10... | collective-permute-start | bytes 1572872 | tf_op jit(solution)/shard_map/cond/branch_0_fun/ppermute | solution.py:25
  13.0 3.7 %softmax_heads.3 = bf16[1,256,1024]{2,1,0:T(8,128)(2,1)S(1)} custom-call(s32[1]{0:T(128)} %get-tuple-element.40.place_ref, bf16[1,256,2048]{2,1,0:T(8,128)(2,1)} %get-tuple-element.54.query_ref, bf16[1,256,256]{2,1,0:T(8,128)(2,1)} %get-tuple-element.49.key_ref, bf16[1,256,256]{2,1,0:T(8,128)(2,1)} %get-tuple-element.50.value_ref, ...), custom_call_target="tpu_custom_call" | custom-call | tf_op jit(solution)/shard_map/cond/branch_0_fun/softmax_heads/pallas_call | solution.py:248
  16.7 1.4 %collective-permute-start.3 = (bf16[1,256,1024]{2,1,0:T(8,128)(2,1)S(1)}, bf16[1,256,1024]{2,1,0:T(8,128)(2,1)S(1)}, u32[]{:S(2)}, u32[]{:S(2)}) collective-permute-start(bf16[1,256,1024]{2,1,0:T(8,128)(2,1)S(1)} %softmax_heads.3), channel_id=1, source_target_pairs={{3,0},{0,1},{1,2},{2,3},{7,4},{4,5},{5,6},{6,7},{11,8},{8,9},{9,10... | collective-permute-start | bytes 1572872 | tf_op jit(solution)/shard_map/cond/branch_0_fun/ppermute | solution.py:25
  18.0 1.2 %collective-permute-start.6 = (bf16[8,128,128]{2,1,0:T(8,128)(2,1)S(1)}, bf16[8,128,128]{2,1,0:T(8,128)(2,1)S(1)}, u32[]{:S(2)}, u32[]{:S(2)}) collective-permute-start(bf16[8,128,128]{2,1,0:T(8,128)(2,1)S(1)} %get-tuple-element.58), channel_id=1, source_target_pairs={{16,0},{0,16},{17,1},{1,17},{18,2},{2,18},{19,3},{3,19},{20,4},{4,... | collective-permute-start | bytes 786440 | tf_op jit(solution)/shard_map/cond/branch_0_fun/ppermute | solution.py:25
  19.3 0.3 collective-permute-start
  19.5 4.1 %collective-permute-done.6.state_ref = bf16[8,128,128]{2,1,0:T(8,128)(2,1)S(1)} collective-permute-done((bf16[8,128,128]{2,1,0:T(8,128)(2,1)S(1)}, bf16[8,128,128]{2,1,0:T(8,128)(2,1)S(1)}, u32[]{:S(2)}, u32[]{:S(2)}) %collective-permute-start.6) | collective-permute-done | bytes 262176 | tf_op jit(solution)/shard_map/cond/branch_0_fun/ppermute | solution.py:25
  23.6 4.0 %collective-permute-done.7.block_ref = bf16[1,256,1024]{2,1,0:T(8,128)(2,1)S(1)} collective-permute-done((bf16[1,256,1024]{2,1,0:T(8,128)(2,1)S(1)}, bf16[1,256,1024]{2,1,0:T(8,128)(2,1)S(1)}, u32[]{:S(2)}, u32[]{:S(2)}) %collective-permute-start.7) | collective-permute-done | bytes 524320 | tf_op jit(solution)/shard_map/cond/branch_0_fun/ppermute | solution.py:25
  27.6 3.7 %lightning_mix.5 = bf16[1,256,1024]{2,1,0:T(8,128)(2,1)S(1)} custom-call(s32[1]{0:T(128)} %get-tuple-element.40.place_ref, bf16[1,256,2048]{2,1,0:T(8,128)(2,1)} %get-tuple-element.41.query_ref, bf16[1,256,2048]{2,1,0:T(8,128)(2,1)} %get-tuple-element.42.key_ref, bf16[1,256,2048]{2,1,0:T(8,128)(2,1)} %get-tuple-element.43.value_ref, ...), custom_call_target="tpu_custom_call" | custom-call | tf_op jit(solution)/shard_map/cond/branch_0_fun/lightning_mix/pallas_call | solution.py:130
  31.3 0.1 collective-permute-start.8
  31.3 0.0 collective-permute-done.state_ref
  31.3 7.4 %collective-permute-done.3.block_ref = bf16[1,256,1024]{2,1,0:T(8,128)(2,1)S(1)} collective-permute-done((bf16[1,256,1024]{2,1,0:T(8,128)(2,1)S(1)}, bf16[1,256,1024]{2,1,0:T(8,128)(2,1)S(1)}, u32[]{:S(2)}, u32[]{:S(2)}) %collective-permute-start.3) | collective-permute-done | bytes 524320 | tf_op jit(solution)/shard_map/cond/branch_0_fun/ppermute | solution.py:25
  38.8 3.7 %lightning_mix.4 = (bf16[1,256,768]{2,1,0:T(8,128)(2,1)S(1)}, bf16[1,256,256]{2,1,0:T(8,128)(2,1)S(1)}) custom-call(s32[1]{0:T(128)} %get-tuple-element.40.place_ref, bf16[1,256,2048]{2,1,0:T(8,128)(2,1)} %get-tuple-element.41.query_ref, bf16[1,256,2048]{2,1,0:T(8,128)(2,1)} %get-tuple-element.42.key_ref, bf16[1,256,2048]{2,1,0:T(8,128)(2,1)} %get-tuple-element.43.value_ref, ...), custom_call_target="tpu_custom_call" | custom-call | tf_op jit(solution)/shard_map/cond/branch_0_fun/lightning_mix/pallas_call | solution.py:130
  42.5 0.1 collective-permute-start.5
  42.6 0.7 %collective-permute-start.4 = (bf16[1,256,256]{2,1,0:T(8,128)(2,1)S(1)}, bf16[1,256,256]{2,1,0:T(8,128)(2,1)S(1)}, u32[]{:S(2)}, u32[]{:S(2)}) collective-permute-start(bf16[1,256,256]{2,1,0:T(8,128)(2,1)S(1)} %get-tuple-element.56), channel_id=1, source_target_pairs={{3,0},{0,1},{1,2},{2,3},{7,4},{4,5},{5,6},{6,7},{11,8},{8,9},{9,10... | collective-permute-start | bytes 393224 | tf_op jit(solution)/shard_map/cond/branch_0_fun/ppermute | solution.py:25
  43.3 0.8 %placed.11.refs_0_ = bf16[1,256,2048]{2,1,0:T(8,128)(2,1)} custom-call(bf16[1,256,1024]{2,1,0:T(8,128)(2,1)S(1)} %collective-permute-done.7.block_ref), custom_call_target="tpu_custom_call" | custom-call | tf_op jit(solution)/shard_map/cond/branch_0_fun/placed/pallas_call | solution.py:366
  44.1 0.8 %placed.12 = bf16[1,256,2048]{2,1,0:T(8,128)(2,1)} custom-call(bf16[1,256,1024]{2,1,0:T(8,128)(2,1)S(1)} %collective-permute-done.3.block_ref, bf16[1,256,2048]{2,1,0:T(8,128)(2,1)} %placed.11.refs_0_), custom_call_target="tpu_custom_call", output_to_operand_aliasing={{}: (1, {})} | custom-call | tf_op jit(solution)/shard_map/cond/branch_0_fun/placed/pallas_call | solution.py:366
  44.9 4.1 %collective-permute-done.8.block_ref = bf16[1,256,1024]{2,1,0:T(8,128)(2,1)S(1)} collective-permute-done((bf16[1,256,1024]{2,1,0:T(8,128)(2,1)S(1)}, bf16[1,256,1024]{2,1,0:T(8,128)(2,1)S(1)}, u32[]{:S(2)}, u32[]{:S(2)}) %collective-permute-start.8) | collective-permute-done | bytes 524320 | tf_op jit(solution)/shard_map/cond/branch_0_fun/ppermute | solution.py:25
  49.0 0.8 %placed.8.refs_0_ = bf16[1,256,2048]{2,1,0:T(8,128)(2,1)} custom-call(bf16[1,256,1024]{2,1,0:T(8,128)(2,1)S(1)} %collective-permute-done.8.block_ref), custom_call_target="tpu_custom_call" | custom-call | tf_op jit(solution)/shard_map/cond/branch_0_fun/placed/pallas_call | solution.py:366
  49.8 3.4 %collective-permute-done.5.block_ref = bf16[1,256,768]{2,1,0:T(8,128)(2,1)S(1)} collective-permute-done((bf16[1,256,768]{2,1,0:T(8,128)(2,1)S(1)}, bf16[1,256,768]{2,1,0:T(8,128)(2,1)S(1)}, u32[]{:S(2)}, u32[]{:S(2)}) %collective-permute-start.5) | collective-permute-done | bytes 393248 | tf_op jit(solution)/shard_map/cond/branch_0_fun/ppermute | solution.py:25
  53.2 0.8 %placed.9.refs_0_ = bf16[1,256,2048]{2,1,0:T(8,128)(2,1)} custom-call(bf16[1,256,768]{2,1,0:T(8,128)(2,1)S(1)} %collective-permute-done.5.block_ref, bf16[1,256,2048]{2,1,0:T(8,128)(2,1)} %placed.8.refs_0_), custom_call_target="tpu_custom_call", output_to_operand_aliasing={{}: (1, {})} | custom-call | tf_op jit(solution)/shard_map/cond/branch_0_fun/placed/pallas_call | solution.py:366
  54.0 0.6 %collective-permute-done.4.block_ref = bf16[1,256,256]{2,1,0:T(8,128)(2,1)S(1)} collective-permute-done((bf16[1,256,256]{2,1,0:T(8,128)(2,1)S(1)}, bf16[1,256,256]{2,1,0:T(8,128)(2,1)S(1)}, u32[]{:S(2)}, u32[]{:S(2)}) %collective-permute-start.4) | collective-permute-done | bytes 131104 | tf_op jit(solution)/shard_map/cond/branch_0_fun/ppermute | solution.py:25
  54.6 0.7 %placed.10 = bf16[1,256,2048]{2,1,0:T(8,128)(2,1)} custom-call(bf16[1,256,256]{2,1,0:T(8,128)(2,1)S(1)} %collective-permute-done.4.block_ref, bf16[1,256,2048]{2,1,0:T(8,128)(2,1)} %placed.9.refs_0_), custom_call_target="tpu_custom_call", output_to_operand_aliasing={{}: (1, {})} | custom-call | tf_op jit(solution)/shard_map/cond/branch_0_fun/placed/pallas_call | solution.py:366
  (1 shorter events, 0.0 us)
Async XLA Ops:
  0.6 6.2 %collective-permute-start.1 = (bf16[1,256,256]{2,1,0:T(8,128)(2,1)}, bf16[1,256,256]{2,1,0:T(8,128)(2,1)S(1)}, u32[]{:S(2)}, u32[]{:S(2)}) collective-permute-start(bf16[1,256,256]{2,1,0:T(8,128)(2,1)} %get-tuple-element.49.key_ref), channel_id=1, source_target_pairs={{16,0},{0,16},{17,1},{1,17},{18,2},{2,18},{19,3},{3,19},{20,4},{4,... | collective-permute-start | bytes 393224 | tf_op jit(solution)/shard_map/cond/branch_0_fun/ppermute | solution.py:25
  2.8 4.1 %collective-permute-start.2 = (bf16[1,256,256]{2,1,0:T(8,128)(2,1)}, bf16[1,256,256]{2,1,0:T(8,128)(2,1)S(1)}, u32[]{:S(2)}, u32[]{:S(2)}) collective-permute-start(bf16[1,256,256]{2,1,0:T(8,128)(2,1)} %get-tuple-element.50.value_ref), channel_id=1, source_target_pairs={{16,0},{0,16},{17,1},{1,17},{18,2},{2,18},{19,3},{3,19},{20,4},{4,... | collective-permute-start | bytes 393224 | tf_op jit(solution)/shard_map/cond/branch_0_fun/ppermute | solution.py:25
  6.8 0.7 %copy-start.1 = (bf16[1,256,256]{2,1,0:T(8,128)(2,1)}, bf16[1,256,256]{2,1,0:T(8,128)(2,1)S(1)}, u32[]{:S(2)}) copy-start(bf16[1,256,256]{2,1,0:T(8,128)(2,1)S(1)} %collective-permute-done.1.before_key_ref) | copy-start | bytes 393220 | tf_op jit(solution)/shard_map/cond
  6.9 0.7 %copy-start.2 = (bf16[1,256,256]{2,1,0:T(8,128)(2,1)}, bf16[1,256,256]{2,1,0:T(8,128)(2,1)S(1)}, u32[]{:S(2)}) copy-start(bf16[1,256,256]{2,1,0:T(8,128)(2,1)S(1)} %collective-permute-done.2.before_value_ref) | copy-start | bytes 393220 | tf_op jit(solution)/shard_map/cond
  11.2 16.3 %collective-permute-start.7 = (bf16[1,256,1024]{2,1,0:T(8,128)(2,1)S(1)}, bf16[1,256,1024]{2,1,0:T(8,128)(2,1)S(1)}, u32[]{:S(2)}, u32[]{:S(2)}) collective-permute-start(bf16[1,256,1024]{2,1,0:T(8,128)(2,1)S(1)} %softmax_heads.2), channel_id=1, source_target_pairs={{3,0},{0,1},{1,2},{2,3},{7,4},{4,5},{5,6},{6,7},{11,8},{8,9},{9,10... | collective-permute-start | bytes 1572872 | tf_op jit(solution)/shard_map/cond/branch_0_fun/ppermute | solution.py:25
  16.7 22.1 %collective-permute-start.3 = (bf16[1,256,1024]{2,1,0:T(8,128)(2,1)S(1)}, bf16[1,256,1024]{2,1,0:T(8,128)(2,1)S(1)}, u32[]{:S(2)}, u32[]{:S(2)}) collective-permute-start(bf16[1,256,1024]{2,1,0:T(8,128)(2,1)S(1)} %softmax_heads.3), channel_id=1, source_target_pairs={{3,0},{0,1},{1,2},{2,3},{7,4},{4,5},{5,6},{6,7},{11,8},{8,9},{9,10... | collective-permute-start | bytes 1572872 | tf_op jit(solution)/shard_map/cond/branch_0_fun/ppermute | solution.py:25
  18.0 5.5 %collective-permute-start.6 = (bf16[8,128,128]{2,1,0:T(8,128)(2,1)S(1)}, bf16[8,128,128]{2,1,0:T(8,128)(2,1)S(1)}, u32[]{:S(2)}, u32[]{:S(2)}) collective-permute-start(bf16[8,128,128]{2,1,0:T(8,128)(2,1)S(1)} %get-tuple-element.58), channel_id=1, source_target_pairs={{16,0},{0,16},{17,1},{1,17},{18,2},{2,18},{19,3},{3,19},{20,4},{4,... | collective-permute-start | bytes 786440 | tf_op jit(solution)/shard_map/cond/branch_0_fun/ppermute | solution.py:25
  19.3 12.1 %collective-permute-start = (bf16[8,128,128]{2,1,0:T(8,128)(2,1)S(1)}, bf16[8,128,128]{2,1,0:T(8,128)(2,1)S(1)}, u32[]{:S(2)}, u32[]{:S(2)}) collective-permute-start(bf16[8,128,128]{2,1,0:T(8,128)(2,1)S(1)} %get-tuple-element.47), channel_id=1, source_target_pairs={{16,0},{0,16},{17,1},{1,17},{18,2},{2,18},{19,3},{3,19},{20,4},{4,... | collective-permute-start | bytes 786440 | tf_op jit(solution)/shard_map/cond/branch_0_fun/ppermute | solution.py:25
  31.3 17.8 %collective-permute-start.8 = (bf16[1,256,1024]{2,1,0:T(8,128)(2,1)S(1)}, bf16[1,256,1024]{2,1,0:T(8,128)(2,1)S(1)}, u32[]{:S(2)}, u32[]{:S(2)}) collective-permute-start(bf16[1,256,1024]{2,1,0:T(8,128)(2,1)S(1)} %lightning_mix.5), channel_id=1, source_target_pairs={{3,0},{0,1},{1,2},{2,3},{7,4},{4,5},{5,6},{6,7},{11,8},{8,9},{9,10... | collective-permute-start | bytes 1572872 | tf_op jit(solution)/shard_map/cond/branch_0_fun/ppermute | solution.py:25
  42.5 10.7 %collective-permute-start.5 = (bf16[1,256,768]{2,1,0:T(8,128)(2,1)S(1)}, bf16[1,256,768]{2,1,0:T(8,128)(2,1)S(1)}, u32[]{:S(2)}, u32[]{:S(2)}) collective-permute-start(bf16[1,256,768]{2,1,0:T(8,128)(2,1)S(1)} %get-tuple-element.57), channel_id=1, source_target_pairs={{3,0},{0,1},{1,2},{2,3},{7,4},{4,5},{5,6},{6,7},{11,8},{8,9},{9,10... | collective-permute-start | bytes 1179656 | tf_op jit(solution)/shard_map/cond/branch_0_fun/ppermute | solution.py:25
  42.6 12.1 %collective-permute-start.4 = (bf16[1,256,256]{2,1,0:T(8,128)(2,1)S(1)}, bf16[1,256,256]{2,1,0:T(8,128)(2,1)S(1)}, u32[]{:S(2)}, u32[]{:S(2)}) collective-permute-start(bf16[1,256,256]{2,1,0:T(8,128)(2,1)S(1)} %get-tuple-element.56), channel_id=1, source_target_pairs={{3,0},{0,1},{1,2},{2,3},{7,4},{4,5},{5,6},{6,7},{11,8},{8,9},{9,10... | collective-permute-start | bytes 393224 | tf_op jit(solution)/shard_map/cond/branch_0_fun/ppermute | solution.py:25

commit v6 on v5

--- a/solution.py
+++ b/solution.py
@@ -495,6 +495,7 @@
     befores = (earlier_blocks(soft_key), earlier_blocks(soft_value))
     closing = list(closing_states(lin_key, lin_value, decay_rows, PARTS))
     closing[0], *befores = lax.optimization_barrier((closing[0], *befores))
+    befores = [pltpu.with_memory_space_constraint(before, pltpu.VMEM) for before in befores]
     incoming = [incoming_states(closing[part], device_logs[part]) for part in range(PARTS)]
     groups = []
     for g in range(kv_count):

time: 56 us -> 56 us (level)
  waiting for transfers between devices: 23.6 us -> 24.4 us
  local copies, waits for them, and re-layouts: 0.67 us -> 0 us
    ppermute x9, waiting for transfers between devices: 23.6 us -> 24.4 us  [passed_along(): lax.ppermute(block, axis, [((i - distance) % devices, i) for i in range(d...]
    cond x4 -> x0, local copies, waits for them, and re-layouts: 0.67 us -> none
where the time goes in v6:
time: 56 us; the launch traced here: 55.7 us
  waiting for transfers between devices  24.4 us (44%)
  Pallas kernels  22.6 us (40%)
  starting transfers between devices  7.59 us (14%)
  between operations  0.82 us (1%)
    ppermute x9, waiting for transfers between devices, passed_along(): lax.ppermute(block, axis, [((i - distance) % devices, i) for i in range(d...  24.4 us
    ppermute x9, starting transfers between devices, passed_along(): lax.ppermute(block, axis, [((i - distance) % devices, i) for i in range(d...  7.59 us
    pallas_call x2, Pallas kernels, lightning(): pl.pallas_call(mix_kernel, grid_spec=pltpu.PrefetchScalarGridSpec(num_sca...  7.41 us
    pallas_call x2, Pallas kernels, softmax_heads(): pl.pallas_call(soft_kernel, grid_spec=pltpu.PrefetchScalarGridSpec(num_sc...  7.34 us
    pallas_call x1, Pallas kernels, closing_states(): pl.pallas_call(states_kernel, grid=(parts,), in_specs=[wide, wide, pl.Blo...  3.98 us
    pallas_call x5, Pallas kernels, placed(): pl.pallas_call(functools.partial(place_kernel, start), in_specs=[anywhere...  3.82 us
  transfers between devices with their start and end apart: 9, of which 6 were waited for; matrix products, arithmetic and copies ran while one was open for 0% of the time, Pallas kernels for 33%

profile of v6, /device:TPU:1, one launch (start us, length us, event | category | flops | bytes accessed | tf_op | source)
XLA Modules:
  0.0 55.7 jit_solution(9738291731062573028)
XLA Ops:
  0.6 54.9 %conditional.1 = (bf16[1,256,2048]{2,1,0:T(8,128)(2,1)}, bf16[1,256,2048]{2,1,0:T(8,128)(2,1)}) conditional(s32[]{:T(128)} %convert_element_type.3, (bf16[1,256,2048]{2,1,0:T(8,128)(2,1)}, bf16[1,256,2048]{2,1,0:T(8,128)(2,1)}, f32[1,16,256]{2,1,0:T(8,128)}, bf16[1,256,256]{2,1,0:T(8,128)(2,1)}, bf16[1,256,256]{2,1,0:T(8,128)(2,1)}, ...), branch_computations={%region_0.0_spmd, %region_1.0_spmd} | conditional | bytes 16777580 | solution.py:545
  0.6 2.1 %collective-permute-start.1 = (bf16[1,256,256]{2,1,0:T(8,128)(2,1)}, bf16[1,256,256]{2,1,0:T(8,128)(2,1)S(1)}, u32[]{:S(2)}, u32[]{:S(2)}) collective-permute-start(bf16[1,256,256]{2,1,0:T(8,128)(2,1)} %get-tuple-element.49.key_ref), channel_id=1, source_target_pairs={{16,0},{0,16},{17,1},{1,17},{18,2},{2,18},{19,3},{3,19},{20,4},{4,... | collective-permute-start | bytes 393224 | tf_op jit(solution)/shard_map/cond/branch_0_fun/ppermute | solution.py:25
  2.8 0.1 collective-permute-start.2
  2.8 4.0 %closing_states.2 = (bf16[8,128,128]{2,1,0:T(8,128)(2,1)S(1)}, bf16[8,128,128]{2,1,0:T(8,128)(2,1)S(1)}) custom-call(bf16[1,256,2048]{2,1,0:T(8,128)(2,1)} %get-tuple-element.42.key_ref, bf16[1,256,2048]{2,1,0:T(8,128)(2,1)} %get-tuple-element.43.value_ref, f32[1,16,256]{2,1,0:T(8,128)} %get-tuple-element.44.decay_ref), custom_call_target="tpu_custom_call" | custom-call | tf_op jit(solution)/shard_map/cond/branch_0_fun/closing_states/pallas_call | solution.py:66
  6.8 0.0 collective-permute-done.1.before_key_ref
  6.8 0.0 collective-permute-done.2.before_value_ref
  6.8 3.7 %softmax_heads.2 = bf16[1,256,1024]{2,1,0:T(8,128)(2,1)S(1)} custom-call(s32[1]{0:T(128)} %get-tuple-element.40.place_ref, bf16[1,256,2048]{2,1,0:T(8,128)(2,1)} %get-tuple-element.54.query_ref, bf16[1,256,256]{2,1,0:T(8,128)(2,1)} %get-tuple-element.49.key_ref, bf16[1,256,256]{2,1,0:T(8,128)(2,1)} %get-tuple-element.50.value_ref, ...), custom_call_target="tpu_custom_call" | custom-call | tf_op jit(solution)/shard_map/cond/branch_0_fun/softmax_heads/pallas_call | solution.py:248
  10.5 1.8 %collective-permute-start.7 = (bf16[1,256,1024]{2,1,0:T(8,128)(2,1)S(1)}, bf16[1,256,1024]{2,1,0:T(8,128)(2,1)S(1)}, u32[]{:S(2)}, u32[]{:S(2)}) collective-permute-start(bf16[1,256,1024]{2,1,0:T(8,128)(2,1)S(1)} %softmax_heads.2), channel_id=1, source_target_pairs={{3,0},{0,1},{1,2},{2,3},{7,4},{4,5},{5,6},{6,7},{11,8},{8,9},{9,10... | collective-permute-start | bytes 1572872 | tf_op jit(solution)/shard_map/cond/branch_0_fun/ppermute | solution.py:25
  12.3 3.7 %softmax_heads.3 = bf16[1,256,1024]{2,1,0:T(8,128)(2,1)S(1)} custom-call(s32[1]{0:T(128)} %get-tuple-element.40.place_ref, bf16[1,256,2048]{2,1,0:T(8,128)(2,1)} %get-tuple-element.54.query_ref, bf16[1,256,256]{2,1,0:T(8,128)(2,1)} %get-tuple-element.49.key_ref, bf16[1,256,256]{2,1,0:T(8,128)(2,1)} %get-tuple-element.50.value_ref, ...), custom_call_target="tpu_custom_call" | custom-call | tf_op jit(solution)/shard_map/cond/branch_0_fun/softmax_heads/pallas_call | solution.py:248
  16.0 1.4 %collective-permute-start.3 = (bf16[1,256,1024]{2,1,0:T(8,128)(2,1)S(1)}, bf16[1,256,1024]{2,1,0:T(8,128)(2,1)S(1)}, u32[]{:S(2)}, u32[]{:S(2)}) collective-permute-start(bf16[1,256,1024]{2,1,0:T(8,128)(2,1)S(1)} %softmax_heads.3), channel_id=1, source_target_pairs={{3,0},{0,1},{1,2},{2,3},{7,4},{4,5},{5,6},{6,7},{11,8},{8,9},{9,10... | collective-permute-start | bytes 1572872 | tf_op jit(solution)/shard_map/cond/branch_0_fun/ppermute | solution.py:25
  17.3 1.2 %collective-permute-start.6 = (bf16[8,128,128]{2,1,0:T(8,128)(2,1)S(1)}, bf16[8,128,128]{2,1,0:T(8,128)(2,1)S(1)}, u32[]{:S(2)}, u32[]{:S(2)}) collective-permute-start(bf16[8,128,128]{2,1,0:T(8,128)(2,1)S(1)} %get-tuple-element.58), channel_id=1, source_target_pairs={{16,0},{0,16},{17,1},{1,17},{18,2},{2,18},{19,3},{3,19},{20,4},{4,... | collective-permute-start | bytes 786440 | tf_op jit(solution)/shard_map/cond/branch_0_fun/ppermute | solution.py:25
  18.5 0.3 collective-permute-start
  18.8 4.1 %collective-permute-done.6.state_ref = bf16[8,128,128]{2,1,0:T(8,128)(2,1)S(1)} collective-permute-done((bf16[8,128,128]{2,1,0:T(8,128)(2,1)S(1)}, bf16[8,128,128]{2,1,0:T(8,128)(2,1)S(1)}, u32[]{:S(2)}, u32[]{:S(2)}) %collective-permute-start.6) | collective-permute-done | bytes 262176 | tf_op jit(solution)/shard_map/cond/branch_0_fun/ppermute | solution.py:25
  22.8 4.0 %collective-permute-done.7.block_ref = bf16[1,256,1024]{2,1,0:T(8,128)(2,1)S(1)} collective-permute-done((bf16[1,256,1024]{2,1,0:T(8,128)(2,1)S(1)}, bf16[1,256,1024]{2,1,0:T(8,128)(2,1)S(1)}, u32[]{:S(2)}, u32[]{:S(2)}) %collective-permute-start.7) | collective-permute-done | bytes 524320 | tf_op jit(solution)/shard_map/cond/branch_0_fun/ppermute | solution.py:25
  26.9 3.7 %lightning_mix.5 = bf16[1,256,1024]{2,1,0:T(8,128)(2,1)S(1)} custom-call(s32[1]{0:T(128)} %get-tuple-element.40.place_ref, bf16[1,256,2048]{2,1,0:T(8,128)(2,1)} %get-tuple-element.41.query_ref, bf16[1,256,2048]{2,1,0:T(8,128)(2,1)} %get-tuple-element.42.key_ref, bf16[1,256,2048]{2,1,0:T(8,128)(2,1)} %get-tuple-element.43.value_ref, ...), custom_call_target="tpu_custom_call" | custom-call | tf_op jit(solution)/shard_map/cond/branch_0_fun/lightning_mix/pallas_call | solution.py:130
  30.6 0.1 collective-permute-start.8
  30.6 0.0 collective-permute-done.state_ref
  30.7 7.4 %collective-permute-done.3.block_ref = bf16[1,256,1024]{2,1,0:T(8,128)(2,1)S(1)} collective-permute-done((bf16[1,256,1024]{2,1,0:T(8,128)(2,1)S(1)}, bf16[1,256,1024]{2,1,0:T(8,128)(2,1)S(1)}, u32[]{:S(2)}, u32[]{:S(2)}) %collective-permute-start.3) | collective-permute-done | bytes 524320 | tf_op jit(solution)/shard_map/cond/branch_0_fun/ppermute | solution.py:25
  38.1 3.7 %lightning_mix.4 = (bf16[1,256,768]{2,1,0:T(8,128)(2,1)S(1)}, bf16[1,256,256]{2,1,0:T(8,128)(2,1)S(1)}) custom-call(s32[1]{0:T(128)} %get-tuple-element.40.place_ref, bf16[1,256,2048]{2,1,0:T(8,128)(2,1)} %get-tuple-element.41.query_ref, bf16[1,256,2048]{2,1,0:T(8,128)(2,1)} %get-tuple-element.42.key_ref, bf16[1,256,2048]{2,1,0:T(8,128)(2,1)} %get-tuple-element.43.value_ref, ...), custom_call_target="tpu_custom_call" | custom-call | tf_op jit(solution)/shard_map/cond/branch_0_fun/lightning_mix/pallas_call | solution.py:130
  41.8 0.1 collective-permute-start.5
  41.9 0.7 %collective-permute-start.4 = (bf16[1,256,256]{2,1,0:T(8,128)(2,1)S(1)}, bf16[1,256,256]{2,1,0:T(8,128)(2,1)S(1)}, u32[]{:S(2)}, u32[]{:S(2)}) collective-permute-start(bf16[1,256,256]{2,1,0:T(8,128)(2,1)S(1)} %get-tuple-element.56), channel_id=1, source_target_pairs={{3,0},{0,1},{1,2},{2,3},{7,4},{4,5},{5,6},{6,7},{11,8},{8,9},{9,10... | collective-permute-start | bytes 393224 | tf_op jit(solution)/shard_map/cond/branch_0_fun/ppermute | solution.py:25
  42.6 0.8 %placed.11.refs_0_ = bf16[1,256,2048]{2,1,0:T(8,128)(2,1)} custom-call(bf16[1,256,1024]{2,1,0:T(8,128)(2,1)S(1)} %collective-permute-done.7.block_ref), custom_call_target="tpu_custom_call" | custom-call | tf_op jit(solution)/shard_map/cond/branch_0_fun/placed/pallas_call | solution.py:366
  43.4 0.8 %placed.12 = bf16[1,256,2048]{2,1,0:T(8,128)(2,1)} custom-call(bf16[1,256,1024]{2,1,0:T(8,128)(2,1)S(1)} %collective-permute-done.3.block_ref, bf16[1,256,2048]{2,1,0:T(8,128)(2,1)} %placed.11.refs_0_), custom_call_target="tpu_custom_call", output_to_operand_aliasing={{}: (1, {})} | custom-call | tf_op jit(solution)/shard_map/cond/branch_0_fun/placed/pallas_call | solution.py:366
  44.2 5.1 %collective-permute-done.8.block_ref = bf16[1,256,1024]{2,1,0:T(8,128)(2,1)S(1)} collective-permute-done((bf16[1,256,1024]{2,1,0:T(8,128)(2,1)S(1)}, bf16[1,256,1024]{2,1,0:T(8,128)(2,1)S(1)}, u32[]{:S(2)}, u32[]{:S(2)}) %collective-permute-start.8) | collective-permute-done | bytes 524320 | tf_op jit(solution)/shard_map/cond/branch_0_fun/ppermute | solution.py:25
  49.3 0.8 %placed.8.refs_0_ = bf16[1,256,2048]{2,1,0:T(8,128)(2,1)} custom-call(bf16[1,256,1024]{2,1,0:T(8,128)(2,1)S(1)} %collective-permute-done.8.block_ref), custom_call_target="tpu_custom_call" | custom-call | tf_op jit(solution)/shard_map/cond/branch_0_fun/placed/pallas_call | solution.py:366
  50.1 3.1 %collective-permute-done.5.block_ref = bf16[1,256,768]{2,1,0:T(8,128)(2,1)S(1)} collective-permute-done((bf16[1,256,768]{2,1,0:T(8,128)(2,1)S(1)}, bf16[1,256,768]{2,1,0:T(8,128)(2,1)S(1)}, u32[]{:S(2)}, u32[]{:S(2)}) %collective-permute-start.5) | collective-permute-done | bytes 393248 | tf_op jit(solution)/shard_map/cond/branch_0_fun/ppermute | solution.py:25
  53.2 0.8 %placed.9.refs_0_ = bf16[1,256,2048]{2,1,0:T(8,128)(2,1)} custom-call(bf16[1,256,768]{2,1,0:T(8,128)(2,1)S(1)} %collective-permute-done.5.block_ref, bf16[1,256,2048]{2,1,0:T(8,128)(2,1)} %placed.8.refs_0_), custom_call_target="tpu_custom_call", output_to_operand_aliasing={{}: (1, {})} | custom-call | tf_op jit(solution)/shard_map/cond/branch_0_fun/placed/pallas_call | solution.py:366
  54.0 0.6 %collective-permute-done.4.block_ref = bf16[1,256,256]{2,1,0:T(8,128)(2,1)S(1)} collective-permute-done((bf16[1,256,256]{2,1,0:T(8,128)(2,1)S(1)}, bf16[1,256,256]{2,1,0:T(8,128)(2,1)S(1)}, u32[]{:S(2)}, u32[]{:S(2)}) %collective-permute-start.4) | collective-permute-done | bytes 131104 | tf_op jit(solution)/shard_map/cond/branch_0_fun/ppermute | solution.py:25
  54.6 0.7 %placed.10 = bf16[1,256,2048]{2,1,0:T(8,128)(2,1)} custom-call(bf16[1,256,256]{2,1,0:T(8,128)(2,1)S(1)} %collective-permute-done.4.block_ref, bf16[1,256,2048]{2,1,0:T(8,128)(2,1)} %placed.9.refs_0_), custom_call_target="tpu_custom_call", output_to_operand_aliasing={{}: (1, {})} | custom-call | tf_op jit(solution)/shard_map/cond/branch_0_fun/placed/pallas_call | solution.py:366
Async XLA Ops:
  0.6 6.2 %collective-permute-start.1 = (bf16[1,256,256]{2,1,0:T(8,128)(2,1)}, bf16[1,256,256]{2,1,0:T(8,128)(2,1)S(1)}, u32[]{:S(2)}, u32[]{:S(2)}) collective-permute-start(bf16[1,256,256]{2,1,0:T(8,128)(2,1)} %get-tuple-element.49.key_ref), channel_id=1, source_target_pairs={{16,0},{0,16},{17,1},{1,17},{18,2},{2,18},{19,3},{3,19},{20,4},{4,... | collective-permute-start | bytes 393224 | tf_op jit(solution)/shard_map/cond/branch_0_fun/ppermute | solution.py:25
  2.8 4.1 %collective-permute-start.2 = (bf16[1,256,256]{2,1,0:T(8,128)(2,1)}, bf16[1,256,256]{2,1,0:T(8,128)(2,1)S(1)}, u32[]{:S(2)}, u32[]{:S(2)}) collective-permute-start(bf16[1,256,256]{2,1,0:T(8,128)(2,1)} %get-tuple-element.50.value_ref), channel_id=1, source_target_pairs={{16,0},{0,16},{17,1},{1,17},{18,2},{2,18},{19,3},{3,19},{20,4},{4,... | collective-permute-start | bytes 393224 | tf_op jit(solution)/shard_map/cond/branch_0_fun/ppermute | solution.py:25
  10.5 16.3 %collective-permute-start.7 = (bf16[1,256,1024]{2,1,0:T(8,128)(2,1)S(1)}, bf16[1,256,1024]{2,1,0:T(8,128)(2,1)S(1)}, u32[]{:S(2)}, u32[]{:S(2)}) collective-permute-start(bf16[1,256,1024]{2,1,0:T(8,128)(2,1)S(1)} %softmax_heads.2), channel_id=1, source_target_pairs={{3,0},{0,1},{1,2},{2,3},{7,4},{4,5},{5,6},{6,7},{11,8},{8,9},{9,10... | collective-permute-start | bytes 1572872 | tf_op jit(solution)/shard_map/cond/branch_0_fun/ppermute | solution.py:25
  16.0 22.1 %collective-permute-start.3 = (bf16[1,256,1024]{2,1,0:T(8,128)(2,1)S(1)}, bf16[1,256,1024]{2,1,0:T(8,128)(2,1)S(1)}, u32[]{:S(2)}, u32[]{:S(2)}) collective-permute-start(bf16[1,256,1024]{2,1,0:T(8,128)(2,1)S(1)} %softmax_heads.3), channel_id=1, source_target_pairs={{3,0},{0,1},{1,2},{2,3},{7,4},{4,5},{5,6},{6,7},{11,8},{8,9},{9,10... | collective-permute-start | bytes 1572872 | tf_op jit(solution)/shard_map/cond/branch_0_fun/ppermute | solution.py:25
  17.3 5.5 %collective-permute-start.6 = (bf16[8,128,128]{2,1,0:T(8,128)(2,1)S(1)}, bf16[8,128,128]{2,1,0:T(8,128)(2,1)S(1)}, u32[]{:S(2)}, u32[]{:S(2)}) collective-permute-start(bf16[8,128,128]{2,1,0:T(8,128)(2,1)S(1)} %get-tuple-element.58), channel_id=1, source_target_pairs={{16,0},{0,16},{17,1},{1,17},{18,2},{2,18},{19,3},{3,19},{20,4},{4,... | collective-permute-start | bytes 786440 | tf_op jit(solution)/shard_map/cond/branch_0_fun/ppermute | solution.py:25
  18.5 12.1 %collective-permute-start = (bf16[8,128,128]{2,1,0:T(8,128)(2,1)S(1)}, bf16[8,128,128]{2,1,0:T(8,128)(2,1)S(1)}, u32[]{:S(2)}, u32[]{:S(2)}) collective-permute-start(bf16[8,128,128]{2,1,0:T(8,128)(2,1)S(1)} %get-tuple-element.47), channel_id=1, source_target_pairs={{16,0},{0,16},{17,1},{1,17},{18,2},{2,18},{19,3},{3,19},{20,4},{4,... | collective-permute-start | bytes 786440 | tf_op jit(solution)/shard_map/cond/branch_0_fun/ppermute | solution.py:25
  30.6 18.7 %collective-permute-start.8 = (bf16[1,256,1024]{2,1,0:T(8,128)(2,1)S(1)}, bf16[1,256,1024]{2,1,0:T(8,128)(2,1)S(1)}, u32[]{:S(2)}, u32[]{:S(2)}) collective-permute-start(bf16[1,256,1024]{2,1,0:T(8,128)(2,1)S(1)} %lightning_mix.5), channel_id=1, source_target_pairs={{3,0},{0,1},{1,2},{2,3},{7,4},{4,5},{5,6},{6,7},{11,8},{8,9},{9,10... | collective-permute-start | bytes 1572872 | tf_op jit(solution)/shard_map/cond/branch_0_fun/ppermute | solution.py:25
  41.8 11.4 %collective-permute-start.5 = (bf16[1,256,768]{2,1,0:T(8,128)(2,1)S(1)}, bf16[1,256,768]{2,1,0:T(8,128)(2,1)S(1)}, u32[]{:S(2)}, u32[]{:S(2)}) collective-permute-start(bf16[1,256,768]{2,1,0:T(8,128)(2,1)S(1)} %get-tuple-element.57), channel_id=1, source_target_pairs={{3,0},{0,1},{1,2},{2,3},{7,4},{4,5},{5,6},{6,7},{11,8},{8,9},{9,10... | collective-permute-start | bytes 1179656 | tf_op jit(solution)/shard_map/cond/branch_0_fun/ppermute | solution.py:25
  41.9 12.8 %collective-permute-start.4 = (bf16[1,256,256]{2,1,0:T(8,128)(2,1)S(1)}, bf16[1,256,256]{2,1,0:T(8,128)(2,1)S(1)}, u32[]{:S(2)}, u32[]{:S(2)}) collective-permute-start(bf16[1,256,256]{2,1,0:T(8,128)(2,1)S(1)} %get-tuple-element.56), channel_id=1, source_target_pairs={{3,0},{0,1},{1,2},{2,3},{7,4},{4,5},{5,6},{6,7},{11,8},{8,9},{9,10... | collective-permute-start | bytes 393224 | tf_op jit(solution)/shard_map/cond/branch_0_fun/ppermute | solution.py:25

commit v7 on v6

--- a/solution.py
+++ b/solution.py
@@ -514,8 +514,7 @@
             )
         )
     groups = [passed_along(group, "pp", 1) for group in groups]
-    for part in range(min(PARTS, kv_count)):
-        incoming[part], groups[part] = lax.optimization_barrier((incoming[part], groups[part]))
+    incoming[0], groups[0] = lax.optimization_barrier((incoming[0], groups[0]))
     arrays = (lin_query, lin_key, lin_value, decay_rows, out_gate, norm_gain)
     chunks = lightning_chunks(place, arrays, incoming)
     soft_handed = joined(groups, soft_query.shape[2])

time: 56 us -> 56 us (level)
  waiting for transfers between devices: 24.4 us -> 23.1 us
  starting transfers between devices: 7.59 us -> 8.87 us
    ppermute x9, starting transfers between devices: 7.59 us -> 8.87 us  [passed_along(): lax.ppermute(block, axis, [((i - distance) % devices, i) for i in range(d...]
    ppermute x9, waiting for transfers between devices: 24.4 us -> 23.1 us  [passed_along(): lax.ppermute(block, axis, [((i - distance) % devices, i) for i in range(d...]
where the time goes in v7:
time: 56 us; the launch traced here: 55.7 us
  waiting for transfers between devices  23.1 us (41%)
  Pallas kernels  22.5 us (40%)
  starting transfers between devices  8.87 us (16%)
  between operations  0.82 us (1%)
    ppermute x9, waiting for transfers between devices, passed_along(): lax.ppermute(block, axis, [((i - distance) % devices, i) for i in range(d...  23.1 us
    ppermute x9, starting transfers between devices, passed_along(): lax.ppermute(block, axis, [((i - distance) % devices, i) for i in range(d...  8.87 us
    pallas_call x2, Pallas kernels, lightning(): pl.pallas_call(mix_kernel, grid_spec=pltpu.PrefetchScalarGridSpec(num_sca...  7.42 us
    pallas_call x2, Pallas kernels, softmax_heads(): pl.pallas_call(soft_kernel, grid_spec=pltpu.PrefetchScalarGridSpec(num_sc...  7.33 us
    pallas_call x1, Pallas kernels, closing_states(): pl.pallas_call(states_kernel, grid=(parts,), in_specs=[wide, wide, pl.Blo...  3.98 us
    pallas_call x5, Pallas kernels, placed(): pl.pallas_call(functools.partial(place_kernel, start), in_specs=[anywhere...  3.82 us
  transfers between devices with their start and end apart: 9, of which 6 were waited for; matrix products, arithmetic and copies ran while one was open for 0% of the time, Pallas kernels for 33%

profile of v7, /device:TPU:1, one launch (start us, length us, event | category | flops | bytes accessed | tf_op | source)
XLA Modules:
  0.0 55.7 jit_solution(1872272404468463216)
XLA Ops:
  0.6 54.9 %conditional.1 = (bf16[1,256,2048]{2,1,0:T(8,128)(2,1)}, bf16[1,256,2048]{2,1,0:T(8,128)(2,1)}) conditional(s32[]{:T(128)} %convert_element_type.3, (bf16[1,256,2048]{2,1,0:T(8,128)(2,1)}, bf16[1,256,2048]{2,1,0:T(8,128)(2,1)}, f32[1,16,256]{2,1,0:T(8,128)}, s32[1]{0:T(128)}, bf16[1,256,2048]{2,1,0:T(8,128)(2,1)}, ...), branch_computations={%region_0.0_spmd, %region_1.0_spmd} | conditional | bytes 16777580 | solution.py:544
  0.6 2.1 %collective-permute-start.3 = (bf16[1,256,256]{2,1,0:T(8,128)(2,1)}, bf16[1,256,256]{2,1,0:T(8,128)(2,1)S(1)}, u32[]{:S(2)}, u32[]{:S(2)}) collective-permute-start(bf16[1,256,256]{2,1,0:T(8,128)(2,1)} %get-tuple-element.51.key_ref), channel_id=1, source_target_pairs={{16,0},{0,16},{17,1},{1,17},{18,2},{2,18},{19,3},{3,19},{20,4},{4,... | collective-permute-start | bytes 393224 | tf_op jit(solution)/shard_map/cond/branch_0_fun/ppermute | solution.py:25
  2.8 0.1 collective-permute-start.4
  2.8 4.0 %closing_states.2 = (bf16[8,128,128]{2,1,0:T(8,128)(2,1)S(1)}, bf16[8,128,128]{2,1,0:T(8,128)(2,1)S(1)}) custom-call(bf16[1,256,2048]{2,1,0:T(8,128)(2,1)} %get-tuple-element.42.key_ref, bf16[1,256,2048]{2,1,0:T(8,128)(2,1)} %get-tuple-element.43.value_ref, f32[1,16,256]{2,1,0:T(8,128)} %get-tuple-element.44.decay_ref), custom_call_target="tpu_custom_call" | custom-call | tf_op jit(solution)/shard_map/cond/branch_0_fun/closing_states/pallas_call | solution.py:66
  6.8 0.0 collective-permute-done.3.before_key_ref
  6.8 0.0 collective-permute-done.4.before_value_ref
  6.8 3.7 %softmax_heads.2 = bf16[1,256,1024]{2,1,0:T(8,128)(2,1)S(1)} custom-call(s32[1]{0:T(128)} %get-tuple-element.40.place_ref, bf16[1,256,2048]{2,1,0:T(8,128)(2,1)} %get-tuple-element.59.query_ref, bf16[1,256,256]{2,1,0:T(8,128)(2,1)} %get-tuple-element.51.key_ref, bf16[1,256,256]{2,1,0:T(8,128)(2,1)} %get-tuple-element.52.value_ref, ...), custom_call_target="tpu_custom_call" | custom-call | tf_op jit(solution)/shard_map/cond/branch_0_fun/softmax_heads/pallas_call | solution.py:248
  10.5 1.8 %collective-permute-start.6 = (bf16[1,256,1024]{2,1,0:T(8,128)(2,1)S(1)}, bf16[1,256,1024]{2,1,0:T(8,128)(2,1)S(1)}, u32[]{:S(2)}, u32[]{:S(2)}) collective-permute-start(bf16[1,256,1024]{2,1,0:T(8,128)(2,1)S(1)} %softmax_heads.2), channel_id=1, source_target_pairs={{3,0},{0,1},{1,2},{2,3},{7,4},{4,5},{5,6},{6,7},{11,8},{8,9},{9,10... | collective-permute-start | bytes 1572872 | tf_op jit(solution)/shard_map/cond/branch_0_fun/ppermute | solution.py:25
  12.3 1.2 %collective-permute-start.5 = (bf16[8,128,128]{2,1,0:T(8,128)(2,1)S(1)}, bf16[8,128,128]{2,1,0:T(8,128)(2,1)S(1)}, u32[]{:S(2)}, u32[]{:S(2)}) collective-permute-start(bf16[8,128,128]{2,1,0:T(8,128)(2,1)S(1)} %get-tuple-element.53), channel_id=1, source_target_pairs={{16,0},{0,16},{17,1},{1,17},{18,2},{2,18},{19,3},{3,19},{20,4},{4,... | collective-permute-start | bytes 786440 | tf_op jit(solution)/shard_map/cond/branch_0_fun/ppermute | solution.py:25
  13.5 0.3 collective-permute-start
  13.8 3.7 %softmax_heads.3 = bf16[1,256,1024]{2,1,0:T(8,128)(2,1)S(1)} custom-call(s32[1]{0:T(128)} %get-tuple-element.40.place_ref, bf16[1,256,2048]{2,1,0:T(8,128)(2,1)} %get-tuple-element.59.query_ref, bf16[1,256,256]{2,1,0:T(8,128)(2,1)} %get-tuple-element.51.key_ref, bf16[1,256,256]{2,1,0:T(8,128)(2,1)} %get-tuple-element.52.value_ref, ...), custom_call_target="tpu_custom_call" | custom-call | tf_op jit(solution)/shard_map/cond/branch_0_fun/softmax_heads/pallas_call | solution.py:248
  17.4 1.4 %collective-permute-start.8 = (bf16[1,256,1024]{2,1,0:T(8,128)(2,1)S(1)}, bf16[1,256,1024]{2,1,0:T(8,128)(2,1)S(1)}, u32[]{:S(2)}, u32[]{:S(2)}) collective-permute-start(bf16[1,256,1024]{2,1,0:T(8,128)(2,1)S(1)} %softmax_heads.3), channel_id=1, source_target_pairs={{3,0},{0,1},{1,2},{2,3},{7,4},{4,5},{5,6},{6,7},{11,8},{8,9},{9,10... | collective-permute-start | bytes 1572872 | tf_op jit(solution)/shard_map/cond/branch_0_fun/ppermute | solution.py:25
  18.8 1.7 %collective-permute-done.5.state_ref = bf16[8,128,128]{2,1,0:T(8,128)(2,1)S(1)} collective-permute-done((bf16[8,128,128]{2,1,0:T(8,128)(2,1)S(1)}, bf16[8,128,128]{2,1,0:T(8,128)(2,1)S(1)}, u32[]{:S(2)}, u32[]{:S(2)}) %collective-permute-start.5) | collective-permute-done | bytes 262176 | tf_op jit(solution)/shard_map/cond/branch_0_fun/ppermute | solution.py:25
  20.5 6.3 %collective-permute-done.6.block_ref = bf16[1,256,1024]{2,1,0:T(8,128)(2,1)S(1)} collective-permute-done((bf16[1,256,1024]{2,1,0:T(8,128)(2,1)S(1)}, bf16[1,256,1024]{2,1,0:T(8,128)(2,1)S(1)}, u32[]{:S(2)}, u32[]{:S(2)}) %collective-permute-start.6) | collective-permute-done | bytes 524320 | tf_op jit(solution)/shard_map/cond/branch_0_fun/ppermute | solution.py:25
  26.9 3.7 %lightning_mix.5 = bf16[1,256,1024]{2,1,0:T(8,128)(2,1)S(1)} custom-call(s32[1]{0:T(128)} %get-tuple-element.40.place_ref, bf16[1,256,2048]{2,1,0:T(8,128)(2,1)} %get-tuple-element.41.query_ref, bf16[1,256,2048]{2,1,0:T(8,128)(2,1)} %get-tuple-element.42.key_ref, bf16[1,256,2048]{2,1,0:T(8,128)(2,1)} %get-tuple-element.43.value_ref, ...), custom_call_target="tpu_custom_call" | custom-call | tf_op jit(solution)/shard_map/cond/branch_0_fun/lightning_mix/pallas_call | solution.py:130
  30.6 0.1 collective-permute-start.7
  30.6 0.0 collective-permute-done.state_ref
  30.7 3.7 %lightning_mix.4 = (bf16[1,256,768]{2,1,0:T(8,128)(2,1)S(1)}, bf16[1,256,256]{2,1,0:T(8,128)(2,1)S(1)}) custom-call(s32[1]{0:T(128)} %get-tuple-element.40.place_ref, bf16[1,256,2048]{2,1,0:T(8,128)(2,1)} %get-tuple-element.41.query_ref, bf16[1,256,2048]{2,1,0:T(8,128)(2,1)} %get-tuple-element.42.key_ref, bf16[1,256,2048]{2,1,0:T(8,128)(2,1)} %get-tuple-element.43.value_ref, ...), custom_call_target="tpu_custom_call" | custom-call | tf_op jit(solution)/shard_map/cond/branch_0_fun/lightning_mix/pallas_call | solution.py:130
  34.4 0.7 %collective-permute-start.2 = (bf16[1,256,768]{2,1,0:T(8,128)(2,1)S(1)}, bf16[1,256,768]{2,1,0:T(8,128)(2,1)S(1)}, u32[]{:S(2)}, u32[]{:S(2)}) collective-permute-start(bf16[1,256,768]{2,1,0:T(8,128)(2,1)S(1)} %get-tuple-element.49), channel_id=1, source_target_pairs={{3,0},{0,1},{1,2},{2,3},{7,4},{4,5},{5,6},{6,7},{11,8},{8,9},{9,10... | collective-permute-start | bytes 1179656 | tf_op jit(solution)/shard_map/cond/branch_0_fun/ppermute | solution.py:25
  35.1 1.3 %collective-permute-start.1 = (bf16[1,256,256]{2,1,0:T(8,128)(2,1)S(1)}, bf16[1,256,256]{2,1,0:T(8,128)(2,1)S(1)}, u32[]{:S(2)}, u32[]{:S(2)}) collective-permute-start(bf16[1,256,256]{2,1,0:T(8,128)(2,1)S(1)} %get-tuple-element.48), channel_id=1, source_target_pairs={{3,0},{0,1},{1,2},{2,3},{7,4},{4,5},{5,6},{6,7},{11,8},{8,9},{9,10... | collective-permute-start | bytes 393224 | tf_op jit(solution)/shard_map/cond/branch_0_fun/ppermute | solution.py:25
  36.4 0.8 %placed.11.refs_0_ = bf16[1,256,2048]{2,1,0:T(8,128)(2,1)} custom-call(bf16[1,256,1024]{2,1,0:T(8,128)(2,1)S(1)} %collective-permute-done.6.block_ref), custom_call_target="tpu_custom_call" | custom-call | tf_op jit(solution)/shard_map/cond/branch_0_fun/placed/pallas_call | solution.py:366
  37.2 0.9 %collective-permute-done.8.block_ref = bf16[1,256,1024]{2,1,0:T(8,128)(2,1)S(1)} collective-permute-done((bf16[1,256,1024]{2,1,0:T(8,128)(2,1)S(1)}, bf16[1,256,1024]{2,1,0:T(8,128)(2,1)S(1)}, u32[]{:S(2)}, u32[]{:S(2)}) %collective-permute-start.8) | collective-permute-done | bytes 524320 | tf_op jit(solution)/shard_map/cond/branch_0_fun/ppermute | solution.py:25
  38.1 0.8 %placed.12 = bf16[1,256,2048]{2,1,0:T(8,128)(2,1)} custom-call(bf16[1,256,1024]{2,1,0:T(8,128)(2,1)S(1)} %collective-permute-done.8.block_ref, bf16[1,256,2048]{2,1,0:T(8,128)(2,1)} %placed.11.refs_0_), custom_call_target="tpu_custom_call", output_to_operand_aliasing={{}: (1, {})} | custom-call | tf_op jit(solution)/shard_map/cond/branch_0_fun/placed/pallas_call | solution.py:366
  38.9 10.4 %collective-permute-done.7.block_ref = bf16[1,256,1024]{2,1,0:T(8,128)(2,1)S(1)} collective-permute-done((bf16[1,256,1024]{2,1,0:T(8,128)(2,1)S(1)}, bf16[1,256,1024]{2,1,0:T(8,128)(2,1)S(1)}, u32[]{:S(2)}, u32[]{:S(2)}) %collective-permute-start.7) | collective-permute-done | bytes 524320 | tf_op jit(solution)/shard_map/cond/branch_0_fun/ppermute | solution.py:25
  49.3 0.8 %placed.8.refs_0_ = bf16[1,256,2048]{2,1,0:T(8,128)(2,1)} custom-call(bf16[1,256,1024]{2,1,0:T(8,128)(2,1)S(1)} %collective-permute-done.7.block_ref), custom_call_target="tpu_custom_call" | custom-call | tf_op jit(solution)/shard_map/cond/branch_0_fun/placed/pallas_call | solution.py:366
  50.1 3.1 %collective-permute-done.2.block_ref = bf16[1,256,768]{2,1,0:T(8,128)(2,1)S(1)} collective-permute-done((bf16[1,256,768]{2,1,0:T(8,128)(2,1)S(1)}, bf16[1,256,768]{2,1,0:T(8,128)(2,1)S(1)}, u32[]{:S(2)}, u32[]{:S(2)}) %collective-permute-start.2) | collective-permute-done | bytes 393248 | tf_op jit(solution)/shard_map/cond/branch_0_fun/ppermute | solution.py:25
  53.2 0.8 %placed.9.refs_0_ = bf16[1,256,2048]{2,1,0:T(8,128)(2,1)} custom-call(bf16[1,256,768]{2,1,0:T(8,128)(2,1)S(1)} %collective-permute-done.2.block_ref, bf16[1,256,2048]{2,1,0:T(8,128)(2,1)} %placed.8.refs_0_), custom_call_target="tpu_custom_call", output_to_operand_aliasing={{}: (1, {})} | custom-call | tf_op jit(solution)/shard_map/cond/branch_0_fun/placed/pallas_call | solution.py:366
  54.0 0.6 %collective-permute-done.1.block_ref = bf16[1,256,256]{2,1,0:T(8,128)(2,1)S(1)} collective-permute-done((bf16[1,256,256]{2,1,0:T(8,128)(2,1)S(1)}, bf16[1,256,256]{2,1,0:T(8,128)(2,1)S(1)}, u32[]{:S(2)}, u32[]{:S(2)}) %collective-permute-start.1) | collective-permute-done | bytes 131104 | tf_op jit(solution)/shard_map/cond/branch_0_fun/ppermute | solution.py:25
  54.6 0.7 %placed.10 = bf16[1,256,2048]{2,1,0:T(8,128)(2,1)} custom-call(bf16[1,256,256]{2,1,0:T(8,128)(2,1)S(1)} %collective-permute-done.1.block_ref, bf16[1,256,2048]{2,1,0:T(8,128)(2,1)} %placed.9.refs_0_), custom_call_target="tpu_custom_call", output_to_operand_aliasing={{}: (1, {})} | custom-call | tf_op jit(solution)/shard_map/cond/branch_0_fun/placed/pallas_call | solution.py:366
Async XLA Ops:
  0.6 6.2 %collective-permute-start.3 = (bf16[1,256,256]{2,1,0:T(8,128)(2,1)}, bf16[1,256,256]{2,1,0:T(8,128)(2,1)S(1)}, u32[]{:S(2)}, u32[]{:S(2)}) collective-permute-start(bf16[1,256,256]{2,1,0:T(8,128)(2,1)} %get-tuple-element.51.key_ref), channel_id=1, source_target_pairs={{16,0},{0,16},{17,1},{1,17},{18,2},{2,18},{19,3},{3,19},{20,4},{4,... | collective-permute-start | bytes 393224 | tf_op jit(solution)/shard_map/cond/branch_0_fun/ppermute | solution.py:25
  2.8 4.1 %collective-permute-start.4 = (bf16[1,256,256]{2,1,0:T(8,128)(2,1)}, bf16[1,256,256]{2,1,0:T(8,128)(2,1)S(1)}, u32[]{:S(2)}, u32[]{:S(2)}) collective-permute-start(bf16[1,256,256]{2,1,0:T(8,128)(2,1)} %get-tuple-element.52.value_ref), channel_id=1, source_target_pairs={{16,0},{0,16},{17,1},{1,17},{18,2},{2,18},{19,3},{3,19},{20,4},{4,... | collective-permute-start | bytes 393224 | tf_op jit(solution)/shard_map/cond/branch_0_fun/ppermute | solution.py:25
  10.5 16.3 %collective-permute-start.6 = (bf16[1,256,1024]{2,1,0:T(8,128)(2,1)S(1)}, bf16[1,256,1024]{2,1,0:T(8,128)(2,1)S(1)}, u32[]{:S(2)}, u32[]{:S(2)}) collective-permute-start(bf16[1,256,1024]{2,1,0:T(8,128)(2,1)S(1)} %softmax_heads.2), channel_id=1, source_target_pairs={{3,0},{0,1},{1,2},{2,3},{7,4},{4,5},{5,6},{6,7},{11,8},{8,9},{9,10... | collective-permute-start | bytes 1572872 | tf_op jit(solution)/shard_map/cond/branch_0_fun/ppermute | solution.py:25
  12.3 8.2 %collective-permute-start.5 = (bf16[8,128,128]{2,1,0:T(8,128)(2,1)S(1)}, bf16[8,128,128]{2,1,0:T(8,128)(2,1)S(1)}, u32[]{:S(2)}, u32[]{:S(2)}) collective-permute-start(bf16[8,128,128]{2,1,0:T(8,128)(2,1)S(1)} %get-tuple-element.53), channel_id=1, source_target_pairs={{16,0},{0,16},{17,1},{1,17},{18,2},{2,18},{19,3},{3,19},{20,4},{4,... | collective-permute-start | bytes 786440 | tf_op jit(solution)/shard_map/cond/branch_0_fun/ppermute | solution.py:25
  13.5 17.2 %collective-permute-start = (bf16[8,128,128]{2,1,0:T(8,128)(2,1)S(1)}, bf16[8,128,128]{2,1,0:T(8,128)(2,1)S(1)}, u32[]{:S(2)}, u32[]{:S(2)}) collective-permute-start(bf16[8,128,128]{2,1,0:T(8,128)(2,1)S(1)} %get-tuple-element.47), channel_id=1, source_target_pairs={{16,0},{0,16},{17,1},{1,17},{18,2},{2,18},{19,3},{3,19},{20,4},{4,... | collective-permute-start | bytes 786440 | tf_op jit(solution)/shard_map/cond/branch_0_fun/ppermute | solution.py:25
  17.4 20.7 %collective-permute-start.8 = (bf16[1,256,1024]{2,1,0:T(8,128)(2,1)S(1)}, bf16[1,256,1024]{2,1,0:T(8,128)(2,1)S(1)}, u32[]{:S(2)}, u32[]{:S(2)}) collective-permute-start(bf16[1,256,1024]{2,1,0:T(8,128)(2,1)S(1)} %softmax_heads.3), channel_id=1, source_target_pairs={{3,0},{0,1},{1,2},{2,3},{7,4},{4,5},{5,6},{6,7},{11,8},{8,9},{9,10... | collective-permute-start | bytes 1572872 | tf_op jit(solution)/shard_map/cond/branch_0_fun/ppermute | solution.py:25
  30.6 18.7 %collective-permute-start.7 = (bf16[1,256,1024]{2,1,0:T(8,128)(2,1)S(1)}, bf16[1,256,1024]{2,1,0:T(8,128)(2,1)S(1)}, u32[]{:S(2)}, u32[]{:S(2)}) collective-permute-start(bf16[1,256,1024]{2,1,0:T(8,128)(2,1)S(1)} %lightning_mix.5), channel_id=1, source_target_pairs={{3,0},{0,1},{1,2},{2,3},{7,4},{4,5},{5,6},{6,7},{11,8},{8,9},{9,10... | collective-permute-start | bytes 1572872 | tf_op jit(solution)/shard_map/cond/branch_0_fun/ppermute | solution.py:25
  34.4 18.9 %collective-permute-start.2 = (bf16[1,256,768]{2,1,0:T(8,128)(2,1)S(1)}, bf16[1,256,768]{2,1,0:T(8,128)(2,1)S(1)}, u32[]{:S(2)}, u32[]{:S(2)}) collective-permute-start(bf16[1,256,768]{2,1,0:T(8,128)(2,1)S(1)} %get-tuple-element.49), channel_id=1, source_target_pairs={{3,0},{0,1},{1,2},{2,3},{7,4},{4,5},{5,6},{6,7},{11,8},{8,9},{9,10... | collective-permute-start | bytes 1179656 | tf_op jit(solution)/shard_map/cond/branch_0_fun/ppermute | solution.py:25
  35.1 19.5 %collective-permute-start.1 = (bf16[1,256,256]{2,1,0:T(8,128)(2,1)S(1)}, bf16[1,256,256]{2,1,0:T(8,128)(2,1)S(1)}, u32[]{:S(2)}, u32[]{:S(2)}) collective-permute-start(bf16[1,256,256]{2,1,0:T(8,128)(2,1)S(1)} %get-tuple-element.48), channel_id=1, source_target_pairs={{3,0},{0,1},{1,2},{2,3},{7,4},{4,5},{5,6},{6,7},{11,8},{8,9},{9,10... | collective-permute-start | bytes 393224 | tf_op jit(solution)/shard_map/cond/branch_0_fun/ppermute | solution.py:25
